TPU v7x, 256 devices: a whole 4x4x8 slice. The times are simulated.
256 devices in a mesh: seq: 16 (over y_hi, z), tp: 16 (over x, y_lo, core).
Axes of the slice: x: 4, y: 4 (y_hi: 2, y_lo: 2; y = y_hi * 2 + y_lo), z: 8, core: 2. Of those that a mesh axis runs over, the one named last changes fastest.
Arguments:
- tokens: bfloat16 [65536, 1024], P(('seq', 'tp')), may hold values from -6 to 6
- fine_gain: float32 [1024], replicated, may hold values from 0.1 to 1.9
- fine_query: bfloat16 [1024, 1024], replicated, may hold values from -2.0625 to 2.0625
- fine_keyval: bfloat16 [1024, 2048], replicated, may hold values from -0.125 to 0.125
- fine_out: bfloat16 [1024, 1024], replicated, may hold values from -0.1875 to 0.1875
- down_weight: bfloat16 [1024, 4096], P(None, 'tp'), may hold values from -0.1875 to 0.1875
- coarse_gain: float32 [4096], replicated, may hold values from 0.1 to 1.9
- coarse_query: bfloat16 [4096, 4096], P('seq', 'tp'), may hold values from -1.03125 to 1.03125
- coarse_keyval: bfloat16 [4096, 2, 4096], P('seq', None, 'tp'), may hold values from -0.0625 to 0.0625
- coarse_out: bfloat16 [4096, 4096], P('tp'), may hold values from -0.09375 to 0.09375
- up_weight: bfloat16 [4096, 1024], P('tp'), may hold values from -0.09375 to 0.09375
Outputs:
- result: bfloat16 [65536, 1024], P(('seq', 'tp'))
All inputs are finite; a program needn't handle non-finite values.
Results may differ from a plain program's by a relative error of at most 0.02.
Values may be sent and summed in bfloat16 or wider, within the bound.
No kernel may reach another device: no remote copies, remote signals or barrier semaphores. Data moves between devices by JAX's collectives and lax.ppermute only.
A program may use at most 192 MiB of HBM per device.

v0:
```python
import math

import jax
import jax.numpy as jnp
from jax import lax
from jax.sharding import PartitionSpec as P

HEAD = 128
WINDOW = 256
SHORT = 8


epsilon = 1e-06
big_negative = -1e30


def from_behind(array, axis, by):
    size = lax.axis_size(axis)
    pairs = [(i, i + by) for i in range(size) if 0 <= i + by < size]
    return lax.ppermute(array, axis, pairs)


def sent_to_all(array, axis):
    copies = jnp.broadcast_to(array, (lax.axis_size(axis), *array.shape))
    return lax.all_to_all(copies, axis, split_axis=0, concat_axis=0, tiled=True)


def joined_along(pieces, dim):
    pieces = jnp.moveaxis(pieces, 0, dim)
    dims = pieces.shape
    return pieces.reshape(*dims[:dim], dims[dim] * dims[dim + 1], *dims[dim + 2 :])


def gathered_copies(array, axis, dim):
    pieces = sent_to_all(array, axis)
    return joined_along(pieces, dim)


def sent_together(arrays, axis, dim, along):
    columns = [a.reshape(*a.shape[:along], -1) for a in arrays]
    both = jnp.concatenate(columns, axis=along)
    out, at, finished = (lax.all_gather(both, axis, axis=dim, tiled=True), 0, [])
    for a, column in zip(arrays, columns):
        piece = out[..., at : at + column.shape[along]]
        finished.append(piece.reshape(*piece.shape[:along], *a.shape[along:]))
        at += column.shape[along]
    return tuple(finished)


def in_blocks(array, dim, size):
    dims = array.shape
    pieces = array.reshape(*dims[:dim], size, dims[dim] // size, *dims[dim + 1 :])
    return jnp.moveaxis(pieces, dim, 0)


def sent_and_summed(array, axis, dim):
    size = lax.axis_size(axis)
    pieces = lax.all_to_all(in_blocks(array, dim, size), axis, 0, 0, tiled=True)
    return jnp.sum(pieces.astype(jnp.float32), axis=0)


def normalize(values, scale_gain):
    mean_square = jnp.mean(values * values, axis=-1, keepdims=True)
    return values * lax.rsqrt(mean_square + epsilon) * scale_gain


def online_update(state, query_heads, key_piece, value_piece, query_index):
    running_max, running_sum, accumulate = state
    scale = 1.0 / math.sqrt(HEAD)
    scores = (
        jnp.einsum("qhd,khd->hqk", query_heads, key_piece, preferred_element_type=jnp.float32)
        * scale
    )
    key_index = jnp.arange(key_piece.shape[0], dtype=jnp.int32)
    allowed = key_index[None, :] <= query_index[:, None]
    scores = jnp.where(allowed[None], scores, big_negative)
    new_max = jnp.maximum(running_max, jnp.max(scores, axis=-1))
    terms = jnp.where(allowed[None], jnp.exp(scores - new_max[..., None]), 0.0)
    new_sum = jnp.sum(terms, axis=-1)
    product = jnp.einsum(
        "hqk,khd->hqd", terms.astype(jnp.bfloat16), value_piece, preferred_element_type=jnp.float32
    )
    return (new_max, new_sum, product)


def body(
    tokens,
    fine_gain,
    fine_query,
    fine_keyval,
    fine_out,
    down_weight,
    coarse_gain,
    coarse_query,
    coarse_keyval,
    coarse_out,
    up_weight,
):
    tok_rows = tokens.shape[0]
    width = tokens.shape[1]
    fine_heads = width // HEAD
    scale = 1.0 / math.sqrt(HEAD)
    start_row = lax.axis_index(("seq", "tp")) * tok_rows
    inputs = tokens.astype(jnp.float32)
    normed = normalize(inputs, fine_gain).astype(jnp.bfloat16)
    queries = jnp.dot(normed, fine_query, preferred_element_type=jnp.float32).astype(jnp.bfloat16)
    keyvals = jnp.dot(normed, fine_keyval, preferred_element_type=jnp.float32).astype(jnp.bfloat16)
    earlier_rows = from_behind(normed, ("seq", "tp"), 1)
    earlier = jnp.dot(earlier_rows, fine_keyval, preferred_element_type=jnp.float32).astype(
        jnp.bfloat16
    )
    key_rows = jnp.concatenate([earlier, keyvals], 0)
    span = key_rows.shape[0]
    key_heads = key_rows[:, :width].reshape(span, fine_heads, HEAD)
    value_heads = key_rows[:, width:].reshape(span, fine_heads, HEAD)
    query_heads = queries.reshape(tok_rows, fine_heads, HEAD)
    scores = (
        jnp.einsum("qhd,khd->hqk", query_heads, key_heads, preferred_element_type=jnp.float32)
        * scale
    )
    row_index = jnp.arange(tok_rows, dtype=jnp.int32)[:, None]
    col_index = jnp.arange(span, dtype=jnp.int32)[None, :]
    offset = row_index + WINDOW - col_index
    allowed = (offset >= 0) & (offset < WINDOW) & (start_row - WINDOW + col_index >= 0)
    scores = jnp.where(allowed[None], scores, big_negative)
    peak = jnp.max(scores, axis=-1, keepdims=True)
    terms = jnp.where(allowed[None], jnp.exp(scores - peak), 0.0)
    denom = jnp.sum(terms, axis=-1)
    mixed = jnp.einsum(
        "hqk,khd->qhd", terms.astype(jnp.bfloat16), value_heads, preferred_element_type=jnp.float32
    )
    local = (mixed / jnp.transpose(denom)[..., None]).reshape(tok_rows, width).astype(jnp.bfloat16)
    fine_state = (inputs + jnp.dot(local, fine_out, preferred_element_type=jnp.float32)).astype(
        jnp.bfloat16
    )
    pooled = jnp.mean(
        fine_state.astype(jnp.float32).reshape(tok_rows // SHORT, SHORT, width), axis=1
    ).astype(jnp.bfloat16)
    pooled_all = gathered_copies(pooled, "tp", 0)
    short_cols = jnp.dot(pooled_all, down_weight, preferred_element_type=jnp.float32).astype(
        jnp.bfloat16
    )
    shortened = lax.all_gather(short_cols, "tp", axis=1, tiled=True)
    coarse_normed = normalize(shortened.astype(jnp.float32), coarse_gain).astype(jnp.bfloat16)
    coarse_rows = coarse_normed.shape[0]
    local_cols = coarse_query.shape[1]
    local_heads = local_cols // HEAD
    query_rows, keyval_rows = sent_together((coarse_query, coarse_keyval), "seq", 0, 1)
    count = query_rows.shape[0]
    query_sum = jnp.dot(coarse_normed, query_rows, preferred_element_type=jnp.float32)
    keyval_sum = jnp.dot(
        coarse_normed,
        keyval_rows.reshape(count, 2 * local_cols),
        preferred_element_type=jnp.float32,
    )
    coarse_queries = query_sum.astype(jnp.bfloat16).reshape(coarse_rows, local_heads, HEAD)
    coarse_kv = keyval_sum.astype(jnp.bfloat16).reshape(coarse_rows, 2, local_cols)
    my_first = lax.axis_index("seq") * coarse_rows
    query_index = my_first + jnp.arange(coarse_rows, dtype=jnp.int32)
    initial = (
        jnp.full((local_heads, coarse_rows), big_negative, jnp.float32),
        jnp.zeros((local_heads, coarse_rows), jnp.float32),
        jnp.zeros((local_heads, coarse_rows, HEAD), jnp.float32),
    )
    piece = lax.all_gather(coarse_kv, "seq", axis=0, tiled=True)
    count = piece.shape[0]
    key_piece = piece[:, 0].reshape(count, local_heads, HEAD)
    value_piece = piece[:, 1].reshape(count, local_heads, HEAD)
    final = lax.cond(
        jnp.int32(0) < my_first + coarse_rows,
        lambda: online_update(initial, coarse_queries, key_piece, value_piece, query_index),
        lambda: initial,
    )
    head_out = final[2] / final[1][..., None]
    coarse_heads = (
        jnp.transpose(head_out, (1, 0, 2)).reshape(coarse_rows, local_cols).astype(jnp.bfloat16)
    )
    out_columns = lax.all_to_all(coarse_out, "tp", split_axis=1, concat_axis=0, tiled=True)
    all_heads = lax.all_gather(coarse_heads, "tp", axis=1, tiled=True)
    attended = jnp.dot(all_heads, out_columns, preferred_element_type=jnp.float32)
    coarse_state = (short_cols.astype(jnp.float32) + attended).astype(jnp.bfloat16)
    prior_row = from_behind(coarse_state[coarse_rows - 1 :], "seq", 1)
    delayed = jnp.concatenate([prior_row, coarse_state[: coarse_rows - 1]], 0)
    lifted = sent_and_summed(
        jnp.dot(delayed, up_weight, preferred_element_type=jnp.float32).astype(jnp.bfloat16),
        "tp",
        0,
    )
    result = fine_state.astype(jnp.float32) + jnp.repeat(lifted, SHORT, axis=0)
    return result.astype(jnp.bfloat16)


def solution(mesh):
    return jax.shard_map(
        body,
        mesh=mesh,
        in_specs=(
            P(("seq", "tp"), None),
            P(),
            P(),
            P(),
            P(),
            P(None, "tp"),
            P(),
            P("seq", "tp"),
            P("seq", None, "tp"),
            P("tp", None),
            P("tp", None),
        ),
        out_specs=P(("seq", "tp"), None),
        check_vma=False,
    )
```

profile of v0, /device:TPU:16, one launch (start us, length us, event | category | flops | bytes accessed | tf_op | source)
XLA Modules:
  0.0 535.3 jit_solution(775924119704233040)
XLA Ops:
  6.5 0.0 copy-start
  6.5 0.0 all-gather.5.cloned.1.call-start
  6.5 1.4 fusion.50
  7.9 1.2 fusion.52
  9.2 1.9 collective-permute-start
  11.1 3.1 fusion.39
  14.2 0.2 fusion.63
  14.4 3.6 convolution_convert_fusion
  18.0 7.4 %collective-permute-done = bf16[256,1024]{1,0:T(8,128)(2,1)} collective-permute-done((bf16[256,1024]{1,0:T(8,128)(2,1)S(1)}, bf16[256,1024]{1,0:T(8,128)(2,1)}, u32[]{:S(2)}, u32[]{:S(2)}) %collective-permute-start) | collective-permute-done | bytes 524320 | tf_op jit(solution)/shard_map/ppermute | solution.py:20
  25.4 0.0 copy-done.9
  25.4 2.3 convolution_convert_fusion.1
  27.7 1.1 fusion.57
  28.9 1.3 copy.35
  30.2 2.1 fusion.54
  32.3 0.0 copy-start.4
  32.3 2.5 fusion.71
  34.8 0.0 copy-done.4
  34.9 0.8 fusion.36
  35.7 0.0 copy-start.10
  35.7 0.0 copy-done
  35.7 0.2 copy-done.3
  35.9 0.9 fusion.48
  36.8 0.1 broadcast_in_dim.70
  37.0 19.1 %all_to_all.29 = bf16[16,32,1024]{2,1,0:T(8,128)(2,1)S(1)} all-to-all(bf16[16,32,1024]{2,1,0:T(8,128)(2,1)S(1)} %broadcast_in_dim.70), channel_id=1, replica_groups=mesh['seq'=16,'tp'=16] {'tp'}, dimensions={0} | all-to-all | bytes 2097152 | tf_op jit(solution)/shard_map/all_to_all | solution.py:25
  56.1 0.0 copy-done.10
  56.1 1.2 convolution_convert_fusion.4
  57.2 0.0 all-gather.5.cloned.1.call-update
  57.2 0.0 all-gather.7.cloned.1.call-start
  57.3 0.0 copy-done.6
  57.3 0.0 copy-done.8
  57.4 0.8 pad_maximum_fusion.1
  58.1 0.0 all-gather.7.cloned.1.call-update
  58.2 0.2 all-gather.9.cloned.1.call-start
  58.4 45.5 %all-gather.5.cloned.1.call-done = bf16[512,4096]{1,0:T(8,128)(2,1)} async-done(((bf16[512,256]{1,0:T(8,128)(2,1)}), bf16[512,4096]{1,0:T(8,128)(2,1)}) %all-gather.5.cloned.1.call-update) | async-done | bytes 4194320 | tf_op jit(solution)/shard_map/all_gather | solution.py:143
  103.9 3.1 fusion.13
  107.0 113.3 %all-gather.7.cloned.1.call-done = bf16[4096,768]{1,0:T(8,128)(2,1)} async-done(((bf16[256,768]{1,0:T(8,128)(2,1)}), bf16[4096,768]{1,0:T(8,128)(2,1)}) %all-gather.7.cloned.1.call-update) | async-done | bytes 6291472 | tf_op jit(solution)/shard_map/all_gather | solution.py:42
  220.3 0.0 copy-done.11
  220.3 6.7 %fusion.33 = bf16[512,512]{0,1:T(8,128)(2,1)} fusion(bf16[4096,768]{1,0:T(8,128)(2,1)} %all-gather.7.cloned.1.call-done, bf16[512,4096]{1,0:T(8,128)(2,1)} %all-gather.5.cloned.1.call-done, f32[4096]{0:T(1024)S(1)} %copy-done.11, f32[512]{0:T(512)S(1)} %add_rsqrt_fusion), kind=kOutput, calls=%fused_computation.48 | convolution fusion | flops 2156134400 | bytes 8931328 | tf_op jit(solution)/shard_map/dot_general | solution.py:151
  227.0 0.0 all-gather.9.cloned.1.call-update
  227.0 0.0 all-gather.11.cloned.1.call-start
  227.1 4.2 fusion.42
  231.3 141.4 %all-gather.9.cloned.1.call-done = bf16[8192,2,256]{0,2,1:T(8,128)(2,1)} async-done(((bf16[512,2,256]{0,2,1:T(8,128)(2,1)}), bf16[8192,2,256]{0,2,1:T(8,128)(2,1)}) %all-gather.9.cloned.1.call-update) | async-done | bytes 8388624 | tf_op jit(solution)/shard_map/all_gather | solution.py:165
  372.7 61.6 %conditional.1 = (f32[2,512]{1,0:T(2,128)S(1)}, f32[2,512,128]{1,2,0:T(8,128)S(1)}) conditional(s32[]{:T(128)} %convert_element_type.92, () %tuple.13, (s32[]{:T(128)}, s32[512]{0:T(512)S(1)}, bf16[512,256]{1,0:T(8,128)(2,1)S(1)}, bf16[8192,2,256]{0,2,1:T(8,128)(2,1)}) %tuple.14), branch_computations={%region_5.6_spmd, %region_6.9_spmd} | conditional | flops 4408212992 | bytes 160200752 | solution.py:169
  372.7 5.2 iota_compare_fusion
  377.9 5.9 %fusion.70 = (bf16[8192,1,256]{0,2,1:T(8,128)(2,1)}, bf16[8192,1,256]{0,2,1:T(8,128)(2,1)}) fusion(bf16[8192,2,256]{0,2,1:T(8,128)(2,1)} %get-tuple-element.24), kind=kLoop, calls=%fused_computation.87 | loop fusion | bytes 16777216 | tf_op jit(solution)/shard_map/slice | solution.py:168
  383.9 17.8 %fusion = (f32[2,512]{1,0:T(2,128)S(1)}, f32[2,512,8192]{2,1,0:T(8,128)}) fusion(pred[512,8192]{1,0:T(8,128)(4,1)} %iota_compare_fusion, bf16[8192,2,128]{0,2,1:T(8,128)(2,1)} %bitcast.69, bf16[512,256]{1,0:T(8,128)(2,1)S(1)} %get-tuple-element.23), kind=kOutput, calls=%fused_computation.2 | convolution fusion | flops 2172648448 | bytes 42209280 | tf_op jit(solution)/shard_map/cond/branch_1_fun/qhd,khd->hqk/dot_general | solution.py:71
  401.7 16.8 %fusion.2 = f32[2,512]{1,0:T(2,128)S(1)} fusion(f32[2,512,8192]{2,1,0:T(8,128)} %get-tuple-element.33, f32[2,512]{1,0:T(2,128)S(1)} %broadcast_maximum_fusion, pred[512,8192]{1,0:T(8,128)(4,1)} %iota_compare_fusion), kind=kLoop, calls=%fused_computation.4 | loop fusion | flops 41942016 | bytes 37756928 | tf_op jit(solution)/shard_map/cond/branch_1_fun/reduce_sum | solution.py:79
  418.5 0.0 copy-done.2
  418.5 15.8 %fusion.3 = f32[2,512,128]{1,2,0:T(8,128)S(1)} fusion(bf16[8192,2,128]{0,2,1:T(8,128)(2,1)} %bitcast.68, f32[2,512,8192]{2,1,0:T(8,128)} %get-tuple-element.33, f32[2,512]{1,0:T(2,128)S(1)} %broadcast_maximum_fusion, pred[512,8192]{1,0:T(8,128)(4,1)S(1)} %copy-done.2), kind=kOutput, calls=%fused_computation.6 | convolution fusion | flops 2189426688 | bytes 42471424 | tf_op jit(solution)/shard_map/cond | solution.py:169
  434.3 0.7 divide_convert_fusion
  435.1 0.0 all-gather.11.cloned.1.call-update
  435.1 4.1 copy.31
  439.2 44.0 %all_to_all.30 = bf16[256,16,256]{0,2,1:T(8,128)(2,1)S(1)} all-to-all(bf16[256,16,256]{0,2,1:T(8,128)(2,1)} %bitcast.66), channel_id=1, replica_groups=mesh['seq'=16,'tp'=16] {'tp'}, dimensions={1} | all-to-all | bytes 4194304 | tf_op jit(solution)/shard_map/all_to_all | solution.py:178
  483.2 2.4 copy.32
  485.5 8.5 %all-gather.11.cloned.1.call-done = bf16[512,4096]{0,1:T(8,128)(2,1)} async-done(((bf16[512,256]{0,1:T(8,128)(2,1)}), bf16[512,4096]{0,1:T(8,128)(2,1)}) %all-gather.11.cloned.1.call-update) | async-done | bytes 4194320 | tf_op jit(solution)/shard_map/all_gather | solution.py:179
  494.0 0.0 copy-done.7
  494.0 4.3 fusion.47
  498.3 3.5 collective-permute-start.1
  501.9 5.6 %collective-permute-done.1 = bf16[1,256]{1,0:T(2,128)(2,1)S(1)} collective-permute-done((bf16[1,256]{1,0:T(2,128)(2,1)S(1)}, bf16[1,256]{1,0:T(2,128)(2,1)S(1)}, u32[]{:S(2)}, u32[]{:S(2)}) %collective-permute-start.1) | collective-permute-done | bytes 544 | tf_op jit(solution)/shard_map/ppermute | solution.py:20
  507.4 0.0 copy-done.5
  507.4 0.4 convolution_convert_fusion.2
  507.9 19.7 %all_to_all.31 = bf16[16,32,1024]{2,1,0:T(8,128)(2,1)S(1)} all-to-all(bf16[16,32,1024]{2,1,0:T(8,128)(2,1)S(1)} %bitcast.67), channel_id=1, replica_groups=mesh['seq'=16,'tp'=16] {'tp'}, dimensions={0} | all-to-all | bytes 2097152 | tf_op jit(solution)/shard_map/all_to_all | solution.py:58
  527.6 0.2 convert_reduce_fusion
  527.8 0.9 fusion.49
  (20 shorter events, 0.1 us)
Async XLA Ops:
  6.5 29.1 %copy-start = (bf16[1024,1024]{1,0:T(8,128)(2,1)S(1)}, bf16[1024,1024]{1,0:T(8,128)(2,1)}, u32[]{:S(2)}) copy-start(bf16[1024,1024]{1,0:T(8,128)(2,1)} %param.17) | copy-start | bytes 6291460
  6.5 97.4 %all-gather.5.cloned.1.call-start = ((), (), s32[]{:S(2)}) async-start(), calls=%async_computation.3 | async-start | bytes 4456448 | tf_op jit(solution)/shard_map/all_gather | solution.py:143
  9.2 16.2 %collective-permute-start = (bf16[256,1024]{1,0:T(8,128)(2,1)S(1)}, bf16[256,1024]{1,0:T(8,128)(2,1)}, u32[]{:S(2)}, u32[]{:S(2)}) collective-permute-start(bf16[256,1024]{1,0:T(8,128)(2,1)S(1)} %fusion.52), channel_id=1, source_target_pairs={{0,1},{1,2},{2,3},{3,4},{4,5},{5,6},{6,7},{7,8},{8,9},{9,10},{10,1... | collective-permute-start | bytes 1572872 | tf_op jit(solution)/shard_map/ppermute | solution.py:20
  14.2 11.2 %copy-start.9 = (bf16[1024,2048]{1,0:T(8,128)(2,1)S(1)}, bf16[1024,2048]{1,0:T(8,128)(2,1)}, u32[]{:S(2)}) copy-start(bf16[1024,2048]{1,0:T(8,128)(2,1)} %param.16) | copy-start | bytes 12582916
  32.3 2.5 copy-start.4
  34.8 1.0 copy-start.3
  35.7 20.4 %copy-start.10 = (bf16[1024,256]{1,0:T(8,128)(2,1)S(1)}, bf16[1024,256]{1,0:T(8,128)(2,1)}, u32[]{:S(2)}) copy-start(bf16[1024,256]{1,0:T(8,128)(2,1)} %param.18) | copy-start | bytes 1572868
  35.9 21.4 %copy-start.6 = (bf16[256,2,256]{2,1,0:T(2,128)(2,1)S(1)}, bf16[256,2,256]{2,1,0:T(2,128)(2,1)}, u32[]{:S(2)}) copy-start(bf16[256,2,256]{2,1,0:T(2,128)(2,1)} %param.21) | copy-start | bytes 786436
  35.9 21.5 %copy-start.8 = (bf16[256,256]{1,0:T(8,128)(2,1)S(1)}, bf16[256,256]{1,0:T(8,128)(2,1)}, u32[]{:S(2)}) copy-start(bf16[256,256]{1,0:T(8,128)(2,1)} %param.20) | copy-start | bytes 393220
  56.1 164.2 %copy-start.11 = (f32[4096]{0:T(1024)S(1)}, f32[4096]{0:T(1024)}, u32[]{:S(2)}) copy-start(f32[4096]{0:T(1024)} %param.19) | copy-start | bytes 49156
  57.2 163.1 %all-gather.7.cloned.1.call-start = ((), (), s32[]{:S(2)}) async-start(), calls=%async_computation.4 | async-start | bytes 6684672 | tf_op jit(solution)/shard_map/all_gather | solution.py:42
  58.2 314.6 %all-gather.9.cloned.1.call-start = ((), (), s32[]{:S(2)}) async-start(), calls=%async_computation.5 | async-start | bytes 8912896 | tf_op jit(solution)/shard_map/all_gather | solution.py:165
  227.0 267.0 %all-gather.11.cloned.1.call-start = ((), (), s32[]{:S(2)}) async-start(), calls=%async_computation.6 | async-start | bytes 4456448 | tf_op jit(solution)/shard_map/all_gather | solution.py:179
  401.7 16.8 %copy-start.2 = (pred[512,8192]{1,0:T(8,128)(4,1)S(1)}, pred[512,8192]{1,0:T(8,128)(4,1)}, u32[]{:S(2)}) copy-start(pred[512,8192]{1,0:T(8,128)(4,1)} %iota_compare_fusion) | copy-start | bytes 12582916 | tf_op jit(solution)/shard_map/cond
  439.2 54.9 %copy-start.7 = (bf16[512,256]{1,0:T(8,128)(2,1)S(1)}, bf16[512,256]{1,0:T(8,128)(2,1)}, u32[]{:S(2)}) copy-start(bf16[512,256]{1,0:T(8,128)(2,1)} %convolution_convert_fusion.4) | copy-start | bytes 786436
  494.0 13.4 %copy-start.5 = (bf16[256,1024]{1,0:T(8,128)(2,1)S(1)}, bf16[256,1024]{1,0:T(8,128)(2,1)}, u32[]{:S(2)}) copy-start(bf16[256,1024]{1,0:T(8,128)(2,1)} %param.23) | copy-start | bytes 1572868
  494.0 34.7 %copy-start.1 = (bf16[1024,1024]{1,0:T(8,128)(2,1)S(1)}, bf16[1024,1024]{1,0:T(8,128)(2,1)}, u32[]{:S(2)}) copy-start(bf16[1024,1024]{1,0:T(8,128)(2,1)} %param.17) | copy-start | bytes 6291460
  498.3 9.1 %collective-permute-start.1 = (bf16[1,256]{1,0:T(2,128)(2,1)S(1)}, bf16[1,256]{1,0:T(2,128)(2,1)S(1)}, u32[]{:S(2)}, u32[]{:S(2)}) collective-permute-start(bf16[1,256]{1,0:T(2,128)(2,1)S(1)} %slice.36), channel_id=1, source_target_pairs={{0,16},{16,32},{32,48},{48,64},{64,80},{80,96},{96,112},{112,128},... | collective-permute-start | bytes 1544 | tf_op jit(solution)/shard_map/ppermute | solution.py:20
Sparse Core Ops, SparseCore 0:
  57.4 46.4 all-gather.4
  106.5 113.7 all-gather.6
  227.2 145.4 all-gather.8
  435.2 58.7 all-gather.10
where the time goes:
time: 536 us; the launch traced here: 535 us
  waiting for transfers between devices  322 us (60%)
  blocking collectives  82.8 us (15%)
  matrix products  63.3 us (12%)
  other arithmetic  34.2 us (6%)
  local copies, waits for them, and re-layouts  14.1 us (3%)
  between operations  13.3 us (2%)
  starting transfers between devices  5.73 us (1%)
    all_gather x1, waiting for transfers between devices, body(): piece = lax.all_gather(coarse_kv, 'seq', axis=0, tiled=True)  141 us
    all_gather x1, waiting for transfers between devices, sent_together(): lax.all_gather(both, axis, axis=dim, tiled=True)  113 us
    all_gather x1, waiting for transfers between devices, body(): shortened = lax.all_gather(short_cols, 'tp', axis=1, tiled=True)  45.5 us
    all_to_all x1, blocking collectives, body(): lax.all_to_all(coarse_out, 'tp', split_axis=1, concat_axis=0, tiled=True)  44 us
    all_to_all x1, blocking collectives, sent_and_summed(): pieces = lax.all_to_all(in_blocks(array, dim, size), axis, 0, 0, tiled=True)  19.7 us
    all_to_all x1, blocking collectives, sent_to_all(): return lax.all_to_all(copies, axis, split_axis=0, concat_axis=0, tiled=True)  19.1 us
    dot_general x1, matrix products, online_update(): jnp.einsum('qhd,khd->hqk', query_heads, key_piece, preferred_element_type...  17.8 us
    reduce_sum x1, other arithmetic, online_update(): new_sum = jnp.sum(terms, axis=-1)  16.8 us
  transfers between devices with their start and end apart: 6, of which 6 were waited for; matrix products, arithmetic and copies ran while one was open for 4% of the time, Pallas kernels for 0%

commit v1 on v0

v1 whole, which is shorter than its diff:
```python
import functools
import math

import jax
import jax.numpy as jnp
from jax import lax
from jax.experimental import pallas as pl
from jax.experimental.pallas import tpu as pltpu
from jax.sharding import Mesh, PartitionSpec as P

HEAD = 128
WINDOW = 256
SHORT = 8

epsilon = 1e-06
big_negative = -1e30

ALL = ("yh", "z", "x", "yl", "c")
SEQ = ("yh", "z")
TP = ("x", "yl", "c")
f32 = jnp.float32
bf16 = jnp.bfloat16


def from_behind(array, axis, by):
    size = lax.axis_size(axis)
    pairs = [(i, i + by) for i in range(size) if 0 <= i + by < size]
    return lax.ppermute(array, axis, pairs)


def rotated(array, axis, by):
    size = lax.axis_size(axis)
    return lax.ppermute(array, axis, [(i, (i + by) % size) for i in range(size)])


def gathered(array, axes):
    copies = jnp.broadcast_to(array, (lax.axis_size(axes), *array.shape))
    return lax.all_to_all(copies, axes, split_axis=0, concat_axis=0, tiled=True)


def exchanged(pieces, axes):
    return lax.all_to_all(pieces, axes, split_axis=0, concat_axis=0, tiled=True)


def normalize(values, scale_gain):
    mean_square = jnp.mean(values * values, axis=-1, keepdims=True)
    return values * lax.rsqrt(mean_square + epsilon) * scale_gain


def dot(a, b):
    return jnp.dot(a, b, preferred_element_type=f32)


def fine_layer(tokens, fine_gain, fine_query, fine_keyval, fine_out):
    tok_rows, width = tokens.shape
    fine_heads = width // HEAD
    scale = 1.0 / math.sqrt(HEAD)
    start_row = lax.axis_index(ALL) * tok_rows
    inputs = tokens.astype(f32)
    normed = normalize(inputs, fine_gain).astype(bf16)
    queries = dot(normed, fine_query).astype(bf16)
    keyvals = dot(normed, fine_keyval).astype(bf16)
    earlier_rows = from_behind(normed, ALL, 1)
    earlier = dot(earlier_rows, fine_keyval).astype(bf16)
    key_rows = jnp.concatenate([earlier, keyvals], 0)
    span = key_rows.shape[0]
    key_heads = key_rows[:, :width].reshape(span, fine_heads, HEAD)
    value_heads = key_rows[:, width:].reshape(span, fine_heads, HEAD)
    query_heads = queries.reshape(tok_rows, fine_heads, HEAD)
    scores = jnp.einsum("qhd,khd->hqk", query_heads, key_heads, preferred_element_type=f32) * scale
    row_index = jnp.arange(tok_rows, dtype=jnp.int32)[:, None]
    col_index = jnp.arange(span, dtype=jnp.int32)[None, :]
    offset = row_index + WINDOW - col_index
    allowed = (offset >= 0) & (offset < WINDOW) & (start_row - WINDOW + col_index >= 0)
    scores = jnp.where(allowed[None], scores, big_negative)
    peak = jnp.max(scores, axis=-1, keepdims=True)
    terms = jnp.where(allowed[None], jnp.exp(scores - peak), 0.0)
    denom = jnp.sum(terms, axis=-1)
    mixed = jnp.einsum("hqk,khd->qhd", terms.astype(bf16), value_heads, preferred_element_type=f32)
    local = (mixed / jnp.transpose(denom)[..., None]).reshape(tok_rows, width).astype(bf16)
    return (inputs + dot(local, fine_out)).astype(bf16)


def attention_kernel(place_ref, q_ref, *refs):
    chunks, out_ref = refs[:-1], refs[-1]
    tile = q_ref.shape[0]
    step = pl.program_id(0)
    q = q_ref[...]
    row = step * tile + lax.broadcasted_iota(jnp.int32, (tile, tile), 0)
    col = step * tile + lax.broadcasted_iota(jnp.int32, (tile, tile), 1)

    def position(index):
        return (index >> 6) * 512 + ((index >> 5) & 1) * 64 + (index & 31)

    ahead = position(row) - position(col)

    def update(state, kt, masked):
        peak, total, acc = state
        rows = pl.ds(pl.multiple_of(kt * tile, tile), tile)
        scores = []
        for j, chunk in enumerate(chunks):
            s = lax.dot_general(
                q, chunk[rows, :HEAD], (((1,), (1,)), ((), ())), preferred_element_type=f32
            )
            if masked:
                s = jnp.where(ahead > place_ref[j], s, big_negative)
            scores.append(s)
        top = functools.reduce(jnp.maximum, scores)
        new_peak = jnp.maximum(peak, jnp.max(top, axis=-1, keepdims=True))
        fade = jnp.exp2(peak - new_peak)
        acc = acc * fade
        sums = None
        for j, chunk in enumerate(chunks):
            p = jnp.exp2(scores[j] - new_peak)
            if masked:
                p = jnp.where(ahead > place_ref[j], p, 0.0)
            sums = p if sums is None else sums + p
            acc = acc + dot(p.astype(bf16), chunk[rows, HEAD:])
        total = total * fade + jnp.sum(sums, axis=-1, keepdims=True)
        return new_peak, total, acc

    state = (
        jnp.full((tile, 1), big_negative, f32),
        jnp.zeros((tile, 1), f32),
        jnp.zeros((tile, HEAD), f32),
    )
    state = lax.fori_loop(0, step, lambda kt, st: update(st, kt, False), state)
    _, total, acc = update(state, step, True)
    out_ref[...] = (acc / jnp.where(total > 0.0, total, 1.0)).astype(bf16)


def coarse_attention(q, chunks, places, tile=256):
    rows = q.shape[0]
    whole = pl.BlockSpec(chunks[0].shape, lambda i, place: (0, 0))
    return pl.pallas_call(
        attention_kernel,
        out_shape=jax.ShapeDtypeStruct((rows, HEAD), bf16),
        grid_spec=pltpu.PrefetchScalarGridSpec(
            num_scalar_prefetch=1,
            grid=(rows // tile,),
            in_specs=[pl.BlockSpec((tile, HEAD), lambda i, place: (i, 0))] + [whole] * len(chunks),
            out_specs=pl.BlockSpec((tile, HEAD), lambda i, place: (i, 0)),
        ),
        compiler_params=pltpu.CompilerParams(vmem_limit_bytes=48 << 20),
    )(places, q, *chunks)


def in_lanes(array):
    rows, cols = array.shape
    return jnp.transpose(array.reshape(rows, cols // 128, 128), (1, 0, 2)).reshape(-1, 128)


def out_of_lanes(array, rows):
    n = array.shape[-2] // rows
    parts = array.reshape(*array.shape[:-2], n, rows, 128)
    parts = jnp.swapaxes(parts, -3, -2)
    return parts.reshape(*array.shape[:-2], rows, n * 128)


def summed_piece(partial):
    core = lax.axis_index("c")
    heads, rows, _ = partial.shape
    parts = partial.reshape(heads, 2, 4, rows // 8, 128)
    keep = lax.dynamic_index_in_dim(parts, core, 1, keepdims=False)
    give = lax.dynamic_index_in_dim(parts, 1 - core, 1, keepdims=False)
    got = rotated(give.astype(bf16), "c", 1)
    both = (keep + got.astype(f32)).astype(bf16)
    pieces = jnp.swapaxes(both, 0, 1).reshape(8, rows // 8, 128)
    pieces = exchanged(pieces, ("x", "yl"))
    return jnp.sum(pieces.astype(f32), axis=0).astype(bf16)


def body(
    tokens,
    fine_gain,
    fine_query,
    fine_keyval,
    fine_out,
    down_weight,
    coarse_gain,
    coarse_query,
    coarse_keyval,
    coarse_out,
    up_weight,
):
    width = tokens.shape[1]
    wide = coarse_gain.shape[0]
    cols = coarse_query.shape[1]
    yh, z, x, yl, c = (lax.axis_index(a) for a in ALL)
    s, t = lax.axis_index(SEQ), lax.axis_index(TP)
    n_seq, n_tp = lax.axis_size(SEQ), lax.axis_size(TP)
    swap = [(b * n_tp + a, a * n_tp + b) for a in range(n_seq) for b in range(n_tp)]

    with jax.named_scope("weights"):
        rows_sent = jnp.concatenate([coarse_query, coarse_keyval[:, 0], coarse_keyval[:, 1]], 1)
        rows_here = lax.ppermute(rows_sent, ALL, swap)
        out_sent = lax.dynamic_slice(coarse_out, (0, s * cols), (cols, cols))
        out_here = lax.ppermute(out_sent, ALL, swap)

    fine_state = fine_layer(tokens, fine_gain, fine_query, fine_keyval, fine_out)
    run_count = tokens.shape[0] // SHORT
    pooled = jnp.mean(fine_state.astype(f32).reshape(run_count, SHORT, width), axis=1).astype(bf16)

    with jax.named_scope("gather_rows"):
        row_before = from_behind(pooled[run_count - 1 :], ALL, 1)
        z_rows = gathered(pooled, ("z",))
        z_before = gathered(row_before, ("z",))
        all_rows = gathered(z_rows, ("yh", "yl")).reshape(-1, width)
        all_before = gathered(z_before, ("yh", "yl")).reshape(-1, width)

    with jax.named_scope("weights"):
        gain = lax.dynamic_slice(coarse_gain, (t * cols,), (cols,))
        scaled = (rows_here.astype(f32) * gain[:, None]).astype(bf16)
        part = dot(down_weight, scaled)
        slot_rows = lax.dynamic_slice(down_weight, (128 * z + 64 * yh, 0), (64, cols))
        gram = lax.dot_general(
            slot_rows, down_weight, (((1,), (1,)), ((), ())), preferred_element_type=f32
        )
        first = jnp.stack(
            [
                jnp.concatenate(
                    [part[:, j * cols + k * HEAD : j * cols + (k + 1) * HEAD] for j in range(3)]
                    + [in_lanes(gram[32 * k : 32 * k + 32])],
                    0,
                )
                for k in range(2)
            ]
        )
        first = gathered(summed_piece(first), ("x", "c"))
        first = jnp.swapaxes(first.reshape(4, 2, -1, 128), 0, 1).reshape(-1, 128)
        proj = out_of_lanes(first[: 3 * width], width)
        gram_slot = out_of_lanes(first[3 * width :], 32)
        after = dot(out_here, up_weight)
        direct = dot(slot_rows, up_weight)
        second = jnp.stack(
            [
                jnp.concatenate(
                    [
                        in_lanes(after[HEAD * k : HEAD * (k + 1)]),
                        in_lanes(direct[32 * k : 32 * k + 32]),
                    ],
                    0,
                )
                for k in range(2)
            ]
        )
        second = gathered(summed_piece(second), ("yh", "yl", "x", "c"))
        second = jnp.swapaxes(second.reshape(4, 4, 2, -1, 128), 1, 2).reshape(4, -1, 128)
        after_all = out_of_lanes(second[:, :width], HEAD).reshape(4 * HEAD, width)
        direct_all = out_of_lanes(second[:, width:], 32).reshape(HEAD, width)

    with jax.named_scope("project"):
        y = yh * 2 + yl
        rows_slot = lax.dynamic_slice(all_rows, (0, 128 * z + 32 * y), (all_rows.shape[0], 32))
        before_slot = lax.dynamic_slice(
            all_before, (0, 128 * z + 32 * y), (all_before.shape[0], 32)
        )

        def square_part(rows, slot):
            product = lax.dot_general(
                rows, gram_slot, (((1,), (1,)), ((), ())), preferred_element_type=f32
            )
            return jnp.sum(product * slot.astype(f32), axis=-1)

        squares = jnp.concatenate(
            [square_part(all_rows, rows_slot), square_part(all_before, before_slot)]
        )
        squares = jnp.sum(gathered(squares[None], ("yh", "yl", "z")), axis=(0, 1))
        inverse = lax.rsqrt(jnp.maximum(squares, 0.0) / wide + epsilon)[:, None]
        n = all_rows.shape[0]
        qkv = dot(all_rows, proj)
        q_before = dot(all_before, proj[:, :HEAD])
        factor = math.log2(math.e) / math.sqrt(HEAD)

        def by_row(values):
            parts = values.reshape(2, 2, 8, run_count, values.shape[-1])
            return jnp.swapaxes(parts, 1, 2).reshape(n, values.shape[-1])

        kv = by_row((qkv[:, HEAD:] * inverse[:n]).astype(bf16))
        q = (qkv[:, :HEAD] * (inverse[:n] * factor)).reshape(-1, run_count, HEAD)
        q_before = (q_before * (inverse[n:] * factor)).reshape(-1, 1, HEAD)
        q = jnp.concatenate([q_before, q[:, : run_count - 1]], 1).astype(bf16).reshape(n, HEAD)
        q = by_row(q)

    with jax.named_scope("attention"):
        chunks, places = [], []
        for by in (0, 1, 3, 2):
            mine = kv if by == 0 else rotated(kv, "x", by)
            other = rotated(mine, "c", 1)
            shift = 128 * ((x + 4 - by) % 4 - x)
            chunks += [mine, other]
            places += [shift, shift + 32 * (1 - 2 * c)]
        heads = coarse_attention(q, chunks, jnp.stack(places).astype(jnp.int32))

    with jax.named_scope("lift"):
        heads = jnp.swapaxes(heads.reshape(2, 8, 2, run_count, HEAD), 1, 2)
        heads = exchanged(heads.reshape(4, 8 * run_count, HEAD), ("yh", "yl"))
        heads = jnp.swapaxes(heads, 0, 1).reshape(8 * run_count, 4 * HEAD)
        shifted = jnp.concatenate(
            [z_before.reshape(8, 1, width), z_rows.reshape(8, run_count, width)[:, : run_count - 1]],
            1,
        ).reshape(8 * run_count, width)
        shifted = lax.dynamic_slice(shifted, (0, 128 * z), (8 * run_count, HEAD))
        lifted = (dot(heads, after_all) + dot(shifted, direct_all)).astype(bf16)
        lifted = exchanged(lifted.reshape(8, run_count, width), ("z",))
        lifted = jnp.sum(lifted.astype(f32), axis=0)
        result = fine_state.astype(f32) + jnp.repeat(lifted, SHORT, axis=0)
    return result.astype(bf16)


def solution(mesh):
    fine = Mesh(mesh.devices.reshape(2, 8, 4, 2, 2), ALL)
    return jax.shard_map(
        body,
        mesh=fine,
        in_specs=(
            P(ALL, None),
            P(),
            P(),
            P(),
            P(),
            P(None, TP),
            P(),
            P(SEQ, TP),
            P(SEQ, None, TP),
            P(TP, None),
            P(TP, None),
        ),
        out_specs=P(ALL, None),
        check_vma=False,
    )
```

time: 536 us -> 321 us (0.60)
  waiting for transfers between devices: 322 us -> 97.4 us
  starting transfers between devices: 5.73 us -> 83.8 us
  matrix products: 63.3 us -> 23.2 us
  blocking collectives: 82.8 us -> 48.8 us
  Pallas kernels: 0 us -> 12.9 us
  between operations: 13.3 us -> 0.7 us
  local copies, waits for them, and re-layouts: 14.1 us -> 24.2 us
  other arithmetic: 34.2 us -> 26.3 us
    all_gather x4 -> x0, waiting for transfers between devices: 309 us -> none  [the longest x1 141 us: body(): piece = lax.all_gather(coarse_kv, 'seq', axis=0, tiled=True)]
    all_to_all x0 -> x8, starting transfers between devices: none -> 59.3 us  [the longest x6 51 us: gathered(): return lax.all_to_all(copies, axes, split_axis=0, concat_axis=0, tiled=True)]
    all_to_all x0 -> x8, waiting for transfers between devices: none -> 56.6 us  [the longest x6 50.1 us: gathered(): return lax.all_to_all(copies, axes, split_axis=0, concat_axis=0, tiled=True)]
    all_to_all x3, blocking collectives: 82.8 us -> 48.8 us  [the longest x2 32.4 us: exchanged(): return lax.all_to_all(pieces, axes, split_axis=0, concat_axis=0, tiled=True)]
    ppermute x0 -> x11, waiting for transfers between devices: none -> 30.7 us  [the longest x9 30.6 us: rotated(): lax.ppermute(array, axis, [(i, (i + by) % size) for i in range(size)])]
    dot_general x12 -> x16, matrix products: 47.5 us -> 23.2 us  [the longest x11 19.1 us: dot(): return jnp.dot(a, b, preferred_element_type=f32)]
    ppermute x0 -> x11, starting transfers between devices: none -> 18.9 us  [the longest x9 9.14 us: rotated(): lax.ppermute(array, axis, [(i, (i + by) % size) for i in range(size)])]
    cond x1 -> x0, matrix products: 15.8 us -> none  [body(): lax.cond(jnp.int32(0) < my_first + coarse_rows, lambda: online_update(ini...]
  transfers between devices with their start and end apart: 6 -> 21, of which waited for: 6 -> 13; matrix products, arithmetic and copies ran while one was open for 4% -> 19% of each run, Pallas kernels for 0% -> 4%
where the time goes in v1:
time: 321 us; the launch traced here: 317 us
  waiting for transfers between devices  97.4 us (30%)
  starting transfers between devices  83.8 us (26%)
  blocking collectives  48.8 us (15%)
  other arithmetic  26.3 us (8%)
  local copies, waits for them, and re-layouts  24.2 us (8%)
  matrix products  23.2 us (7%)
  Pallas kernels  12.9 us (4%)
    all_to_all x6, starting transfers between devices, gathered(): return lax.all_to_all(copies, axes, split_axis=0, concat_axis=0, tiled=True)  51 us
    all_to_all x6, waiting for transfers between devices, gathered(): return lax.all_to_all(copies, axes, split_axis=0, concat_axis=0, tiled=True)  50.1 us
    all_to_all x2, blocking collectives, exchanged(): return lax.all_to_all(pieces, axes, split_axis=0, concat_axis=0, tiled=True)  32.4 us
    ppermute x9, waiting for transfers between devices, rotated(): lax.ppermute(array, axis, [(i, (i + by) % size) for i in range(size)])  30.6 us
    dot_general x11, matrix products, dot(): return jnp.dot(a, b, preferred_element_type=f32)  19.1 us
    all_to_all x1, blocking collectives, gathered(): return lax.all_to_all(copies, axes, split_axis=0, concat_axis=0, tiled=True)  16.4 us
    pallas_call x1, Pallas kernels, coarse_attention(): pl.pallas_call(attention_kernel, out_shape=jax.ShapeDtypeStruct((rows, HE...  12.9 us
    ppermute x2, waiting for transfers between devices, from_behind(): return lax.ppermute(array, axis, pairs)  10.1 us
  transfers between devices with their start and end apart: 21, of which 13 were waited for; matrix products, arithmetic and copies ran while one was open for 19% of the time, Pallas kernels for 4%

profile of v1, /device:TPU:16, one launch (start us, length us, event | category | flops | bytes accessed | tf_op | source)
XLA Modules:
  0.0 317.2 jit_solution(12297038148510202966)
XLA Ops:
  0.0 1.6 fusion.79
  1.7 1.7 pad_maximum_fusion.6
  3.4 4.7 %collective-permute-start.2 = (bf16[256,768]{1,0:T(8,128)(2,1)}, bf16[256,768]{1,0:T(8,128)(2,1)}, u32[]{:S(2)}, u32[]{:S(2)}) collective-permute-start(bf16[256,768]{1,0:T(8,128)(2,1)} %pad_maximum_fusion.6), channel_id=1, source_target_pairs={{0,0},{16,1},{32,2},{48,3},{64,4},{80,5},{96,6},{112,7},{128,8},{1... | collective-permute-start | bytes 1179656 | tf_op jit(solution)/shard_map/weights/ppermute | solution.py:196
  8.3 1.0 fusion.32
  9.3 3.4 %collective-permute-start = (bf16[256,1024]{1,0:T(8,128)(2,1)}, bf16[256,1024]{1,0:T(8,128)(2,1)}, u32[]{:S(2)}, u32[]{:S(2)}) collective-permute-start(bf16[256,1024]{1,0:T(8,128)(2,1)} %fusion.32), channel_id=1, source_target_pairs={{0,1},{1,2},{2,3},{3,4},{4,5},{5,6},{6,7},{7,8},{8,9},{9,10},{10,1... | collective-permute-start | bytes 1572872 | tf_op jit(solution)/shard_map/ppermute | solution.py:28
  12.7 0.9 constant_dynamic-slice_fusion
  13.6 5.0 %collective-permute-start.11 = (bf16[256,256]{1,0:T(8,128)(2,1)S(1)}, bf16[256,256]{1,0:T(8,128)(2,1)S(1)}, u32[]{:S(2)}, u32[]{:S(2)}) collective-permute-start(bf16[256,256]{1,0:T(8,128)(2,1)S(1)} %constant_dynamic-slice_fusion), channel_id=1, source_target_pairs={{0,0},{16,1},{32,2},{48,3},{64,4},{80,5},{96,6},{112,7},{128,8},{1... | collective-permute-start | bytes 393224 | tf_op jit(solution)/shard_map/weights/ppermute | solution.py:198
  19.9 4.8 %convolution_convert_fusion = bf16[256,2048]{1,0:T(8,128)(2,1)} fusion(bf16[256,1024]{1,0:T(8,128)(2,1)} %fusion.32, bf16[1024,2048]{1,0:T(8,128)(2,1)} %param.14), kind=kOutput, calls=%fused_computation.8 | convolution fusion | flops 1074266112 | bytes 5767168 | tf_op jit(solution)/shard_map/dot_general | solution.py:51
  24.7 2.7 fusion.24
  28.4 0.8 fusion.56
  30.8 1.9 collective-permute-start.12
  32.7 1.7 convolution_bitcast_fusion
  34.4 1.3 fusion.78
  35.7 1.3 pad_maximum_fusion
  37.0 2.7 copy.151
  39.7 2.7 pad_maximum_fusion.1
  42.4 2.7 copy.154
  45.1 2.6 fusion.43
  48.0 2.4 convolution_convert_fusion.1
  50.4 1.6 fusion.41
  51.9 2.3 copy.176
  54.2 2.1 fusion.37
  56.4 2.5 fusion.81
  58.9 0.8 fusion.21
  59.9 1.7 fusion.28
  61.7 2.2 collective-permute-start.1
  64.0 10.1 %collective-permute-done.1 = bf16[1,1024]{1,0:T(2,128)(2,1)S(1)} collective-permute-done((bf16[1,1024]{1,0:T(2,128)(2,1)S(1)}, bf16[1,1024]{1,0:T(2,128)(2,1)S(1)}, u32[]{:S(2)}, u32[]{:S(2)}) %collective-permute-start.1) | collective-permute-done | bytes 2080 | tf_op jit(solution)/shard_map/gather_rows/ppermute | solution.py:28
  75.9 24.1 %all-to-all-start = ((bf16[8,2,512]{2,1,0:T(2,128)(2,1)}), bf16[8,2,512]{2,1,0:T(2,128)(2,1)S(1)}, u32[]{:S(2)}, u32[]{:S(2)}) async-start(bf16[8,2,512]{2,1,0:T(2,128)(2,1)} %reshape.261), calls=%async_computation | async-start | bytes 32768 | tf_op jit(solution)/shard_map/gather_rows/all_to_all | solution.py:38
  100.0 7.8 %all-to-all-done = bf16[8,2,512]{2,1,0:T(2,128)(2,1)S(1)} async-done(((bf16[8,2,512]{2,1,0:T(2,128)(2,1)}), bf16[8,2,512]{2,1,0:T(2,128)(2,1)S(1)}, u32[]{:S(2)}, u32[]{:S(2)}) %all-to-all-start) | async-done | bytes 16416 | tf_op jit(solution)/shard_map/gather_rows/all_to_all | solution.py:38
  108.5 4.8 %all-to-all-start.1 = ((bf16[4,8,1,1024]{3,1,2,0:T(8,128)(2,1)}), bf16[4,8,1,1024]{3,1,2,0:T(8,128)(2,1)S(1)}, u32[]{:S(2)}, u32[]{:S(2)}) async-start(bf16[4,8,1,1024]{3,1,2,0:T(8,128)(2,1)} %broadcast_in_dim.57), calls=%async_computation.1 | async-start | bytes 131072 | tf_op jit(solution)/shard_map/gather_rows/all_to_all | solution.py:38
  113.3 1.8 fusion.49
  115.0 1.3 all-to-all-done.1
  116.4 3.4 %all-to-all-start.8 = ((bf16[8,160,128]{2,1,0:T(8,128)(2,1)}), bf16[8,160,128]{2,1,0:T(8,128)(2,1)S(1)}, u32[]{:S(2)}, u32[]{:S(2)}) async-start(bf16[8,160,128]{2,1,0:T(8,128)(2,1)} %bitcast.66), calls=%async_computation.8 | async-start | bytes 655360 | tf_op jit(solution)/shard_map/weights/all_to_all | solution.py:42
  119.8 1.6 fusion.42
  121.5 5.5 %all-to-all-done.8 = bf16[8,160,128]{2,1,0:T(8,128)(2,1)S(1)} async-done(((bf16[8,160,128]{2,1,0:T(8,128)(2,1)}), bf16[8,160,128]{2,1,0:T(8,128)(2,1)S(1)}, u32[]{:S(2)}, u32[]{:S(2)}) %all-to-all-start.8) | async-done | bytes 327712 | tf_op jit(solution)/shard_map/weights/all_to_all | solution.py:42
  127.0 13.4 %all_to_all.58 = bf16[8,416,128]{2,1,0:T(8,128)(2,1)S(1)} all-to-all(bf16[8,416,128]{2,1,0:T(8,128)(2,1)S(1)} %bitcast.222), channel_id=1, replica_groups=mesh['yh'=2,'z'=8,'x'=4,'yl'=2,'c'=2] {'x','yl'}, dimensions={0} | all-to-all | bytes 1703936 | tf_op jit(solution)/shard_map/weights/all_to_all | solution.py:42
  140.3 0.9 broadcast_in_dim.59
  141.2 3.5 %all-to-all-start.4 = ((bf16[8,32,1024]{2,1,0:T(8,128)(2,1)}), bf16[8,32,1024]{2,1,0:T(8,128)(2,1)S(1)}, u32[]{:S(2)}, u32[]{:S(2)}) async-start(bf16[8,32,1024]{2,1,0:T(8,128)(2,1)} %broadcast_in_dim.59), calls=%async_computation.4 | async-start | bytes 1048576 | tf_op jit(solution)/shard_map/gather_rows/all_to_all | solution.py:38
  144.8 13.1 %all-to-all-done.4 = bf16[8,32,1024]{2,1,0:T(8,128)(2,1)S(1)} async-done(((bf16[8,32,1024]{2,1,0:T(8,128)(2,1)}), bf16[8,32,1024]{2,1,0:T(8,128)(2,1)S(1)}, u32[]{:S(2)}, u32[]{:S(2)}) %all-to-all-start.4) | async-done | bytes 524320 | tf_op jit(solution)/shard_map/gather_rows/all_to_all | solution.py:38
  158.0 16.4 %all_to_all.59 = bf16[8,416,128]{2,1,0:T(8,128)(2,1)S(1)} all-to-all(bf16[8,416,128]{2,1,0:T(8,128)(2,1)S(1)} %broadcast_in_dim.58), channel_id=1, replica_groups=mesh['yh'=2,'z'=8,'x'=4,'yl'=2,'c'=2] {'x','c'}, dimensions={0} | all-to-all | bytes 1703936 | tf_op jit(solution)/shard_map/weights/all_to_all | solution.py:38
  174.4 1.6 broadcast_in_dim.60
  176.0 6.1 %all-to-all-start.5 = ((bf16[4,8,32,1024]{3,2,1,0:T(8,128)(2,1)}), bf16[4,8,32,1024]{3,2,1,0:T(8,128)(2,1)S(1)}, u32[]{:S(2)}, u32[]{:S(2)}) async-start(bf16[4,8,32,1024]{3,2,1,0:T(8,128)(2,1)} %broadcast_in_dim.60), calls=%async_computation.5 | async-start | bytes 4194304 | tf_op jit(solution)/shard_map/gather_rows/all_to_all | solution.py:38
  182.5 1.2 copy.157
  183.9 21.8 %all-to-all-done.5 = bf16[4,8,32,1024]{3,2,1,0:T(8,128)(2,1)S(1)} async-done(((bf16[4,8,32,1024]{3,2,1,0:T(8,128)(2,1)}), bf16[4,8,32,1024]{3,2,1,0:T(8,128)(2,1)S(1)}, u32[]{:S(2)}, u32[]{:S(2)}) %all-to-all-start.5) | async-done | bytes 2097184 | tf_op jit(solution)/shard_map/gather_rows/all_to_all | solution.py:38
  207.5 6.6 %all-to-all-start.6 = ((f32[32,1,1056]{2,1,0:T(1,128)}), f32[32,1,1056]{2,1,0:T(1,128)S(1)}, u32[]{:S(2)}, u32[]{:S(2)}) async-start(f32[32,1,1056]{2,1,0:T(1,128)} %broadcast_in_dim.61), calls=%async_computation.6 | async-start | bytes 294912 | tf_op jit(solution)/shard_map/project/all_to_all | solution.py:38
  214.1 2.4 fusion.82
  216.5 6.1 %all-to-all-done.6 = f32[32,1,1056]{2,1,0:T(1,128)S(1)} async-done(((f32[32,1,1056]{2,1,0:T(1,128)}), f32[32,1,1056]{2,1,0:T(1,128)S(1)}, u32[]{:S(2)}, u32[]{:S(2)}) %all-to-all-start.6) | async-done | bytes 135200 | tf_op jit(solution)/shard_map/project/all_to_all | solution.py:38
  222.6 1.2 broadcast_in_dim.62
  223.9 5.9 %all-to-all-start.9 = ((bf16[32,160,128]{2,1,0:T(8,128)(2,1)}), bf16[32,160,128]{2,1,0:T(8,128)(2,1)S(1)}, u32[]{:S(2)}, u32[]{:S(2)}) async-start(bf16[32,160,128]{2,1,0:T(8,128)(2,1)} %broadcast_in_dim.62), calls=%async_computation.9 | async-start | bytes 2621440 | tf_op jit(solution)/shard_map/weights/all_to_all | solution.py:38
  229.8 1.0 reduce_sum.93
  230.8 1.4 fusion.40
  232.3 3.3 %collective-permute-start.9 = (bf16[1024,256]{1,0:T(8,128)(2,1)S(1)}, bf16[1024,256]{1,0:T(8,128)(2,1)S(1)}, u32[]{:S(2)}, u32[]{:S(2)}) collective-permute-start(bf16[1024,256]{1,0:T(8,128)(2,1)S(1)} %bitcast.195), channel_id=1, source_target_pairs={{0,8},{4,12},{8,0},{12,4},{1,9},{5,13},{9,1},{13,5},{2,10},{6,14},... | collective-permute-start | bytes 1572872 | tf_op jit(solution)/shard_map/attention/ppermute | solution.py:33
  236.2 2.7 collective-permute-start.7
  239.0 1.2 fusion.52
  240.3 19.4 %collective-permute-done.9.refs_6_ = bf16[1024,256]{1,0:T(8,128)(2,1)S(1)} collective-permute-done((bf16[1024,256]{1,0:T(8,128)(2,1)S(1)}, bf16[1024,256]{1,0:T(8,128)(2,1)S(1)}, u32[]{:S(2)}, u32[]{:S(2)}) %collective-permute-start.9) | collective-permute-done | bytes 524320 | tf_op jit(solution)/shard_map/attention/ppermute | solution.py:33
  259.8 10.4 %collective-permute-done.5.refs_2_ = bf16[1024,256]{1,0:T(8,128)(2,1)S(1)} collective-permute-done((bf16[1024,256]{1,0:T(8,128)(2,1)S(1)}, bf16[1024,256]{1,0:T(8,128)(2,1)S(1)}, u32[]{:S(2)}, u32[]{:S(2)}) %collective-permute-start.5) | collective-permute-done | bytes 524320 | tf_op jit(solution)/shard_map/attention/ppermute | solution.py:33
  270.6 1.1 fusion.26
  272.8 12.9 %attention.1 = bf16[1024,128]{1,0:T(8,128)(2,1)S(1)} custom-call(s32[8]{0:T(128)S(1)} %stack.53.place_ref, bf16[1024,128]{1,0:T(8,128)(2,1)S(1)} %bitcast.200, bf16[1024,256]{1,0:T(8,128)(2,1)S(1)} %bitcast.199, bf16[1024,256]{1,0:T(8,128)(2,1)S(1)} %collective-permute-done.4.refs_1_, bf16[1024,256]{1,0:T(8,128)(2,1)S(1)} %collective-permute-done.5.refs_2_, ...), custom_call_target="tpu_custom_call" | custom-call | tf_op jit(solution)/shard_map/attention/pallas_call | solution.py:135
  286.4 4.8 %all-to-all-start.7 = ((bf16[4,256,128]{2,1,0:T(8,128)(2,1)}), bf16[4,256,128]{2,1,0:T(8,128)(2,1)S(1)}, u32[]{:S(2)}, u32[]{:S(2)}) async-start(bf16[4,256,128]{2,1,0:T(8,128)(2,1)} %bitcast.48), calls=%async_computation.7 | async-start | bytes 524288 | tf_op jit(solution)/shard_map/lift/all_to_all | solution.py:42
  291.2 2.0 pad_maximum_fusion.5
  294.2 1.0 all-to-all-done.7
  295.8 1.3 fusion.20
  297.1 19.1 %all_to_all.60 = bf16[8,32,1024]{2,1,0:T(8,128)(2,1)S(1)} all-to-all(bf16[8,32,1024]{2,1,0:T(8,128)(2,1)S(1)} %bitcast.227), channel_id=1, replica_groups=mesh['yh'=2,'z'=8,'x'=4,'yl'=2,'c'=2] {'z'}, dimensions={0} | all-to-all | bytes 1048576 | tf_op jit(solution)/shard_map/lift/all_to_all | solution.py:42
  316.3 0.9 fusion.29
  (118 shorter events, 14.3 us)
Async XLA Ops:
  0.0 59.7 %copy-start = (bf16[1024,1024]{1,0:T(8,128)(2,1)S(1)}, bf16[1024,1024]{1,0:T(8,128)(2,1)}, u32[]{:S(2)}) copy-start(bf16[1024,1024]{1,0:T(8,128)(2,1)} %param.15) | copy-start | bytes 6291460
  0.0 8.1 %copy-start.4 = (bf16[256,1024]{1,0:T(8,128)(2,1)S(1)}, bf16[256,1024]{1,0:T(8,128)(2,1)}, u32[]{:S(2)}) copy-start(bf16[256,1024]{1,0:T(8,128)(2,1)} %param.11) | copy-start | bytes 1572868
  0.0 8.3 %copy-start.16 = (f32[1024]{0:T(1024)S(1)}, f32[1024]{0:T(1024)}, u32[]{:S(2)}) copy-start(f32[1024]{0:T(1024)} %param.12) | copy-start | bytes 12292
  0.0 18.7 %copy-start.6 = (bf16[1024,256]{1,0:T(8,128)(2,1)S(1)}, bf16[1024,256]{1,0:T(8,128)(2,1)}, u32[]{:S(2)}) copy-start(bf16[1024,256]{1,0:T(8,128)(2,1)} %param.16) | copy-start | bytes 1572868
  3.4 29.3 %collective-permute-start.2 = (bf16[256,768]{1,0:T(8,128)(2,1)}, bf16[256,768]{1,0:T(8,128)(2,1)}, u32[]{:S(2)}, u32[]{:S(2)}) collective-permute-start(bf16[256,768]{1,0:T(8,128)(2,1)} %pad_maximum_fusion.6), channel_id=1, source_target_pairs={{0,0},{16,1},{32,2},{48,3},{64,4},{80,5},{96,6},{112,7},{128,8},{1... | collective-permute-start | bytes 1179656 | tf_op jit(solution)/shard_map/weights/ppermute | solution.py:196
  9.3 38.6 %collective-permute-start = (bf16[256,1024]{1,0:T(8,128)(2,1)}, bf16[256,1024]{1,0:T(8,128)(2,1)}, u32[]{:S(2)}, u32[]{:S(2)}) collective-permute-start(bf16[256,1024]{1,0:T(8,128)(2,1)} %fusion.32), channel_id=1, source_target_pairs={{0,1},{1,2},{2,3},{3,4},{4,5},{5,6},{6,7},{7,8},{8,9},{9,10},{10,1... | collective-permute-start | bytes 1572872 | tf_op jit(solution)/shard_map/ppermute | solution.py:28
  13.6 15.8 %collective-permute-start.11 = (bf16[256,256]{1,0:T(8,128)(2,1)S(1)}, bf16[256,256]{1,0:T(8,128)(2,1)S(1)}, u32[]{:S(2)}, u32[]{:S(2)}) collective-permute-start(bf16[256,256]{1,0:T(8,128)(2,1)S(1)} %constant_dynamic-slice_fusion), channel_id=1, source_target_pairs={{0,0},{16,1},{32,2},{48,3},{64,4},{80,5},{96,6},{112,7},{128,8},{1... | collective-permute-start | bytes 393224 | tf_op jit(solution)/shard_map/weights/ppermute | solution.py:198
  19.9 4.8 %copy-start.18 = (bf16[1024,1024]{1,0:T(8,128)(2,1)S(1)}, bf16[1024,1024]{1,0:T(8,128)(2,1)}, u32[]{:S(2)}) copy-start(bf16[1024,1024]{1,0:T(8,128)(2,1)} %param.13) | copy-start | bytes 6291460
  24.7 2.7 copy-start.8
  29.9 2.8 copy-start.7
  30.8 82.5 %collective-permute-start.12 = (bf16[2,4,160,128]{3,2,0,1:T(8,128)(2,1)}, bf16[2,4,160,128]{3,2,0,1:T(8,128)(2,1)}, u32[]{:S(2)}, u32[]{:S(2)}) collective-permute-start(bf16[2,4,160,128]{3,2,0,1:T(8,128)(2,1)} %fusion.58), channel_id=1, source_target_pairs={{0,1},{1,0},{2,3},{3,2},{4,5},{5,4},{6,7},{7,6},{8,9},{9,8},{10,11... | collective-permute-start | bytes 983048 | tf_op jit(solution)/shard_map/weights/ppermute | solution.py:33
  34.4 1.3 copy-start.14
  45.1 2.9 copy-start.17
  47.7 2.6 copy-start.11
  47.7 72.1 %collective-permute-start.3 = (bf16[2,4,416,128]{3,2,1,0:T(8,128)(2,1)}, bf16[2,4,416,128]{3,2,1,0:T(8,128)(2,1)}, u32[]{:S(2)}, u32[]{:S(2)}) collective-permute-start(bf16[2,4,416,128]{3,2,1,0:T(8,128)(2,1)} %fusion.43), channel_id=1, source_target_pairs={{0,1},{1,0},{2,3},{3,2},{4,5},{5,4},{6,7},{7,6},{8,9},{9,8},{10,11... | collective-permute-start | bytes 2555912 | tf_op jit(solution)/shard_map/weights/ppermute | solution.py:33
  54.2 2.1 copy-start.15
  56.4 2.5 copy-start.10
  58.9 1.0 copy-start.5
  61.7 58.1 %copy-start.2 = (f32[3328,128]{1,0:T(8,128)S(1)}, f32[3328,128]{1,0:T(8,128)}, u32[]{:S(2)}) copy-start(f32[3328,128]{1,0:T(8,128)} %copy.151) | copy-start | bytes 5111812
  61.7 12.3 %collective-permute-start.1 = (bf16[1,1024]{1,0:T(2,128)(2,1)S(1)}, bf16[1,1024]{1,0:T(2,128)(2,1)S(1)}, u32[]{:S(2)}, u32[]{:S(2)}) collective-permute-start(bf16[1,1024]{1,0:T(2,128)(2,1)S(1)} %slice.118), channel_id=1, source_target_pairs={{0,1},{1,2},{2,3},{3,4},{4,5},{5,6},{6,7},{7,8},{8,9},{9,10},{10,1... | collective-permute-start | bytes 6152 | tf_op jit(solution)/shard_map/gather_rows/ppermute | solution.py:28
  75.9 31.9 %all-to-all-start = ((bf16[8,2,512]{2,1,0:T(2,128)(2,1)}), bf16[8,2,512]{2,1,0:T(2,128)(2,1)S(1)}, u32[]{:S(2)}, u32[]{:S(2)}) async-start(bf16[8,2,512]{2,1,0:T(2,128)(2,1)} %reshape.261), calls=%async_computation | async-start | bytes 32768 | tf_op jit(solution)/shard_map/gather_rows/all_to_all | solution.py:38
  108.5 7.9 %all-to-all-start.1 = ((bf16[4,8,1,1024]{3,1,2,0:T(8,128)(2,1)}), bf16[4,8,1,1024]{3,1,2,0:T(8,128)(2,1)S(1)}, u32[]{:S(2)}, u32[]{:S(2)}) async-start(bf16[4,8,1,1024]{3,1,2,0:T(8,128)(2,1)} %broadcast_in_dim.57), calls=%async_computation.1 | async-start | bytes 131072 | tf_op jit(solution)/shard_map/gather_rows/all_to_all | solution.py:38
  116.4 10.6 %all-to-all-start.8 = ((bf16[8,160,128]{2,1,0:T(8,128)(2,1)}), bf16[8,160,128]{2,1,0:T(8,128)(2,1)S(1)}, u32[]{:S(2)}, u32[]{:S(2)}) async-start(bf16[8,160,128]{2,1,0:T(8,128)(2,1)} %bitcast.66), calls=%async_computation.8 | async-start | bytes 655360 | tf_op jit(solution)/shard_map/weights/all_to_all | solution.py:42
  141.2 16.7 %all-to-all-start.4 = ((bf16[8,32,1024]{2,1,0:T(8,128)(2,1)}), bf16[8,32,1024]{2,1,0:T(8,128)(2,1)S(1)}, u32[]{:S(2)}, u32[]{:S(2)}) async-start(bf16[8,32,1024]{2,1,0:T(8,128)(2,1)} %broadcast_in_dim.59), calls=%async_computation.4 | async-start | bytes 1048576 | tf_op jit(solution)/shard_map/gather_rows/all_to_all | solution.py:38
  157.9 18.1 %copy-start.3 = (bf16[8,32,1024]{2,1,0:T(8,128)(2,1)}, bf16[8,32,1024]{2,1,0:T(8,128)(2,1)S(1)}, u32[]{:S(2)}) copy-start(bf16[8,32,1024]{2,1,0:T(8,128)(2,1)S(1)} %all-to-all-done.4) | copy-start | bytes 1572868
  176.0 29.7 %all-to-all-start.5 = ((bf16[4,8,32,1024]{3,2,1,0:T(8,128)(2,1)}), bf16[4,8,32,1024]{3,2,1,0:T(8,128)(2,1)S(1)}, u32[]{:S(2)}, u32[]{:S(2)}) async-start(bf16[4,8,32,1024]{3,2,1,0:T(8,128)(2,1)} %broadcast_in_dim.60), calls=%async_computation.5 | async-start | bytes 4194304 | tf_op jit(solution)/shard_map/gather_rows/all_to_all | solution.py:38
  183.7 30.4 %copy-start.12 = (bf16[3,1024,128]{1,2,0:T(8,128)(2,1)S(1)}, bf16[3,1024,128]{1,2,0:T(8,128)(2,1)}, u32[]{:S(2)}) copy-start(bf16[3,1024,128]{1,2,0:T(8,128)(2,1)} %copy.157) | copy-start | bytes 2359300
  207.5 15.2 %all-to-all-start.6 = ((f32[32,1,1056]{2,1,0:T(1,128)}), f32[32,1,1056]{2,1,0:T(1,128)S(1)}, u32[]{:S(2)}, u32[]{:S(2)}) async-start(f32[32,1,1056]{2,1,0:T(1,128)} %broadcast_in_dim.61), calls=%async_computation.6 | async-start | bytes 294912 | tf_op jit(solution)/shard_map/project/all_to_all | solution.py:38
  222.6 1.2 copy-start.13
  223.9 62.5 %all-to-all-start.9 = ((bf16[32,160,128]{2,1,0:T(8,128)(2,1)}), bf16[32,160,128]{2,1,0:T(8,128)(2,1)S(1)}, u32[]{:S(2)}, u32[]{:S(2)}) async-start(bf16[32,160,128]{2,1,0:T(8,128)(2,1)} %broadcast_in_dim.62), calls=%async_computation.9 | async-start | bytes 2621440 | tf_op jit(solution)/shard_map/weights/all_to_all | solution.py:38
  232.3 27.4 %collective-permute-start.9 = (bf16[1024,256]{1,0:T(8,128)(2,1)S(1)}, bf16[1024,256]{1,0:T(8,128)(2,1)S(1)}, u32[]{:S(2)}, u32[]{:S(2)}) collective-permute-start(bf16[1024,256]{1,0:T(8,128)(2,1)S(1)} %bitcast.195), channel_id=1, source_target_pairs={{0,8},{4,12},{8,0},{12,4},{1,9},{5,13},{9,1},{13,5},{2,10},{6,14},... | collective-permute-start | bytes 1572872 | tf_op jit(solution)/shard_map/attention/ppermute | solution.py:33
  235.6 34.5 %collective-permute-start.5 = (bf16[1024,256]{1,0:T(8,128)(2,1)S(1)}, bf16[1024,256]{1,0:T(8,128)(2,1)S(1)}, u32[]{:S(2)}, u32[]{:S(2)}) collective-permute-start(bf16[1024,256]{1,0:T(8,128)(2,1)S(1)} %bitcast.196), channel_id=1, source_target_pairs={{0,4},{4,8},{8,12},{12,0},{1,5},{5,9},{9,13},{13,1},{2,6},{6,10},{... | collective-permute-start | bytes 1572872 | tf_op jit(solution)/shard_map/attention/ppermute | solution.py:33
  236.2 33.9 %collective-permute-start.7 = (bf16[1024,256]{1,0:T(8,128)(2,1)S(1)}, bf16[1024,256]{1,0:T(8,128)(2,1)S(1)}, u32[]{:S(2)}, u32[]{:S(2)}) collective-permute-start(bf16[1024,256]{1,0:T(8,128)(2,1)S(1)} %bitcast.197), channel_id=1, source_target_pairs={{0,12},{4,0},{8,4},{12,8},{1,13},{5,1},{9,5},{13,9},{2,14},{6,2},{... | collective-permute-start | bytes 1572872 | tf_op jit(solution)/shard_map/attention/ppermute | solution.py:33
  238.9 33.0 %collective-permute-start.4 = (bf16[1024,256]{1,0:T(8,128)(2,1)S(1)}, bf16[1024,256]{1,0:T(8,128)(2,1)S(1)}, u32[]{:S(2)}, u32[]{:S(2)}) collective-permute-start(bf16[1024,256]{1,0:T(8,128)(2,1)S(1)} %bitcast.198), channel_id=1, source_target_pairs={{0,1},{1,0},{2,3},{3,2},{4,5},{5,4},{6,7},{7,6},{8,9},{9,8},{10,11... | collective-permute-start | bytes 1572872 | tf_op jit(solution)/shard_map/attention/ppermute | solution.py:33
  259.8 12.2 %collective-permute-start.10 = (bf16[1024,256]{1,0:T(8,128)(2,1)S(1)}, bf16[1024,256]{1,0:T(8,128)(2,1)S(1)}, u32[]{:S(2)}, u32[]{:S(2)}) collective-permute-start(bf16[1024,256]{1,0:T(8,128)(2,1)S(1)} %collective-permute-done.9.refs_6_), channel_id=1, source_target_pairs={{0,1},{1,0},{2,3},{3,2},{4,5},{5,4},{6,7},{7,6},{8,9},{9,8},{10,11... | collective-permute-start | bytes 1572872 | tf_op jit(solution)/shard_map/attention/ppermute | solution.py:33
  270.1 1.9 collective-permute-start.6
  270.1 2.7 collective-permute-start.8
  286.4 8.8 %all-to-all-start.7 = ((bf16[4,256,128]{2,1,0:T(8,128)(2,1)}), bf16[4,256,128]{2,1,0:T(8,128)(2,1)S(1)}, u32[]{:S(2)}, u32[]{:S(2)}) async-start(bf16[4,256,128]{2,1,0:T(8,128)(2,1)} %bitcast.48), calls=%async_computation.7 | async-start | bytes 524288 | tf_op jit(solution)/shard_map/lift/all_to_all | solution.py:42
  295.8 20.5 %copy-start.9 = (bf16[256,1024]{1,0:T(8,128)(2,1)S(1)}, bf16[256,1024]{1,0:T(8,128)(2,1)}, u32[]{:S(2)}) copy-start(bf16[256,1024]{1,0:T(8,128)(2,1)} %get-tuple-element.26) | copy-start | bytes 1572868
  295.8 21.4 %copy-start.1 = (bf16[1024,1024]{1,0:T(8,128)(2,1)S(1)}, bf16[1024,1024]{1,0:T(8,128)(2,1)}, u32[]{:S(2)}) copy-start(bf16[1024,1024]{1,0:T(8,128)(2,1)} %param.15) | copy-start | bytes 6291460

commit v2 on v1

v2 whole, which is shorter than its diff:
```python
import functools
import math

import jax
import jax.numpy as jnp
from jax import lax
from jax.experimental import pallas as pl
from jax.experimental.pallas import tpu as pltpu
from jax.sharding import Mesh, PartitionSpec as P

HEAD = 128
WINDOW = 256
SHORT = 8

epsilon = 1e-06
big_negative = -1e30

ALL = ("yh", "z", "x", "yl", "c")
SEQ = ("yh", "z")
TP = ("x", "yl", "c")
f32 = jnp.float32
bf16 = jnp.bfloat16


def from_behind(array, axis, by):
    size = lax.axis_size(axis)
    pairs = [(i, i + by) for i in range(size) if 0 <= i + by < size]
    return lax.ppermute(array, axis, pairs)


def rotated(array, axis, by):
    size = lax.axis_size(axis)
    return lax.ppermute(array, axis, [(i, (i + by) % size) for i in range(size)])


def gathered(array, axes):
    copies = jnp.broadcast_to(array, (lax.axis_size(axes), *array.shape))
    return lax.all_to_all(copies, axes, split_axis=0, concat_axis=0, tiled=True)


def exchanged(pieces, axes):
    return lax.all_to_all(pieces, axes, split_axis=0, concat_axis=0, tiled=True)


def normalize(values, scale_gain):
    mean_square = jnp.mean(values * values, axis=-1, keepdims=True)
    return values * lax.rsqrt(mean_square + epsilon) * scale_gain


def dot(a, b):
    return jnp.dot(a, b, preferred_element_type=f32)


def fine_layer(tokens, fine_gain, fine_query, fine_keyval, fine_out):
    tok_rows, width = tokens.shape
    fine_heads = width // HEAD
    scale = 1.0 / math.sqrt(HEAD)
    start_row = lax.axis_index(ALL) * tok_rows
    inputs = tokens.astype(f32)
    normed = normalize(inputs, fine_gain).astype(bf16)
    queries = dot(normed, fine_query).astype(bf16)
    keyvals = dot(normed, fine_keyval).astype(bf16)
    earlier_rows = from_behind(normed, ALL, 1)
    earlier = dot(earlier_rows, fine_keyval).astype(bf16)
    key_rows = jnp.concatenate([earlier, keyvals], 0)
    span = key_rows.shape[0]
    key_heads = key_rows[:, :width].reshape(span, fine_heads, HEAD)
    value_heads = key_rows[:, width:].reshape(span, fine_heads, HEAD)
    query_heads = queries.reshape(tok_rows, fine_heads, HEAD)
    scores = jnp.einsum("qhd,khd->hqk", query_heads, key_heads, preferred_element_type=f32) * scale
    row_index = jnp.arange(tok_rows, dtype=jnp.int32)[:, None]
    col_index = jnp.arange(span, dtype=jnp.int32)[None, :]
    offset = row_index + WINDOW - col_index
    allowed = (offset >= 0) & (offset < WINDOW) & (start_row - WINDOW + col_index >= 0)
    scores = jnp.where(allowed[None], scores, big_negative)
    peak = jnp.max(scores, axis=-1, keepdims=True)
    terms = jnp.where(allowed[None], jnp.exp(scores - peak), 0.0)
    denom = jnp.sum(terms, axis=-1)
    mixed = jnp.einsum("hqk,khd->qhd", terms.astype(bf16), value_heads, preferred_element_type=f32)
    local = (mixed / jnp.transpose(denom)[..., None]).reshape(tok_rows, width).astype(bf16)
    return (inputs + dot(local, fine_out)).astype(bf16)


def attention_kernel(place_ref, q_ref, *refs):
    chunks, out_ref = refs[:-1], refs[-1]
    tile = q_ref.shape[0]
    step = pl.program_id(0)
    q = q_ref[...]
    row = step * tile + lax.broadcasted_iota(jnp.int32, (tile, tile), 0)
    col = step * tile + lax.broadcasted_iota(jnp.int32, (tile, tile), 1)

    def position(index):
        return (index >> 6) * 512 + ((index >> 5) & 1) * 64 + (index & 31)

    ahead = position(row) - position(col)

    def update(state, kt, masked):
        peak, total, acc = state
        rows = pl.ds(pl.multiple_of(kt * tile, tile), tile)
        scores = []
        for j, chunk in enumerate(chunks):
            s = lax.dot_general(
                q, chunk[rows, :HEAD], (((1,), (1,)), ((), ())), preferred_element_type=f32
            )
            if masked:
                s = jnp.where(ahead >= place_ref[j], s, big_negative)
            scores.append(s)
        top = functools.reduce(jnp.maximum, scores)
        new_peak = jnp.maximum(peak, jnp.max(top, axis=-1, keepdims=True))
        fade = jnp.exp2(peak - new_peak)
        acc = acc * fade
        sums = None
        for j, chunk in enumerate(chunks):
            p = jnp.exp2(scores[j] - new_peak)
            if masked:
                p = jnp.where(ahead >= place_ref[j], p, 0.0)
            sums = p if sums is None else sums + p
            acc = acc + dot(p.astype(bf16), chunk[rows, HEAD:])
        total = total * fade + jnp.sum(sums, axis=-1, keepdims=True)
        return new_peak, total, acc

    state = (
        jnp.full((tile, 1), big_negative, f32),
        jnp.zeros((tile, 1), f32),
        jnp.zeros((tile, HEAD), f32),
    )
    state = lax.fori_loop(0, step, lambda kt, st: update(st, kt, False), state)
    _, total, acc = update(state, step, True)
    out_ref[...] = (acc / total).astype(bf16)


def coarse_attention(q, chunks, places, tile=256):
    rows = q.shape[0]
    whole = pl.BlockSpec(chunks[0].shape, lambda i, place: (0, 0))
    return pl.pallas_call(
        attention_kernel,
        out_shape=jax.ShapeDtypeStruct((rows, HEAD), bf16),
        grid_spec=pltpu.PrefetchScalarGridSpec(
            num_scalar_prefetch=1,
            grid=(rows // tile,),
            in_specs=[pl.BlockSpec((tile, HEAD), lambda i, place: (i, 0))] + [whole] * len(chunks),
            out_specs=pl.BlockSpec((tile, HEAD), lambda i, place: (i, 0)),
        ),
        compiler_params=pltpu.CompilerParams(vmem_limit_bytes=48 << 20),
    )(places, q, *chunks)


def gate(array, earlier):
    return lax.optimization_barrier((array, earlier))[0]


def summed_piece(left, right, pieces):
    core = lax.axis_index("c")
    half = left.shape[0] // 2
    mine = lax.dynamic_slice(left, (core * half, 0), (half, left.shape[1]))
    other = lax.dynamic_slice(left, ((1 - core) * half, 0), (half, left.shape[1]))
    got = rotated(dot(other, right).astype(bf16), "c", 1)
    both = (dot(mine, right) + got.astype(f32)).astype(bf16)
    return jnp.sum(exchanged(pieces(both), ("x", "yl")).astype(f32), axis=0).astype(bf16)


def body(
    tokens,
    fine_gain,
    fine_query,
    fine_keyval,
    fine_out,
    down_weight,
    coarse_gain,
    coarse_query,
    coarse_keyval,
    coarse_out,
    up_weight,
):
    width = tokens.shape[1]
    wide = coarse_gain.shape[0]
    cols = coarse_query.shape[1]
    yh, z, x, yl, c = (lax.axis_index(a) for a in ALL)
    y = yh * 2 + yl
    s, t = lax.axis_index(SEQ), lax.axis_index(TP)
    n_seq, n_tp = lax.axis_size(SEQ), lax.axis_size(TP)
    swap = [(b * n_tp + a, a * n_tp + b) for a in range(n_seq) for b in range(n_tp)]

    with jax.named_scope("weights"):
        three = (coarse_query, coarse_keyval[:, 0], coarse_keyval[:, 1])
        sent = [w[:, k * HEAD : (k + 1) * HEAD] for k in range(2) for w in three]
        rows_here = lax.ppermute(jnp.concatenate(sent, 1), ALL, swap)

    fine_state = fine_layer(tokens, fine_gain, fine_query, fine_keyval, fine_out)
    run_count = tokens.shape[0] // SHORT
    pooled = jnp.mean(fine_state.astype(f32).reshape(run_count, SHORT, width), axis=1).astype(bf16)

    with jax.named_scope("gather_rows"):
        z_rows = gathered(pooled, ("z",)).reshape(-1, width)
        z_count = z_rows.shape[0]
        y_rows = [z_rows] + [rotated(z_rows, ("yh", "yl"), by) for by in (3, 2, 1)]
        all_rows = jnp.concatenate(y_rows, 0)
        n = all_rows.shape[0]

    with jax.named_scope("weights"):
        rows_here = gate(rows_here, pooled)
        gain = lax.dynamic_slice(coarse_gain, (t * cols,), (cols,))
        scaled = (rows_here.astype(f32) * gain[:, None]).astype(bf16)
        gram_rows = jnp.transpose(lax.dynamic_slice(down_weight, (128 * z, 0), (128, cols)))
        half = 3 * HEAD
        right = jnp.concatenate([scaled[:, :half], gram_rows, scaled[:, half:], gram_rows], 1)
        first = summed_piece(
            down_weight,
            right,
            lambda v: jnp.swapaxes(v.reshape(4, 128, 2, 512), 1, 2).reshape(8, 128, 512),
        )
        proj = gathered(first, ("c", "x")).reshape(width, 512)

        out_sent = lax.dynamic_slice(gate(coarse_out, pooled), (0, s * cols), (cols, cols))
        out_here = lax.ppermute(out_sent, ALL, swap)
        slot_rows = lax.dynamic_slice(down_weight, (128 * z + 64 * yh, 0), (64, cols))
        left = jnp.concatenate([out_here[:HEAD], slot_rows[:32], out_here[HEAD:], slot_rows[32:]], 0)
        left = gate(left, first)
        flipped = jnp.transpose(up_weight)
        second = summed_piece(
            flipped,
            jnp.transpose(left),
            lambda v: jnp.swapaxes(v.reshape(4, 128, 2, 160), 1, 2).reshape(8, 128, 160),
        )
        second = gathered(second, ("c", "x")).reshape(width, 160)
        second = lax.all_gather(jnp.transpose(second), ("yh", "yl"), axis=0)

    with jax.named_scope("project"):
        qkv = dot(all_rows, proj)
        slot = lax.dynamic_slice(all_rows, (0, 128 * z), (n, 128))
        squares = jnp.sum(qkv[:, half:] * slot.astype(f32), axis=-1)
        squares = jnp.sum(gathered(squares[None], ("z",)), axis=(0, 1))
        inverse = lax.rsqrt(jnp.maximum(squares, 0.0) / wide + epsilon)

        def by_row(values):
            parts = values.reshape(4, 8, run_count, -1)
            twice = jnp.concatenate([parts, parts[:3]], 0)
            parts = lax.dynamic_slice_in_dim(twice, (4 - y) % 4, 4, 0)
            return jnp.swapaxes(parts.reshape(2, 2, 8, run_count, -1), 1, 2).reshape(n, -1)

        kv = by_row(qkv[:, HEAD:half].astype(bf16))
        inverse = by_row(inverse)
        factor = math.log2(math.e) / math.sqrt(HEAD)
        q = (by_row(qkv[:, :HEAD]) * (inverse * factor)).astype(bf16)
        every_inverse = gathered(inverse.reshape(1, n), ("x", "c")).reshape(4, 2, n, 1)

    with jax.named_scope("attention"):
        chunks, places = [], []
        for by in (0, 1, 3, 2):
            mine = kv if by == 0 else rotated(kv, "x", by)
            other = rotated(mine, "c", 1)
            source = (x + 4 - by) % 4
            shift = 128 * (source - x)
            for chunk, core, place in ((mine, c, shift), (other, 1 - c, shift + 32 * (1 - 2 * c))):
                scale = lax.dynamic_slice(every_inverse, (source, core, 0, 0), (1, 1, n, 1))
                chunks.append((chunk.astype(f32) * scale.reshape(n, 1)).astype(bf16))
                places.append(place)
        heads = coarse_attention(q, chunks, jnp.stack(places).astype(jnp.int32))

    with jax.named_scope("lift"):
        heads = jnp.swapaxes(heads.reshape(2, 8, 2, run_count, HEAD), 1, 2)
        heads = heads.reshape(4, z_count, HEAD)
        total = None
        for by in range(4):
            part = lax.dynamic_index_in_dim(heads, (y + by) % 4, 0, keepdims=False)
            if by:
                part = rotated(part, ("yh", "yl"), by)
            matrix = lax.dynamic_index_in_dim(second, (y + 4 - by) % 4, 0, keepdims=False)
            product = dot(part, matrix[:HEAD])
            total = product if total is None else total + product
        slot = lax.dynamic_slice(z_rows, (0, 128 * z), (z_count, 128))
        total = total + dot(slot, second[:, HEAD:].reshape(128, width))
        lifted = exchanged(total.astype(bf16).reshape(8, run_count, width), ("z",))
        lifted = jnp.sum(lifted.astype(f32), axis=0)
        before = from_behind(lifted[run_count - 1 :], ALL, 1)
        lifted = jnp.concatenate([before, lifted[: run_count - 1]], 0)
        result = fine_state.astype(f32) + jnp.repeat(lifted, SHORT, axis=0)
    return result.astype(bf16)


def solution(mesh):
    fine = Mesh(mesh.devices.reshape(2, 8, 4, 2, 2), ALL)
    return jax.shard_map(
        body,
        mesh=fine,
        in_specs=(
            P(ALL, None),
            P(),
            P(),
            P(),
            P(),
            P(None, TP),
            P(),
            P(SEQ, TP),
            P(SEQ, None, TP),
            P(TP, None),
            P(TP, None),
        ),
        out_specs=P(ALL, None),
        check_vma=False,
    )
```

time: 321 us -> 260 us (0.81)
  waiting for transfers between devices: 97.4 us -> 75.7 us
  starting transfers between devices: 83.8 us -> 65 us
  blocking collectives: 48.8 us -> 31 us
  between operations: 0.7 us -> 14.3 us
  other arithmetic: 26.3 us -> 16.5 us
  local copies, waits for them, and re-layouts: 24.2 us -> 18.7 us
    all_to_all x6 -> x5, starting transfers between devices: 51 us -> 20.9 us  [gathered(): return lax.all_to_all(copies, axes, split_axis=0, concat_axis=0, tiled=True)]
    all_to_all x6 -> x5, waiting for transfers between devices: 50.1 us -> 32.4 us  [gathered(): return lax.all_to_all(copies, axes, split_axis=0, concat_axis=0, tiled=True)]
    all_to_all x1 -> x0, blocking collectives: 16.4 us -> none  [gathered(): return lax.all_to_all(copies, axes, split_axis=0, concat_axis=0, tiled=True)]
    ppermute x1, waiting for transfers between devices: 0.11 us -> 16.3 us  [body(): out_here = lax.ppermute(out_sent, ALL, swap)]
    ppermute x9 -> x15, waiting for transfers between devices: 30.6 us -> 19.8 us  [rotated(): lax.ppermute(array, axis, [(i, (i + by) % size) for i in range(size)])]
    ppermute x9 -> x15, starting transfers between devices: 9.14 us -> 17.7 us  [rotated(): lax.ppermute(array, axis, [(i, (i + by) % size) for i in range(size)])]
    all_to_all x2 -> x1, waiting for transfers between devices: 6.5 us -> 0.01 us  [exchanged(): return lax.all_to_all(pieces, axes, split_axis=0, concat_axis=0, tiled=True)]
    concatenate x7 -> x6, other arithmetic: 7.78 us -> 2.92 us  [the longest x1 2.56 us: body(): all_rows = jnp.concatenate(y_rows, 0)]
  transfers between devices with their start and end apart: 21 -> 26, of which waited for: 13 -> 11; matrix products, arithmetic and copies ran while one was open for 19% -> 18% of each run, Pallas kernels for 4% -> 5%
where the time goes in v2:
time: 260 us; the launch traced here: 259 us
  waiting for transfers between devices  75.7 us (29%)
  starting transfers between devices  65 us (25%)
  blocking collectives  31 us (12%)
  matrix products  24.5 us (9%)
  local copies, waits for them, and re-layouts  18.7 us (7%)
  other arithmetic  16.5 us (6%)
  between operations  14.3 us (6%)
  Pallas kernels  12.9 us (5%)
    all_to_all x5, waiting for transfers between devices, gathered(): return lax.all_to_all(copies, axes, split_axis=0, concat_axis=0, tiled=True)  32.4 us
    all_to_all x2, blocking collectives, exchanged(): return lax.all_to_all(pieces, axes, split_axis=0, concat_axis=0, tiled=True)  31 us
    dot_general x14, matrix products, dot(): return jnp.dot(a, b, preferred_element_type=f32)  21.6 us
    all_to_all x5, starting transfers between devices, gathered(): return lax.all_to_all(copies, axes, split_axis=0, concat_axis=0, tiled=True)  20.9 us
    ppermute x15, waiting for transfers between devices, rotated(): lax.ppermute(array, axis, [(i, (i + by) % size) for i in range(size)])  19.8 us
    ppermute x15, starting transfers between devices, rotated(): lax.ppermute(array, axis, [(i, (i + by) % size) for i in range(size)])  17.7 us
    ppermute x1, waiting for transfers between devices, body(): out_here = lax.ppermute(out_sent, ALL, swap)  16.3 us
    pallas_call x1, Pallas kernels, coarse_attention(): pl.pallas_call(attention_kernel, out_shape=jax.ShapeDtypeStruct((rows, HE...  12.9 us
  transfers between devices with their start and end apart: 26, of which 11 were waited for; matrix products, arithmetic and copies ran while one was open for 18% of the time, Pallas kernels for 5%

profile of v2, /device:TPU:16, one launch (start us, length us, event | category | flops | bytes accessed | tf_op | source)
XLA Modules:
  0.0 258.5 jit_solution(10205454108174579979)
XLA Ops:
  6.5 1.4 fusion.23
  7.9 1.2 fusion.25
  9.2 1.9 collective-permute-start
  11.1 1.5 fusion.72
  16.5 4.7 %collective-permute-start.4 = (bf16[256,768]{1,0:T(8,128)(2,1)}, bf16[256,768]{1,0:T(8,128)(2,1)S(1)}, u32[]{:S(2)}, u32[]{:S(2)}) collective-permute-start(bf16[256,768]{1,0:T(8,128)(2,1)} %slice_dynamic-update-slice_fusion), channel_id=1, source_target_pairs={{0,0},{16,1},{32,2},{48,3},{64,4},{80,5},{96,6},{112,7},{128,8},{1... | collective-permute-start | bytes 1179656 | tf_op jit(solution)/shard_map/weights/ppermute | solution.py:187
  21.3 3.1 %fusion.20 = bf16[32,8,8,128]{3,2,1,0:T(8,128)(2,1)} fusion(bf16[256,1024]{1,0:T(8,128)(2,1)S(1)} %fusion.25, bf16[1024,1024]{1,0:T(8,128)(2,1)} %param.13), kind=kOutput, calls=%fused_computation.31 | convolution fusion | flops 537133056 | bytes 3145728 | tf_op jit(solution)/shard_map/dot_general | solution.py:51
  24.4 0.8 constant_dynamic-slice_fusion.11
  26.7 0.9 fusion.40
  27.6 3.6 %convolution_convert_fusion = bf16[256,2048]{1,0:T(8,128)(2,1)S(1)} fusion(bf16[256,1024]{1,0:T(8,128)(2,1)S(1)} %fusion.25, bf16[1024,2048]{1,0:T(8,128)(2,1)} %param.14), kind=kOutput, calls=%fused_computation.4 | convolution fusion | flops 1074266112 | bytes 5767168 | tf_op jit(solution)/shard_map/dot_general | solution.py:51
  31.2 2.3 convolution_convert_fusion.1
  33.5 1.2 fusion.30
  34.7 1.3 copy.69
  36.0 2.1 fusion.27
  38.2 2.5 fusion.74
  40.7 0.8 fusion.17
  41.7 1.7 fusion.21
  44.1 1.6 collective-permute-start.5
  45.7 2.4 collective-permute-done.5
  48.1 1.7 add_convert_fusion
  49.8 0.8 reshape.206
  50.6 1.2 copy.61
  51.8 11.9 %all-to-all-start.1 = ((bf16[8,128,512]{2,1,0:T(8,128)(2,1)}), bf16[8,128,512]{2,1,0:T(8,128)(2,1)S(1)}, u32[]{:S(2)}, u32[]{:S(2)}) async-start(bf16[8,128,512]{2,1,0:T(8,128)(2,1)} %bitcast.18), calls=%async_computation.1 | async-start | bytes 2097152 | tf_op jit(solution)/shard_map/weights/all_to_all | solution.py:42
  63.6 0.9 constant_dynamic-slice_fusion.1
  64.5 6.0 %collective-permute-start.13 = (bf16[256,256]{1,0:T(8,128)(2,1)S(1)}, bf16[256,256]{1,0:T(8,128)(2,1)S(1)}, u32[]{:S(2)}, u32[]{:S(2)}) collective-permute-start(bf16[256,256]{1,0:T(8,128)(2,1)S(1)} %constant_dynamic-slice_fusion.1), channel_id=1, source_target_pairs={{0,0},{16,1},{32,2},{48,3},{64,4},{80,5},{96,6},{112,7},{128,8},{1... | collective-permute-start | bytes 393224 | tf_op jit(solution)/shard_map/weights/ppermute | solution.py:215
  70.6 16.3 %collective-permute-done.13 = bf16[256,256]{1,0:T(8,128)(2,1)S(1)} collective-permute-done((bf16[256,256]{1,0:T(8,128)(2,1)S(1)}, bf16[256,256]{1,0:T(8,128)(2,1)S(1)}, u32[]{:S(2)}, u32[]{:S(2)}) %collective-permute-start.13) | collective-permute-done | bytes 131104 | tf_op jit(solution)/shard_map/weights/ppermute | solution.py:215
  87.6 1.6 collective-permute-done.14
  89.6 11.0 %all_to_all.40 = bf16[8,128,160]{1,2,0:T(8,128)(2,1)S(1)} all-to-all(bf16[8,128,160]{1,2,0:T(8,128)(2,1)S(1)} %bitcast.150), channel_id=1, replica_groups=mesh['yh'=2,'z'=8,'x'=4,'yl'=2,'c'=2] {'x','yl'}, dimensions={0} | all-to-all | bytes 655360 | tf_op jit(solution)/shard_map/weights/all_to_all | solution.py:42
  100.6 0.9 broadcast_in_dim.49
  101.5 6.9 %all-to-all-start = ((bf16[8,32,1024]{2,1,0:T(8,128)(2,1)}), bf16[8,32,1024]{2,1,0:T(8,128)(2,1)S(1)}, u32[]{:S(2)}, u32[]{:S(2)}) async-start(bf16[8,32,1024]{2,1,0:T(8,128)(2,1)} %broadcast_in_dim.49), calls=%async_computation | async-start | bytes 1048576 | tf_op jit(solution)/shard_map/gather_rows/all_to_all | solution.py:38
  108.4 16.3 %all-to-all-done = bf16[8,32,1024]{2,1,0:T(8,128)(2,1)S(1)} async-done(((bf16[8,32,1024]{2,1,0:T(8,128)(2,1)}), bf16[8,32,1024]{2,1,0:T(8,128)(2,1)S(1)}, u32[]{:S(2)}, u32[]{:S(2)}) %all-to-all-start) | async-done | bytes 524320 | tf_op jit(solution)/shard_map/gather_rows/all_to_all | solution.py:38
  125.5 3.4 %all-to-all-start.6 = ((bf16[8,128,160]{1,2,0:T(8,128)(2,1)}), bf16[8,128,160]{1,2,0:T(8,128)(2,1)S(1)}, u32[]{:S(2)}, u32[]{:S(2)}) async-start(bf16[8,128,160]{1,2,0:T(8,128)(2,1)} %broadcast_in_dim.53), calls=%async_computation.6 | async-start | bytes 655360 | tf_op jit(solution)/shard_map/weights/all_to_all | solution.py:38
  128.9 1.5 collective-permute-start.1
  130.4 1.8 collective-permute-start.2
  132.2 1.2 collective-permute-start.3
  133.4 3.1 %all-to-all-done.6 = bf16[8,128,160]{1,2,0:T(8,128)(2,1)S(1)} async-done(((bf16[8,128,160]{1,2,0:T(8,128)(2,1)}), bf16[8,128,160]{1,2,0:T(8,128)(2,1)S(1)}, u32[]{:S(2)}, u32[]{:S(2)}) %all-to-all-start.6) | async-done | bytes 327712 | tf_op jit(solution)/shard_map/weights/all_to_all | solution.py:38
  136.5 1.1 broadcast_in_dim.50
  137.5 3.6 %all-to-all-start.2 = ((bf16[8,128,512]{2,1,0:T(8,128)(2,1)}), bf16[8,128,512]{2,1,0:T(8,128)(2,1)S(1)}, u32[]{:S(2)}, u32[]{:S(2)}) async-start(bf16[8,128,512]{2,1,0:T(8,128)(2,1)} %broadcast_in_dim.50), calls=%async_computation.2 | async-start | bytes 2097152 | tf_op jit(solution)/shard_map/weights/all_to_all | solution.py:38
  141.4 2.4 collective-permute-done.1
  143.7 3.0 %collective-permute-done.2 = bf16[256,1024]{1,0:T(8,128)(2,1)S(1)} collective-permute-done((bf16[256,1024]{1,0:T(8,128)(2,1)S(1)}, bf16[256,1024]{1,0:T(8,128)(2,1)S(1)}, u32[]{:S(2)}, u32[]{:S(2)}) %collective-permute-start.2) | collective-permute-done | bytes 524320 | tf_op jit(solution)/shard_map/gather_rows/ppermute | solution.py:33
  146.7 10.4 %collective-permute-done.3 = bf16[256,1024]{1,0:T(8,128)(2,1)} collective-permute-done((bf16[256,1024]{1,0:T(8,128)(2,1)S(1)}, bf16[256,1024]{1,0:T(8,128)(2,1)}, u32[]{:S(2)}, u32[]{:S(2)}) %collective-permute-start.3) | collective-permute-done | bytes 524320 | tf_op jit(solution)/shard_map/gather_rows/ppermute | solution.py:33
  157.1 2.6 pad_maximum_fusion
  160.5 2.8 %fusion.75 = (bf16[1024,512]{1,0:T(8,128)(2,1)S(1)}, f32[1024,512]{1,0:T(8,128)S(1)}) fusion(bf16[1024,1024]{1,0:T(8,128)(2,1)} %pad_maximum_fusion, bf16[1024,512]{1,0:T(8,128)(2,1)S(1)} %bitcast.159), kind=kOutput, calls=%fused_computation.141 | convolution fusion | flops 1074266112 | bytes 6291456 | tf_op jit(solution)/shard_map/project/dot_general | solution.py:51
  163.7 3.3 %collective-permute-start.11 = (bf16[1024,256]{1,0:T(8,128)(2,1)S(1)}, bf16[1024,256]{1,0:T(8,128)(2,1)}, u32[]{:S(2)}, u32[]{:S(2)}) collective-permute-start(bf16[1024,256]{1,0:T(8,128)(2,1)S(1)} %bitcast.140), channel_id=1, source_target_pairs={{0,8},{4,12},{8,0},{12,4},{1,9},{5,13},{9,1},{13,5},{2,10},{6,14},... | collective-permute-start | bytes 1572872 | tf_op jit(solution)/shard_map/attention/ppermute | solution.py:33
  166.9 1.2 collective-permute-start.9
  168.1 0.9 collective-permute-start.7
  169.0 1.2 fusion.35
  170.8 3.3 %all-to-all-start.3 = ((f32[8,1,1024]{2,1,0:T(1,128)}), f32[8,1,1024]{2,1,0:T(1,128)S(1)}, u32[]{:S(2)}, u32[]{:S(2)}) async-start(f32[8,1,1024]{2,1,0:T(1,128)} %broadcast_in_dim.51), calls=%async_computation.3 | async-start | bytes 65536 | tf_op jit(solution)/shard_map/project/all_to_all | solution.py:38
  174.3 7.8 %all-to-all-done.3 = f32[8,1,1024]{2,1,0:T(1,128)S(1)} async-done(((f32[8,1,1024]{2,1,0:T(1,128)}), f32[8,1,1024]{2,1,0:T(1,128)S(1)}, u32[]{:S(2)}, u32[]{:S(2)}) %all-to-all-start.3) | async-done | bytes 32800 | tf_op jit(solution)/shard_map/project/all_to_all | solution.py:38
  183.0 3.6 %all-to-all-start.4 = ((f32[8,1,1024]{2,1,0:T(1,128)}), f32[8,1,1024]{2,1,0:T(1,128)S(1)}, u32[]{:S(2)}, u32[]{:S(2)}) async-start(f32[8,1,1024]{2,1,0:T(1,128)} %broadcast_in_dim.52), calls=%async_computation.4 | async-start | bytes 65536 | tf_op jit(solution)/shard_map/project/all_to_all | solution.py:38
  186.9 5.2 %all-to-all-done.4 = f32[8,1,1024]{2,1,0:T(1,128)S(1)} async-done(((f32[8,1,1024]{2,1,0:T(1,128)}), f32[8,1,1024]{2,1,0:T(1,128)S(1)}, u32[]{:S(2)}, u32[]{:S(2)}) %all-to-all-start.4) | async-done | bytes 32800 | tf_op jit(solution)/shard_map/project/all_to_all | solution.py:38
  192.5 1.2 multiply_convert_fusion.1.refs_6_
  195.1 1.2 multiply_convert_fusion.6.refs_1_
  197.0 12.9 %attention.1 = bf16[1024,128]{1,0:T(8,128)(2,1)S(1)} custom-call(s32[8]{0:T(128)S(1)} %stack.35.place_ref, bf16[1024,128]{1,0:T(8,128)(2,1)S(1)} %fusion.36.q_ref, bf16[1024,256]{1,0:T(8,128)(2,1)S(1)} %multiply_convert_fusion.7.refs_0_, bf16[1024,256]{1,0:T(8,128)(2,1)S(1)} %multiply_convert_fusion.6.refs_1_, ...), custom_call_target="tpu_custom_call" | custom-call | tf_op jit(solution)/shard_map/attention/pallas_call | solution.py:135
  210.3 1.7 collective-permute-start.17
  212.0 3.0 %collective-permute-start.16 = (bf16[256,128]{1,0:T(8,128)(2,1)S(1)}, bf16[256,128]{1,0:T(8,128)(2,1)S(1)}, u32[]{:S(2)}, u32[]{:S(2)}) collective-permute-start(bf16[256,128]{1,0:T(8,128)(2,1)S(1)} %get-tuple-element.19), channel_id=1, source_target_pairs={{0,128},{2,130},{128,0},{130,2},{1,129},{3,131},{129,1},{131,3},{4... | collective-permute-start | bytes 196616 | tf_op jit(solution)/shard_map/lift/ppermute | solution.py:33
  215.0 1.2 fusion.42
  216.3 1.0 slice.164
  217.2 1.2 convolution_add_fusion.1
  218.8 1.2 fusion.41
  220.1 1.4 fusion.16
  221.5 20.0 %all_to_all.41 = bf16[8,32,1024]{2,1,0:T(8,128)(2,1)S(1)} all-to-all(bf16[8,32,1024]{2,1,0:T(8,128)(2,1)S(1)} %bitcast.139), channel_id=1, replica_groups=mesh['yh'=2,'z'=8,'x'=4,'yl'=2,'c'=2] {'z'}, dimensions={0} | all-to-all | bytes 1048576 | tf_op jit(solution)/shard_map/lift/all_to_all | solution.py:42
  241.6 1.9 collective-permute-start.18
  243.5 7.2 %collective-permute-done.18 = f32[1,1024]{1,0:T(1,128)S(1)} collective-permute-done((f32[1,1024]{1,0:T(1,128)S(1)}, f32[1,1024]{1,0:T(1,128)S(1)}, u32[]{:S(2)}, u32[]{:S(2)}) %collective-permute-start.18) | collective-permute-done | bytes 4128 | tf_op jit(solution)/shard_map/lift/ppermute | solution.py:28
  250.7 0.9 fusion.22
  (104 shorter events, 14.4 us)
Async XLA Ops:
  6.5 35.0 %copy-start = (bf16[1024,1024]{1,0:T(8,128)(2,1)S(1)}, bf16[1024,1024]{1,0:T(8,128)(2,1)}, u32[]{:S(2)}) copy-start(bf16[1024,1024]{1,0:T(8,128)(2,1)} %param.15) | copy-start | bytes 6291460
  6.5 6.1 %copy-start.6 = (bf16[256,256]{1,0:T(8,128)(2,1)S(1)}, bf16[256,256]{1,0:T(8,128)(2,1)}, u32[]{:S(2)}) copy-start(bf16[256,256]{1,0:T(8,128)(2,1)} %param.18) | copy-start | bytes 393220
  9.2 22.0 %collective-permute-start = (bf16[256,1024]{1,0:T(8,128)(2,1)S(1)}, bf16[256,1024]{1,0:T(8,128)(2,1)}, u32[]{:S(2)}, u32[]{:S(2)}) collective-permute-start(bf16[256,1024]{1,0:T(8,128)(2,1)S(1)} %fusion.25), channel_id=1, source_target_pairs={{0,1},{1,2},{2,3},{3,4},{4,5},{5,6},{6,7},{7,8},{8,9},{9,10},{10,1... | collective-permute-start | bytes 1572872 | tf_op jit(solution)/shard_map/ppermute | solution.py:28
  16.5 26.9 %collective-permute-start.4 = (bf16[256,768]{1,0:T(8,128)(2,1)}, bf16[256,768]{1,0:T(8,128)(2,1)S(1)}, u32[]{:S(2)}, u32[]{:S(2)}) collective-permute-start(bf16[256,768]{1,0:T(8,128)(2,1)} %slice_dynamic-update-slice_fusion), channel_id=1, source_target_pairs={{0,0},{16,1},{32,2},{48,3},{64,4},{80,5},{96,6},{112,7},{128,8},{1... | collective-permute-start | bytes 1179656 | tf_op jit(solution)/shard_map/weights/ppermute | solution.py:187
  27.6 3.6 %copy-start.10 = (bf16[1024,2048]{1,0:T(8,128)(2,1)S(1)}, bf16[1024,2048]{1,0:T(8,128)(2,1)}, u32[]{:S(2)}) copy-start(bf16[1024,2048]{1,0:T(8,128)(2,1)} %param.14) | copy-start | bytes 12582916
  36.0 2.1 copy-start.7
  38.2 2.5 copy-start.4
  40.7 1.0 copy-start.2
  41.7 1.9 copy-start.8
  41.7 2.0 copy-start.9
  44.1 4.0 %collective-permute-start.5 = (bf16[512,1024]{1,0:T(8,128)(2,1)S(1)}, bf16[512,1024]{1,0:T(8,128)(2,1)}, u32[]{:S(2)}, u32[]{:S(2)}) collective-permute-start(bf16[512,1024]{1,0:T(8,128)(2,1)S(1)} %convolution_convert_fusion.2), channel_id=1, source_target_pairs={{0,1},{1,0},{2,3},{3,2},{4,5},{5,4},{6,7},{7,6},{8,9},{9,8},{10,11... | collective-permute-start | bytes 3145736 | tf_op jit(solution)/shard_map/weights/ppermute | solution.py:33
  51.8 35.3 %copy-start.5 = (bf16[256,1024]{1,0:T(8,128)(2,1)S(1)}, bf16[256,1024]{1,0:T(8,128)(2,1)}, u32[]{:S(2)}) copy-start(bf16[256,1024]{1,0:T(8,128)(2,1)} %param.21) | copy-start | bytes 1572868
  51.8 35.1 %all-to-all-start.1 = ((bf16[8,128,512]{2,1,0:T(8,128)(2,1)}), bf16[8,128,512]{2,1,0:T(8,128)(2,1)S(1)}, u32[]{:S(2)}, u32[]{:S(2)}) async-start(bf16[8,128,512]{2,1,0:T(8,128)(2,1)} %bitcast.18), calls=%async_computation.1 | async-start | bytes 2097152 | tf_op jit(solution)/shard_map/weights/all_to_all | solution.py:42
  64.5 22.3 %collective-permute-start.13 = (bf16[256,256]{1,0:T(8,128)(2,1)S(1)}, bf16[256,256]{1,0:T(8,128)(2,1)S(1)}, u32[]{:S(2)}, u32[]{:S(2)}) collective-permute-start(bf16[256,256]{1,0:T(8,128)(2,1)S(1)} %constant_dynamic-slice_fusion.1), channel_id=1, source_target_pairs={{0,0},{16,1},{32,2},{48,3},{64,4},{80,5},{96,6},{112,7},{128,8},{1... | collective-permute-start | bytes 393224 | tf_op jit(solution)/shard_map/weights/ppermute | solution.py:215
  87.3 1.9 collective-permute-start.14
  101.5 23.2 %all-to-all-start = ((bf16[8,32,1024]{2,1,0:T(8,128)(2,1)}), bf16[8,32,1024]{2,1,0:T(8,128)(2,1)S(1)}, u32[]{:S(2)}, u32[]{:S(2)}) async-start(bf16[8,32,1024]{2,1,0:T(8,128)(2,1)} %broadcast_in_dim.49), calls=%async_computation | async-start | bytes 1048576 | tf_op jit(solution)/shard_map/gather_rows/all_to_all | solution.py:38
  125.5 11.0 %all-to-all-start.6 = ((bf16[8,128,160]{1,2,0:T(8,128)(2,1)}), bf16[8,128,160]{1,2,0:T(8,128)(2,1)S(1)}, u32[]{:S(2)}, u32[]{:S(2)}) async-start(bf16[8,128,160]{1,2,0:T(8,128)(2,1)} %broadcast_in_dim.53), calls=%async_computation.6 | async-start | bytes 655360 | tf_op jit(solution)/shard_map/weights/all_to_all | solution.py:38
  128.9 14.8 %collective-permute-start.1 = (bf16[256,1024]{1,0:T(8,128)(2,1)S(1)}, bf16[256,1024]{1,0:T(8,128)(2,1)S(1)}, u32[]{:S(2)}, u32[]{:S(2)}) collective-permute-start(bf16[256,1024]{1,0:T(8,128)(2,1)S(1)} %bitcast.134), channel_id=1, source_target_pairs={{0,130},{2,0},{128,2},{130,128},{1,131},{3,1},{129,3},{131,129},{4... | collective-permute-start | bytes 1572872 | tf_op jit(solution)/shard_map/gather_rows/ppermute | solution.py:33
  130.4 16.3 %collective-permute-start.2 = (bf16[256,1024]{1,0:T(8,128)(2,1)S(1)}, bf16[256,1024]{1,0:T(8,128)(2,1)S(1)}, u32[]{:S(2)}, u32[]{:S(2)}) collective-permute-start(bf16[256,1024]{1,0:T(8,128)(2,1)S(1)} %bitcast.135), channel_id=1, source_target_pairs={{0,128},{2,130},{128,0},{130,2},{1,129},{3,131},{129,1},{131,3},{4... | collective-permute-start | bytes 1572872 | tf_op jit(solution)/shard_map/gather_rows/ppermute | solution.py:33
  132.2 24.9 %collective-permute-start.3 = (bf16[256,1024]{1,0:T(8,128)(2,1)S(1)}, bf16[256,1024]{1,0:T(8,128)(2,1)}, u32[]{:S(2)}, u32[]{:S(2)}) collective-permute-start(bf16[256,1024]{1,0:T(8,128)(2,1)S(1)} %bitcast.136), channel_id=1, source_target_pairs={{0,2},{2,128},{128,130},{130,0},{1,3},{3,129},{129,131},{131,1},{4... | collective-permute-start | bytes 1572872 | tf_op jit(solution)/shard_map/gather_rows/ppermute | solution.py:33
  137.5 23.0 %all-to-all-start.2 = ((bf16[8,128,512]{2,1,0:T(8,128)(2,1)}), bf16[8,128,512]{2,1,0:T(8,128)(2,1)S(1)}, u32[]{:S(2)}, u32[]{:S(2)}) async-start(bf16[8,128,512]{2,1,0:T(8,128)(2,1)} %broadcast_in_dim.50), calls=%async_computation.2 | async-start | bytes 2097152 | tf_op jit(solution)/shard_map/weights/all_to_all | solution.py:38
  141.1 73.9 %all-gather.3.cloned.1.call-start = ((), (), s32[]{:S(2)}) async-start(), calls=%async_computation.8 | async-start | bytes 1638400 | tf_op jit(solution)/shard_map/weights/all_gather | solution.py:226
  163.7 28.7 %collective-permute-start.11 = (bf16[1024,256]{1,0:T(8,128)(2,1)S(1)}, bf16[1024,256]{1,0:T(8,128)(2,1)}, u32[]{:S(2)}, u32[]{:S(2)}) collective-permute-start(bf16[1024,256]{1,0:T(8,128)(2,1)S(1)} %bitcast.140), channel_id=1, source_target_pairs={{0,8},{4,12},{8,0},{12,4},{1,9},{5,13},{9,1},{13,5},{2,10},{6,14},... | collective-permute-start | bytes 1572872 | tf_op jit(solution)/shard_map/attention/ppermute | solution.py:33
  166.9 26.8 %collective-permute-start.9 = (bf16[1024,256]{1,0:T(8,128)(2,1)S(1)}, bf16[1024,256]{1,0:T(8,128)(2,1)S(1)}, u32[]{:S(2)}, u32[]{:S(2)}) collective-permute-start(bf16[1024,256]{1,0:T(8,128)(2,1)S(1)} %bitcast.141), channel_id=1, source_target_pairs={{0,12},{4,0},{8,4},{12,8},{1,13},{5,1},{9,5},{13,9},{2,14},{6,2},{... | collective-permute-start | bytes 1572872 | tf_op jit(solution)/shard_map/attention/ppermute | solution.py:33
  168.1 26.4 %collective-permute-start.7 = (bf16[1024,256]{1,0:T(8,128)(2,1)S(1)}, bf16[1024,256]{1,0:T(8,128)(2,1)S(1)}, u32[]{:S(2)}, u32[]{:S(2)}) collective-permute-start(bf16[1024,256]{1,0:T(8,128)(2,1)S(1)} %bitcast.142), channel_id=1, source_target_pairs={{0,4},{4,8},{8,12},{12,0},{1,5},{5,9},{9,13},{13,1},{2,6},{6,10},{... | collective-permute-start | bytes 1572872 | tf_op jit(solution)/shard_map/attention/ppermute | solution.py:33
  169.0 26.1 %collective-permute-start.6 = (bf16[1024,256]{1,0:T(8,128)(2,1)S(1)}, bf16[1024,256]{1,0:T(8,128)(2,1)}, u32[]{:S(2)}, u32[]{:S(2)}) collective-permute-start(bf16[1024,256]{1,0:T(8,128)(2,1)S(1)} %bitcast.143), channel_id=1, source_target_pairs={{0,1},{1,0},{2,3},{3,2},{4,5},{5,4},{6,7},{7,6},{8,9},{9,8},{10,11... | collective-permute-start | bytes 1572872 | tf_op jit(solution)/shard_map/attention/ppermute | solution.py:33
  170.8 11.3 %all-to-all-start.3 = ((f32[8,1,1024]{2,1,0:T(1,128)}), f32[8,1,1024]{2,1,0:T(1,128)S(1)}, u32[]{:S(2)}, u32[]{:S(2)}) async-start(f32[8,1,1024]{2,1,0:T(1,128)} %broadcast_in_dim.51), calls=%async_computation.3 | async-start | bytes 65536 | tf_op jit(solution)/shard_map/project/all_to_all | solution.py:38
  183.0 9.1 %all-to-all-start.4 = ((f32[8,1,1024]{2,1,0:T(1,128)}), f32[8,1,1024]{2,1,0:T(1,128)S(1)}, u32[]{:S(2)}, u32[]{:S(2)}) async-start(f32[8,1,1024]{2,1,0:T(1,128)} %broadcast_in_dim.52), calls=%async_computation.4 | async-start | bytes 65536 | tf_op jit(solution)/shard_map/project/all_to_all | solution.py:38
  192.4 4.0 %collective-permute-start.12 = (bf16[1024,256]{1,0:T(8,128)(2,1)}, bf16[1024,256]{1,0:T(8,128)(2,1)S(1)}, u32[]{:S(2)}, u32[]{:S(2)}) collective-permute-start(bf16[1024,256]{1,0:T(8,128)(2,1)} %collective-permute-done.11), channel_id=1, source_target_pairs={{0,1},{1,0},{2,3},{3,2},{4,5},{5,4},{6,7},{7,6},{8,9},{9,8},{10,11... | collective-permute-start | bytes 1572872 | tf_op jit(solution)/shard_map/attention/ppermute | solution.py:33
  193.7 2.8 %collective-permute-start.10 = (bf16[1024,256]{1,0:T(8,128)(2,1)S(1)}, bf16[1024,256]{1,0:T(8,128)(2,1)S(1)}, u32[]{:S(2)}, u32[]{:S(2)}) collective-permute-start(bf16[1024,256]{1,0:T(8,128)(2,1)S(1)} %collective-permute-done.9), channel_id=1, source_target_pairs={{0,1},{1,0},{2,3},{3,2},{4,5},{5,4},{6,7},{7,6},{8,9},{9,8},{10,11... | collective-permute-start | bytes 1572872 | tf_op jit(solution)/shard_map/attention/ppermute | solution.py:33
  194.5 2.2 collective-permute-start.8
  209.9 7.3 %collective-permute-start.15 = (bf16[256,128]{1,0:T(8,128)(2,1)S(1)}, bf16[256,128]{1,0:T(8,128)(2,1)S(1)}, u32[]{:S(2)}, u32[]{:S(2)}) collective-permute-start(bf16[256,128]{1,0:T(8,128)(2,1)S(1)} %get-tuple-element.21), channel_id=1, source_target_pairs={{0,2},{2,128},{128,130},{130,0},{1,3},{3,129},{129,131},{131,1},{4... | collective-permute-start | bytes 196616 | tf_op jit(solution)/shard_map/lift/ppermute | solution.py:33
  210.3 8.4 %collective-permute-start.17 = (bf16[256,128]{1,0:T(8,128)(2,1)S(1)}, bf16[256,128]{1,0:T(8,128)(2,1)S(1)}, u32[]{:S(2)}, u32[]{:S(2)}) collective-permute-start(bf16[256,128]{1,0:T(8,128)(2,1)S(1)} %get-tuple-element.20), channel_id=1, source_target_pairs={{0,130},{2,0},{128,2},{130,128},{1,131},{3,1},{129,3},{131,129},{4... | collective-permute-start | bytes 196616 | tf_op jit(solution)/shard_map/lift/ppermute | solution.py:33
  212.0 8.0 %collective-permute-start.16 = (bf16[256,128]{1,0:T(8,128)(2,1)S(1)}, bf16[256,128]{1,0:T(8,128)(2,1)S(1)}, u32[]{:S(2)}, u32[]{:S(2)}) collective-permute-start(bf16[256,128]{1,0:T(8,128)(2,1)S(1)} %get-tuple-element.19), channel_id=1, source_target_pairs={{0,128},{2,130},{128,0},{130,2},{1,129},{3,131},{129,1},{131,3},{4... | collective-permute-start | bytes 196616 | tf_op jit(solution)/shard_map/lift/ppermute | solution.py:33
  220.0 30.7 %copy-start.3 = (bf16[256,1024]{1,0:T(8,128)(2,1)S(1)}, bf16[256,1024]{1,0:T(8,128)(2,1)}, u32[]{:S(2)}) copy-start(bf16[256,1024]{1,0:T(8,128)(2,1)} %get-tuple-element.37) | copy-start | bytes 1572868
  220.0 31.6 %copy-start.1 = (bf16[1024,1024]{1,0:T(8,128)(2,1)S(1)}, bf16[1024,1024]{1,0:T(8,128)(2,1)}, u32[]{:S(2)}) copy-start(bf16[1024,1024]{1,0:T(8,128)(2,1)} %param.15) | copy-start | bytes 6291460
  241.6 9.1 %collective-permute-start.18 = (f32[1,1024]{1,0:T(1,128)S(1)}, f32[1,1024]{1,0:T(1,128)S(1)}, u32[]{:S(2)}, u32[]{:S(2)}) collective-permute-start(f32[1,1024]{1,0:T(1,128)S(1)} %slice.165), channel_id=1, source_target_pairs={{0,1},{1,2},{2,3},{3,4},{4,5},{5,6},{6,7},{7,8},{8,9},{9,10},{10,1... | collective-permute-start | bytes 12296 | tf_op jit(solution)/shard_map/lift/ppermute | solution.py:28
Sparse Core Ops, SparseCore 0:
  160.6 23.0 all-gather.2

commit v3 on v2

--- a/solution.py
+++ b/solution.py
@@ -31,6 +31,13 @@
 def rotated(array, axis, by):
     size = lax.axis_size(axis)
     return lax.ppermute(array, axis, [(i, (i + by) % size) for i in range(size)])
+
+
+def around_four(array, axes):
+    above, below = rotated(array, axes, 3), rotated(array, axes, 1)
+    half = array.shape[0] // 2
+    top, bottom = rotated(above[:half], axes, 3), rotated(below[half:], axes, 1)
+    return [array, above, jnp.concatenate([top, bottom], 0), below]
 
 
 def gathered(array, axes):
@@ -149,16 +156,6 @@
     return lax.optimization_barrier((array, earlier))[0]
 
 
-def summed_piece(left, right, pieces):
-    core = lax.axis_index("c")
-    half = left.shape[0] // 2
-    mine = lax.dynamic_slice(left, (core * half, 0), (half, left.shape[1]))
-    other = lax.dynamic_slice(left, ((1 - core) * half, 0), (half, left.shape[1]))
-    got = rotated(dot(other, right).astype(bf16), "c", 1)
-    both = (dot(mine, right) + got.astype(f32)).astype(bf16)
-    return jnp.sum(exchanged(pieces(both), ("x", "yl")).astype(f32), axis=0).astype(bf16)
-
-
 def body(
     tokens,
     fine_gain,
@@ -182,9 +179,10 @@
     swap = [(b * n_tp + a, a * n_tp + b) for a in range(n_seq) for b in range(n_tp)]
 
     with jax.named_scope("weights"):
-        three = (coarse_query, coarse_keyval[:, 0], coarse_keyval[:, 1])
-        sent = [w[:, k * HEAD : (k + 1) * HEAD] for k in range(2) for w in three]
-        rows_here = lax.ppermute(jnp.concatenate(sent, 1), ALL, swap)
+        query_here = lax.ppermute(coarse_query, ALL, swap)
+        keyval_here = lax.ppermute(coarse_keyval, ALL, swap)
+        out_sent = lax.dynamic_slice(coarse_out, (0, s * cols), (cols, cols))
+        out_here = lax.ppermute(out_sent, ALL, swap)
 
     fine_state = fine_layer(tokens, fine_gain, fine_query, fine_keyval, fine_out)
     run_count = tokens.shape[0] // SHORT
@@ -193,37 +191,44 @@
     with jax.named_scope("gather_rows"):
         z_rows = gathered(pooled, ("z",)).reshape(-1, width)
         z_count = z_rows.shape[0]
-        y_rows = [z_rows] + [rotated(z_rows, ("yh", "yl"), by) for by in (3, 2, 1)]
+        y_rows = around_four(z_rows, ("yh", "yl"))
         all_rows = jnp.concatenate(y_rows, 0)
         n = all_rows.shape[0]
 
     with jax.named_scope("weights"):
-        rows_here = gate(rows_here, pooled)
-        gain = lax.dynamic_slice(coarse_gain, (t * cols,), (cols,))
-        scaled = (rows_here.astype(f32) * gain[:, None]).astype(bf16)
-        gram_rows = jnp.transpose(lax.dynamic_slice(down_weight, (128 * z, 0), (128, cols)))
+        query_here, keyval_here, out_here = gate((query_here, keyval_here, out_here), pooled)
+        gain = lax.dynamic_slice(coarse_gain, (t * cols,), (cols,))[:, None]
+        slot_rows = lax.dynamic_slice(down_weight, (128 * z, 0), (128, cols))
+        gram_rows = jnp.transpose(slot_rows)
         half = 3 * HEAD
-        right = jnp.concatenate([scaled[:, :half], gram_rows, scaled[:, half:], gram_rows], 1)
-        first = summed_piece(
-            down_weight,
-            right,
-            lambda v: jnp.swapaxes(v.reshape(4, 128, 2, 512), 1, 2).reshape(8, 128, 512),
-        )
-        proj = gathered(first, ("c", "x")).reshape(width, 512)
-
-        out_sent = lax.dynamic_slice(gate(coarse_out, pooled), (0, s * cols), (cols, cols))
-        out_here = lax.ppermute(out_sent, ALL, swap)
-        slot_rows = lax.dynamic_slice(down_weight, (128 * z + 64 * yh, 0), (64, cols))
-        left = jnp.concatenate([out_here[:HEAD], slot_rows[:32], out_here[HEAD:], slot_rows[32:]], 0)
-        left = gate(left, first)
-        flipped = jnp.transpose(up_weight)
-        second = summed_piece(
-            flipped,
-            jnp.transpose(left),
-            lambda v: jnp.swapaxes(v.reshape(4, 128, 2, 160), 1, 2).reshape(8, 128, 160),
-        )
-        second = gathered(second, ("c", "x")).reshape(width, 160)
-        second = lax.all_gather(jnp.transpose(second), ("yh", "yl"), axis=0)
+        from_rows, from_lift = [], []
+        for k in range(2):
+            for w in (query_here, keyval_here[:, 0], keyval_here[:, 1]):
+                w = w[:, k * HEAD : (k + 1) * HEAD]
+                from_rows.append((w.astype(f32) * gain).astype(bf16))
+            from_rows.append(gram_rows)
+            direct = lax.dynamic_slice(slot_rows, (64 * yh + 32 * k, 0), (32, cols))
+            from_lift.append(jnp.transpose(out_here[k * HEAD : (k + 1) * HEAD]))
+            from_lift.append(jnp.transpose(direct))
+        from_rows = jnp.concatenate(from_rows, 1)
+        from_lift = jnp.concatenate(from_lift, 1)
+        down, flipped = gate((down_weight, jnp.transpose(up_weight)), z_rows)
+
+        def products(core):
+            start = core * (width // 2)
+            one = lax.dynamic_slice(down, (start, 0), (width // 2, cols))
+            two = lax.dynamic_slice(flipped, (start, 0), (width // 2, cols))
+            return dot(one, from_rows), dot(two, from_lift)
+
+        sent = [v.astype(bf16) for v in products(1 - c)]
+        both = [v + rotated(w, "c", 1).astype(f32) for v, w in zip(products(c), sent)]
+        pieces = [jnp.swapaxes(v.astype(bf16).reshape(4, 128, 2, -1), 1, 2) for v in both]
+        pieces = jnp.concatenate(pieces, 3).reshape(8, 128, -1)
+        piece = jnp.sum(exchanged(pieces, ("x", "yl")).astype(f32), axis=0).astype(bf16)
+        piece = gate(piece, (y_rows[1], y_rows[3]))
+        summed = gathered(piece, ("c", "x")).reshape(width, -1)
+        proj = summed[:, : 4 * HEAD]
+        second = lax.all_gather(jnp.transpose(summed[:, 4 * HEAD :]), ("yh", "yl"), axis=0)
 
     with jax.named_scope("project"):
         qkv = dot(all_rows, proj)
@@ -242,14 +247,16 @@
         inverse = by_row(inverse)
         factor = math.log2(math.e) / math.sqrt(HEAD)
         q = (by_row(qkv[:, :HEAD]) * (inverse * factor)).astype(bf16)
-        every_inverse = gathered(inverse.reshape(1, n), ("x", "c")).reshape(4, 2, n, 1)
+        near = around_four(kv, ("x",))
+        every_inverse = gate(inverse.reshape(1, n), (near[1], near[3]))
+        every_inverse = gathered(every_inverse, ("x", "c")).reshape(4, 2, n, 1)
 
     with jax.named_scope("attention"):
         chunks, places = [], []
         for by in (0, 1, 3, 2):
-            mine = kv if by == 0 else rotated(kv, "x", by)
+            mine = near[by]
             other = rotated(mine, "c", 1)
-            source = (x + 4 - by) % 4
+            source = (x + by) % 4
             shift = 128 * (source - x)
             for chunk, core, place in ((mine, c, shift), (other, 1 - c, shift + 32 * (1 - 2 * c))):
                 scale = lax.dynamic_slice(every_inverse, (source, core, 0, 0), (1, 1, n, 1))

time: 260 us -> 258 us (level)
  blocking collectives: 31 us -> 19.8 us
  local copies, waits for them, and re-layouts: 18.7 us -> 24.4 us
  waiting for transfers between devices: 75.7 us -> 70.1 us
  starting transfers between devices: 65 us -> 69.1 us
  matrix products: 24.5 us -> 27.1 us
    all_to_all x1, waiting for transfers between devices: 0.01 us -> 18.1 us  [exchanged(): return lax.all_to_all(pieces, axes, split_axis=0, concat_axis=0, tiled=True)]
    ppermute x1, waiting for transfers between devices: 16.3 us -> 0.01 us  [body(): out_here = lax.ppermute(out_sent, ALL, swap)]
    all_to_all x2 -> x1, blocking collectives: 31 us -> 19.8 us  [exchanged(): return lax.all_to_all(pieces, axes, split_axis=0, concat_axis=0, tiled=True)]
    all_to_all x5 -> x4, waiting for transfers between devices: 32.4 us -> 23.9 us  [gathered(): return lax.all_to_all(copies, axes, split_axis=0, concat_axis=0, tiled=True)]
    all_to_all x1, starting transfers between devices: 11.9 us -> 3.57 us  [exchanged(): return lax.all_to_all(pieces, axes, split_axis=0, concat_axis=0, tiled=True)]
    all_to_all x5 -> x4, starting transfers between devices: 20.9 us -> 28 us  [gathered(): return lax.all_to_all(copies, axes, split_axis=0, concat_axis=0, tiled=True)]
    ppermute x1 -> x2, starting transfers between devices: 4.69 us -> 9.74 us  [the longest x1 5.03 us: body(): keyval_here = lax.ppermute(coarse_keyval, ALL, swap)]
    dot_general x14, matrix products: 21.6 us -> 24.2 us  [dot(): return jnp.dot(a, b, preferred_element_type=f32)]
  transfers between devices with their start and end apart: 26 -> 28, of which waited for: 11 -> 13; matrix products, arithmetic and copies ran while one was open for 18% -> 20% of each run, Pallas kernels for 5% -> 5%
where the time goes in v3:
time: 258 us; the launch traced here: 256 us
  waiting for transfers between devices  70.1 us (27%)
  starting transfers between devices  69.1 us (27%)
  matrix products  27.1 us (11%)
  local copies, waits for them, and re-layouts  24.4 us (9%)
  blocking collectives  19.8 us (8%)
  other arithmetic  18.5 us (7%)
  between operations  14.1 us (5%)
  Pallas kernels  12.9 us (5%)
    all_to_all x4, starting transfers between devices, gathered(): return lax.all_to_all(copies, axes, split_axis=0, concat_axis=0, tiled=True)  28 us
    dot_general x14, matrix products, dot(): return jnp.dot(a, b, preferred_element_type=f32)  24.2 us
    all_to_all x4, waiting for transfers between devices, gathered(): return lax.all_to_all(copies, axes, split_axis=0, concat_axis=0, tiled=True)  23.9 us
    ppermute x17, waiting for transfers between devices, rotated(): lax.ppermute(array, axis, [(i, (i + by) % size) for i in range(size)])  20.9 us
    all_to_all x1, blocking collectives, exchanged(): return lax.all_to_all(pieces, axes, split_axis=0, concat_axis=0, tiled=True)  19.8 us
    ppermute x17, starting transfers between devices, rotated(): lax.ppermute(array, axis, [(i, (i + by) % size) for i in range(size)])  19.2 us
    all_to_all x1, waiting for transfers between devices, exchanged(): return lax.all_to_all(pieces, axes, split_axis=0, concat_axis=0, tiled=True)  18.1 us
    pallas_call x1, Pallas kernels, coarse_attention(): pl.pallas_call(attention_kernel, out_shape=jax.ShapeDtypeStruct((rows, HE...  12.9 us
  transfers between devices with their start and end apart: 28, of which 13 were waited for; matrix products, arithmetic and copies ran while one was open for 20% of the time, Pallas kernels for 5%

profile of v3, /device:TPU:16, one launch (start us, length us, event | category | flops | bytes accessed | tf_op | source)
XLA Modules:
  0.0 256.1 jit_solution(629011412739247699)
XLA Ops:
  6.5 1.4 fusion.23
  7.9 1.2 fusion.25
  9.2 1.9 collective-permute-start
  11.1 4.7 %collective-permute-start.5 = (bf16[256,256]{1,0:T(8,128)(2,1)}, bf16[256,256]{1,0:T(8,128)(2,1)}, u32[]{:S(2)}, u32[]{:S(2)}) collective-permute-start(bf16[256,256]{1,0:T(8,128)(2,1)} %param.18), channel_id=1, source_target_pairs={{0,0},{16,1},{32,2},{48,3},{64,4},{80,5},{96,6},{112,7},{128,8},{1... | collective-permute-start | bytes 393224 | tf_op jit(solution)/shard_map/weights/ppermute | solution.py:182
  15.8 1.7 copy.59
  17.5 5.0 %collective-permute-start.6 = (bf16[256,2,256]{2,0,1:T(8,128)(2,1)}, bf16[256,2,256]{2,0,1:T(8,128)(2,1)S(1)}, u32[]{:S(2)}, u32[]{:S(2)}) collective-permute-start(bf16[256,2,256]{2,0,1:T(8,128)(2,1)} %copy.59), channel_id=1, source_target_pairs={{0,0},{16,1},{32,2},{48,3},{64,4},{80,5},{96,6},{112,7},{128,8},{1... | collective-permute-start | bytes 786440 | tf_op jit(solution)/shard_map/weights/ppermute | solution.py:183
  22.5 1.6 constant_dynamic-slice_fusion.9
  24.1 4.7 %collective-permute-start.7 = (bf16[256,256]{1,0:T(8,128)(2,1)}, bf16[256,256]{1,0:T(8,128)(2,1)}, u32[]{:S(2)}, u32[]{:S(2)}) collective-permute-start(bf16[256,256]{1,0:T(8,128)(2,1)} %constant_dynamic-slice_fusion.9), channel_id=1, source_target_pairs={{0,0},{16,1},{32,2},{48,3},{64,4},{80,5},{96,6},{112,7},{128,8},{1... | collective-permute-start | bytes 393224 | tf_op jit(solution)/shard_map/weights/ppermute | solution.py:185
  28.9 3.1 %fusion.20 = bf16[32,8,8,128]{3,2,1,0:T(8,128)(2,1)} fusion(bf16[256,1024]{1,0:T(8,128)(2,1)S(1)} %fusion.25, bf16[1024,1024]{1,0:T(8,128)(2,1)} %param.13), kind=kOutput, calls=%fused_computation.32 | convolution fusion | flops 537133056 | bytes 3145728 | tf_op jit(solution)/shard_map/dot_general | solution.py:58
  34.5 3.6 %convolution_convert_fusion = bf16[256,2048]{1,0:T(8,128)(2,1)S(1)} fusion(bf16[256,1024]{1,0:T(8,128)(2,1)S(1)} %fusion.25, bf16[1024,2048]{1,0:T(8,128)(2,1)} %param.14), kind=kOutput, calls=%fused_computation.4 | convolution fusion | flops 1074266112 | bytes 5767168 | tf_op jit(solution)/shard_map/dot_general | solution.py:58
  38.2 2.3 convolution_convert_fusion.1
  40.5 1.2 fusion.32
  41.6 1.3 copy.70
  43.0 2.1 fusion.27
  45.1 2.5 fusion.79
  48.7 1.7 fusion.21
  51.3 17.2 %all-to-all-start = ((bf16[8,32,1024]{2,1,0:T(8,128)(2,1)}), bf16[8,32,1024]{2,1,0:T(8,128)(2,1)S(1)}, u32[]{:S(2)}, u32[]{:S(2)}) async-start(bf16[8,32,1024]{2,1,0:T(8,128)(2,1)} %broadcast_in_dim.46), calls=%async_computation | async-start | bytes 1048576 | tf_op jit(solution)/shard_map/gather_rows/all_to_all | solution.py:45
  68.5 0.9 fusion.55
  69.8 1.0 fusion.58
  71.0 10.8 %all-to-all-done = bf16[8,32,1024]{2,1,0:T(8,128)(2,1)S(1)} async-done(((bf16[8,32,1024]{2,1,0:T(8,128)(2,1)}), bf16[8,32,1024]{2,1,0:T(8,128)(2,1)S(1)}, u32[]{:S(2)}, u32[]{:S(2)}) %all-to-all-start) | async-done | bytes 524320 | tf_op jit(solution)/shard_map/gather_rows/all_to_all | solution.py:45
  81.8 1.4 convolution_convert_fusion.2
  84.1 1.2 convolution_convert_fusion.4
  86.1 1.3 collective-permute-done.9
  87.4 1.2 add_convert_fusion.1
  88.7 1.4 add_convert_fusion
  91.8 1.2 pad_maximum_fusion
  93.0 3.6 %all-to-all-start.1 = ((bf16[8,128,672]{1,2,0:T(8,128)(2,1)}), bf16[8,128,672]{1,2,0:T(8,128)(2,1)S(1)}, u32[]{:S(2)}, u32[]{:S(2)}) async-start(bf16[8,128,672]{1,2,0:T(8,128)(2,1)} %bitcast.24), calls=%async_computation.1 | async-start | bytes 2752512 | tf_op jit(solution)/shard_map/weights/all_to_all | solution.py:49
  96.6 4.3 %collective-permute-start.1 = (bf16[256,1024]{1,0:T(8,128)(2,1)S(1)}, bf16[256,1024]{1,0:T(8,128)(2,1)S(1)}, u32[]{:S(2)}, u32[]{:S(2)}) collective-permute-start(bf16[256,1024]{1,0:T(8,128)(2,1)S(1)} %bitcast.146), channel_id=1, source_target_pairs={{0,130},{2,0},{128,2},{130,128},{1,131},{3,1},{129,3},{131,129},{4... | collective-permute-start | bytes 1572872 | tf_op jit(solution)/shard_map/gather_rows/ppermute | solution.py:33
  100.9 18.1 %all-to-all-done.1 = bf16[8,128,672]{1,2,0:T(8,128)(2,1)S(1)} async-done(((bf16[8,128,672]{1,2,0:T(8,128)(2,1)}), bf16[8,128,672]{1,2,0:T(8,128)(2,1)S(1)}, u32[]{:S(2)}, u32[]{:S(2)}) %all-to-all-start.1) | async-done | bytes 1376288 | tf_op jit(solution)/shard_map/weights/all_to_all | solution.py:49
  119.2 6.6 %collective-permute-done.1 = bf16[256,1024]{1,0:T(8,128)(2,1)S(1)} collective-permute-done((bf16[256,1024]{1,0:T(8,128)(2,1)S(1)}, bf16[256,1024]{1,0:T(8,128)(2,1)S(1)}, u32[]{:S(2)}, u32[]{:S(2)}) %collective-permute-start.1) | collective-permute-done | bytes 524320 | tf_op jit(solution)/shard_map/gather_rows/ppermute | solution.py:33
  125.8 1.3 broadcast_in_dim.47
  127.1 4.1 %all-to-all-start.2 = ((bf16[8,128,672]{1,2,0:T(8,128)(2,1)}), bf16[8,128,672]{1,2,0:T(8,128)(2,1)S(1)}, u32[]{:S(2)}, u32[]{:S(2)}) async-start(bf16[8,128,672]{1,2,0:T(8,128)(2,1)} %broadcast_in_dim.47), calls=%async_computation.2 | async-start | bytes 2752512 | tf_op jit(solution)/shard_map/weights/all_to_all | solution.py:45
  132.0 2.6 %collective-permute-start.2 = (bf16[128,1024]{1,0:T(8,128)(2,1)}, bf16[128,1024]{1,0:T(8,128)(2,1)S(1)}, u32[]{:S(2)}, u32[]{:S(2)}) collective-permute-start(bf16[128,1024]{1,0:T(8,128)(2,1)} %slice.161), channel_id=1, source_target_pairs={{0,130},{2,0},{128,2},{130,128},{1,131},{3,1},{129,3},{131,129},{4... | collective-permute-start | bytes 786440 | tf_op jit(solution)/shard_map/gather_rows/ppermute | solution.py:33
  136.5 4.6 %collective-permute-done.2 = bf16[128,1024]{1,0:T(8,128)(2,1)S(1)} collective-permute-done((bf16[128,1024]{1,0:T(8,128)(2,1)}, bf16[128,1024]{1,0:T(8,128)(2,1)S(1)}, u32[]{:S(2)}, u32[]{:S(2)}) %collective-permute-start.2) | collective-permute-done | bytes 262176 | tf_op jit(solution)/shard_map/gather_rows/ppermute | solution.py:33
  141.8 1.3 collective-permute-done.4
  144.7 5.3 %all-to-all-done.2 = bf16[8,128,672]{1,2,0:T(8,128)(2,1)S(1)} async-done(((bf16[8,128,672]{1,2,0:T(8,128)(2,1)}), bf16[8,128,672]{1,2,0:T(8,128)(2,1)S(1)}, u32[]{:S(2)}, u32[]{:S(2)}) %all-to-all-start.2) | async-done | bytes 1376288 | tf_op jit(solution)/shard_map/weights/all_to_all | solution.py:45
  151.0 2.9 %fusion.80 = (bf16[1024,512]{1,0:T(8,128)(2,1)S(1)}, f32[1024,512]{1,0:T(8,128)S(1)}) fusion(bf16[1024,1024]{1,0:T(8,128)(2,1)} %constant_dynamic-update-slice_fusion, bf16[1024,672]{0,1:T(8,128)(2,1)S(1)} %copy_bitcast_fusion), kind=kOutput, calls=%fused_computation.157 | convolution fusion | flops 1074266112 | bytes 6291456 | tf_op jit(solution)/shard_map/project/dot_general | solution.py:58
  153.9 1.2 fusion.37
  155.5 1.9 collective-permute-start.10
  158.2 3.3 %all-to-all-start.3 = ((f32[8,1,1024]{2,1,0:T(1,128)}), f32[8,1,1024]{2,1,0:T(1,128)S(1)}, u32[]{:S(2)}, u32[]{:S(2)}) async-start(f32[8,1,1024]{2,1,0:T(1,128)} %broadcast_in_dim.48), calls=%async_computation.3 | async-start | bytes 65536 | tf_op jit(solution)/shard_map/project/all_to_all | solution.py:45
  161.7 7.8 %all-to-all-done.3 = f32[8,1,1024]{2,1,0:T(1,128)S(1)} async-done(((f32[8,1,1024]{2,1,0:T(1,128)}), f32[8,1,1024]{2,1,0:T(1,128)S(1)}, u32[]{:S(2)}, u32[]{:S(2)}) %all-to-all-start.3) | async-done | bytes 32800 | tf_op jit(solution)/shard_map/project/all_to_all | solution.py:45
  169.9 1.9 collective-permute-done.11
  172.5 3.3 %all-to-all-start.4 = ((f32[8,1,1024]{2,1,0:T(1,128)}), f32[8,1,1024]{2,1,0:T(1,128)S(1)}, u32[]{:S(2)}, u32[]{:S(2)}) async-start(f32[8,1,1024]{2,1,0:T(1,128)} %broadcast_in_dim.49), calls=%async_computation.4 | async-start | bytes 65536 | tf_op jit(solution)/shard_map/project/all_to_all | solution.py:45
  176.0 1.7 slice.173
  177.7 3.2 %collective-permute-start.15 = (bf16[512,256]{1,0:T(8,128)(2,1)}, bf16[512,256]{1,0:T(8,128)(2,1)}, u32[]{:S(2)}, u32[]{:S(2)}) collective-permute-start(bf16[512,256]{1,0:T(8,128)(2,1)} %slice.173), channel_id=1, source_target_pairs={{0,12},{4,0},{8,4},{12,8},{1,13},{5,1},{9,5},{13,9},{2,14},{6,2},{... | collective-permute-start | bytes 786440 | tf_op jit(solution)/shard_map/project/ppermute | solution.py:33
  180.8 1.7 slice.174
  183.0 1.5 multiply_convert_fusion.3
  184.8 1.2 multiply_convert_fusion.6.refs_1_
  186.0 1.0 collective-permute-done.15
  187.0 1.0 constant_dynamic-update-slice_fusion.6
  188.0 4.0 %collective-permute-done.16 = bf16[512,256]{1,0:T(8,128)(2,1)S(1)} collective-permute-done((bf16[512,256]{1,0:T(8,128)(2,1)}, bf16[512,256]{1,0:T(8,128)(2,1)S(1)}, u32[]{:S(2)}, u32[]{:S(2)}) %collective-permute-start.16) | collective-permute-done | bytes 262176 | tf_op jit(solution)/shard_map/project/ppermute | solution.py:33
  192.3 1.2 multiply_convert_fusion.4.refs_3_
  194.2 12.9 %attention.1 = bf16[1024,128]{1,0:T(8,128)(2,1)S(1)} custom-call(s32[8]{0:T(128)S(1)} %stack.35.place_ref, bf16[1024,128]{1,0:T(8,128)(2,1)S(1)} %fusion.38.q_ref, bf16[1024,256]{1,0:T(8,128)(2,1)S(1)} %multiply_convert_fusion.7.refs_0_, bf16[1024,256]{1,0:T(8,128)(2,1)S(1)} %multiply_convert_fusion.6.refs_1_, ...), custom_call_target="tpu_custom_call" | custom-call | tf_op jit(solution)/shard_map/attention/pallas_call | solution.py:142
  207.1 2.7 %collective-permute-start.20 = (bf16[256,128]{1,0:T(8,128)(2,1)S(1)}, bf16[256,128]{1,0:T(8,128)(2,1)S(1)}, u32[]{:S(2)}, u32[]{:S(2)}) collective-permute-start(bf16[256,128]{1,0:T(8,128)(2,1)S(1)} %get-tuple-element.26), channel_id=1, source_target_pairs={{0,130},{2,0},{128,2},{130,128},{1,131},{3,1},{129,3},{131,129},{4... | collective-permute-start | bytes 196616 | tf_op jit(solution)/shard_map/lift/ppermute | solution.py:33
  209.8 2.9 %collective-permute-start.19 = (bf16[256,128]{1,0:T(8,128)(2,1)S(1)}, bf16[256,128]{1,0:T(8,128)(2,1)S(1)}, u32[]{:S(2)}, u32[]{:S(2)}) collective-permute-start(bf16[256,128]{1,0:T(8,128)(2,1)S(1)} %get-tuple-element.25), channel_id=1, source_target_pairs={{0,128},{2,130},{128,0},{130,2},{1,129},{3,131},{129,1},{131,3},{4... | collective-permute-start | bytes 196616 | tf_op jit(solution)/shard_map/lift/ppermute | solution.py:33
  212.7 1.2 fusion.44
  214.0 1.0 slice.176
  215.0 1.2 convolution_add_fusion.1
  216.5 1.2 fusion.43
  217.8 1.4 fusion.16
  219.2 19.8 %all_to_all.30 = bf16[8,32,1024]{2,1,0:T(8,128)(2,1)S(1)} all-to-all(bf16[8,32,1024]{2,1,0:T(8,128)(2,1)S(1)} %bitcast.150), channel_id=1, replica_groups=mesh['yh'=2,'z'=8,'x'=4,'yl'=2,'c'=2] {'z'}, dimensions={0} | all-to-all | bytes 1048576 | tf_op jit(solution)/shard_map/lift/all_to_all | solution.py:49
  239.1 1.9 collective-permute-start.21
  241.0 7.2 %collective-permute-done.21 = f32[1,1024]{1,0:T(1,128)S(1)} collective-permute-done((f32[1,1024]{1,0:T(1,128)S(1)}, f32[1,1024]{1,0:T(1,128)S(1)}, u32[]{:S(2)}, u32[]{:S(2)}) %collective-permute-start.21) | collective-permute-done | bytes 4128 | tf_op jit(solution)/shard_map/lift/ppermute | solution.py:28
  248.3 0.9 fusion.22
  (111 shorter events, 19.4 us)
Async XLA Ops:
  6.5 41.9 %copy-start = (bf16[1024,1024]{1,0:T(8,128)(2,1)S(1)}, bf16[1024,1024]{1,0:T(8,128)(2,1)}, u32[]{:S(2)}) copy-start(bf16[1024,1024]{1,0:T(8,128)(2,1)} %param.15) | copy-start | bytes 6291460
  9.2 29.0 %collective-permute-start = (bf16[256,1024]{1,0:T(8,128)(2,1)S(1)}, bf16[256,1024]{1,0:T(8,128)(2,1)}, u32[]{:S(2)}, u32[]{:S(2)}) collective-permute-start(bf16[256,1024]{1,0:T(8,128)(2,1)S(1)} %fusion.25), channel_id=1, source_target_pairs={{0,1},{1,2},{2,3},{3,4},{4,5},{5,6},{6,7},{7,8},{8,9},{9,10},{10,1... | collective-permute-start | bytes 1572872 | tf_op jit(solution)/shard_map/ppermute | solution.py:28
  11.1 57.4 %collective-permute-start.5 = (bf16[256,256]{1,0:T(8,128)(2,1)}, bf16[256,256]{1,0:T(8,128)(2,1)}, u32[]{:S(2)}, u32[]{:S(2)}) collective-permute-start(bf16[256,256]{1,0:T(8,128)(2,1)} %param.18), channel_id=1, source_target_pairs={{0,0},{16,1},{32,2},{48,3},{64,4},{80,5},{96,6},{112,7},{128,8},{1... | collective-permute-start | bytes 393224 | tf_op jit(solution)/shard_map/weights/ppermute | solution.py:182
  17.5 51.0 %collective-permute-start.6 = (bf16[256,2,256]{2,0,1:T(8,128)(2,1)}, bf16[256,2,256]{2,0,1:T(8,128)(2,1)S(1)}, u32[]{:S(2)}, u32[]{:S(2)}) collective-permute-start(bf16[256,2,256]{2,0,1:T(8,128)(2,1)} %copy.59), channel_id=1, source_target_pairs={{0,0},{16,1},{32,2},{48,3},{64,4},{80,5},{96,6},{112,7},{128,8},{1... | collective-permute-start | bytes 786440 | tf_op jit(solution)/shard_map/weights/ppermute | solution.py:183
  24.1 44.4 %collective-permute-start.7 = (bf16[256,256]{1,0:T(8,128)(2,1)}, bf16[256,256]{1,0:T(8,128)(2,1)}, u32[]{:S(2)}, u32[]{:S(2)}) collective-permute-start(bf16[256,256]{1,0:T(8,128)(2,1)} %constant_dynamic-slice_fusion.9), channel_id=1, source_target_pairs={{0,0},{16,1},{32,2},{48,3},{64,4},{80,5},{96,6},{112,7},{128,8},{1... | collective-permute-start | bytes 393224 | tf_op jit(solution)/shard_map/weights/ppermute | solution.py:185
  34.5 3.6 %copy-start.7 = (bf16[1024,2048]{1,0:T(8,128)(2,1)S(1)}, bf16[1024,2048]{1,0:T(8,128)(2,1)}, u32[]{:S(2)}) copy-start(bf16[1024,2048]{1,0:T(8,128)(2,1)} %param.14) | copy-start | bytes 12582916
  43.0 2.1 copy-start.6
  45.1 2.5 copy-start.4
  47.6 1.0 copy-start.2
  50.4 31.4 %copy-start.5 = (bf16[1024,256]{1,0:T(8,128)(2,1)S(1)}, bf16[1024,256]{1,0:T(8,128)(2,1)}, u32[]{:S(2)}) copy-start(bf16[1024,256]{1,0:T(8,128)(2,1)} %param.16) | copy-start | bytes 1572868
  51.3 30.5 %all-to-all-start = ((bf16[8,32,1024]{2,1,0:T(8,128)(2,1)}), bf16[8,32,1024]{2,1,0:T(8,128)(2,1)S(1)}, u32[]{:S(2)}, u32[]{:S(2)}) async-start(bf16[8,32,1024]{2,1,0:T(8,128)(2,1)} %broadcast_in_dim.46), calls=%async_computation | async-start | bytes 1048576 | tf_op jit(solution)/shard_map/gather_rows/all_to_all | solution.py:45
  83.2 5.5 %collective-permute-start.8 = (bf16[512,1024]{1,0:T(8,128)(2,1)}, bf16[512,1024]{1,0:T(8,128)(2,1)S(1)}, u32[]{:S(2)}, u32[]{:S(2)}) collective-permute-start(bf16[512,1024]{1,0:T(8,128)(2,1)} %convolution_convert_fusion.2), channel_id=1, source_target_pairs={{0,1},{1,0},{2,3},{3,2},{4,5},{5,4},{6,7},{7,6},{8,9},{9,8},{10,11... | collective-permute-start | bytes 3145736 | tf_op jit(solution)/shard_map/weights/ppermute | solution.py:33
  85.3 2.0 collective-permute-start.9
  93.0 26.0 %all-to-all-start.1 = ((bf16[8,128,672]{1,2,0:T(8,128)(2,1)}), bf16[8,128,672]{1,2,0:T(8,128)(2,1)S(1)}, u32[]{:S(2)}, u32[]{:S(2)}) async-start(bf16[8,128,672]{1,2,0:T(8,128)(2,1)} %bitcast.24), calls=%async_computation.1 | async-start | bytes 2752512 | tf_op jit(solution)/shard_map/weights/all_to_all | solution.py:49
  96.6 29.2 %collective-permute-start.1 = (bf16[256,1024]{1,0:T(8,128)(2,1)S(1)}, bf16[256,1024]{1,0:T(8,128)(2,1)S(1)}, u32[]{:S(2)}, u32[]{:S(2)}) collective-permute-start(bf16[256,1024]{1,0:T(8,128)(2,1)S(1)} %bitcast.146), channel_id=1, source_target_pairs={{0,130},{2,0},{128,2},{130,128},{1,131},{3,1},{129,3},{131,129},{4... | collective-permute-start | bytes 1572872 | tf_op jit(solution)/shard_map/gather_rows/ppermute | solution.py:33
  100.9 24.9 %collective-permute-start.3 = (bf16[256,1024]{1,0:T(8,128)(2,1)S(1)}, bf16[256,1024]{1,0:T(8,128)(2,1)S(1)}, u32[]{:S(2)}, u32[]{:S(2)}) collective-permute-start(bf16[256,1024]{1,0:T(8,128)(2,1)S(1)} %bitcast.147), channel_id=1, source_target_pairs={{0,2},{2,128},{128,130},{130,0},{1,3},{3,129},{129,131},{131,1},{4... | collective-permute-start | bytes 1572872 | tf_op jit(solution)/shard_map/gather_rows/ppermute | solution.py:33
  127.1 23.0 %all-to-all-start.2 = ((bf16[8,128,672]{1,2,0:T(8,128)(2,1)}), bf16[8,128,672]{1,2,0:T(8,128)(2,1)S(1)}, u32[]{:S(2)}, u32[]{:S(2)}) async-start(bf16[8,128,672]{1,2,0:T(8,128)(2,1)} %broadcast_in_dim.47), calls=%async_computation.2 | async-start | bytes 2752512 | tf_op jit(solution)/shard_map/weights/all_to_all | solution.py:45
  131.2 81.5 %all-gather.3.cloned.1.call-start = ((), (), s32[]{:S(2)}) async-start(), calls=%async_computation.6 | async-start | bytes 1638400 | tf_op jit(solution)/shard_map/weights/all_gather | solution.py:231
  132.0 9.1 %collective-permute-start.2 = (bf16[128,1024]{1,0:T(8,128)(2,1)}, bf16[128,1024]{1,0:T(8,128)(2,1)S(1)}, u32[]{:S(2)}, u32[]{:S(2)}) collective-permute-start(bf16[128,1024]{1,0:T(8,128)(2,1)} %slice.161), channel_id=1, source_target_pairs={{0,130},{2,0},{128,2},{130,128},{1,131},{3,1},{129,3},{131,129},{4... | collective-permute-start | bytes 786440 | tf_op jit(solution)/shard_map/gather_rows/ppermute | solution.py:33
  134.7 8.5 %collective-permute-start.4 = (bf16[128,1024]{1,0:T(8,128)(2,1)S(1)}, bf16[128,1024]{1,0:T(8,128)(2,1)S(1)}, u32[]{:S(2)}, u32[]{:S(2)}) collective-permute-start(bf16[128,1024]{1,0:T(8,128)(2,1)S(1)} %slice.162), channel_id=1, source_target_pairs={{0,2},{2,128},{128,130},{130,0},{1,3},{3,129},{129,131},{131,1},{4... | collective-permute-start | bytes 786440 | tf_op jit(solution)/shard_map/gather_rows/ppermute | solution.py:33
  155.5 14.5 %collective-permute-start.10 = (bf16[1024,256]{1,0:T(8,128)(2,1)S(1)}, bf16[1024,256]{1,0:T(8,128)(2,1)}, u32[]{:S(2)}, u32[]{:S(2)}) collective-permute-start(bf16[1024,256]{1,0:T(8,128)(2,1)S(1)} %bitcast.151), channel_id=1, source_target_pairs={{0,12},{4,0},{8,4},{12,8},{1,13},{5,1},{9,5},{13,9},{2,14},{6,2},{... | collective-permute-start | bytes 1572872 | tf_op jit(solution)/shard_map/project/ppermute | solution.py:33
  157.3 14.5 %collective-permute-start.11 = (bf16[1024,256]{1,0:T(8,128)(2,1)S(1)}, bf16[1024,256]{1,0:T(8,128)(2,1)}, u32[]{:S(2)}, u32[]{:S(2)}) collective-permute-start(bf16[1024,256]{1,0:T(8,128)(2,1)S(1)} %bitcast.152), channel_id=1, source_target_pairs={{0,4},{4,8},{8,12},{12,0},{1,5},{5,9},{9,13},{13,1},{2,6},{6,10},{... | collective-permute-start | bytes 1572872 | tf_op jit(solution)/shard_map/project/ppermute | solution.py:33
  157.6 27.2 %collective-permute-start.12 = (bf16[1024,256]{1,0:T(8,128)(2,1)S(1)}, bf16[1024,256]{1,0:T(8,128)(2,1)}, u32[]{:S(2)}, u32[]{:S(2)}) collective-permute-start(bf16[1024,256]{1,0:T(8,128)(2,1)S(1)} %bitcast.153), channel_id=1, source_target_pairs={{0,1},{1,0},{2,3},{3,2},{4,5},{5,4},{6,7},{7,6},{8,9},{9,8},{10,11... | collective-permute-start | bytes 1572872 | tf_op jit(solution)/shard_map/attention/ppermute | solution.py:33
  158.2 11.3 %all-to-all-start.3 = ((f32[8,1,1024]{2,1,0:T(1,128)}), f32[8,1,1024]{2,1,0:T(1,128)S(1)}, u32[]{:S(2)}, u32[]{:S(2)}) async-start(f32[8,1,1024]{2,1,0:T(1,128)} %broadcast_in_dim.48), calls=%async_computation.3 | async-start | bytes 65536 | tf_op jit(solution)/shard_map/project/all_to_all | solution.py:45
  172.5 10.5 %all-to-all-start.4 = ((f32[8,1,1024]{2,1,0:T(1,128)}), f32[8,1,1024]{2,1,0:T(1,128)S(1)}, u32[]{:S(2)}, u32[]{:S(2)}) async-start(f32[8,1,1024]{2,1,0:T(1,128)} %broadcast_in_dim.49), calls=%async_computation.4 | async-start | bytes 65536 | tf_op jit(solution)/shard_map/project/all_to_all | solution.py:45
  177.7 9.4 %collective-permute-start.15 = (bf16[512,256]{1,0:T(8,128)(2,1)}, bf16[512,256]{1,0:T(8,128)(2,1)}, u32[]{:S(2)}, u32[]{:S(2)}) collective-permute-start(bf16[512,256]{1,0:T(8,128)(2,1)} %slice.173), channel_id=1, source_target_pairs={{0,12},{4,0},{8,4},{12,8},{1,13},{5,1},{9,5},{13,9},{2,14},{6,2},{... | collective-permute-start | bytes 786440 | tf_op jit(solution)/shard_map/project/ppermute | solution.py:33
  182.5 9.5 %collective-permute-start.16 = (bf16[512,256]{1,0:T(8,128)(2,1)}, bf16[512,256]{1,0:T(8,128)(2,1)S(1)}, u32[]{:S(2)}, u32[]{:S(2)}) collective-permute-start(bf16[512,256]{1,0:T(8,128)(2,1)} %slice.174), channel_id=1, source_target_pairs={{0,4},{4,8},{8,12},{12,0},{1,5},{5,9},{9,13},{13,1},{2,6},{6,10},{... | collective-permute-start | bytes 786440 | tf_op jit(solution)/shard_map/project/ppermute | solution.py:33
  182.5 9.8 %collective-permute-start.13 = (bf16[1024,256]{1,0:T(8,128)(2,1)}, bf16[1024,256]{1,0:T(8,128)(2,1)}, u32[]{:S(2)}, u32[]{:S(2)}) collective-permute-start(bf16[1024,256]{1,0:T(8,128)(2,1)} %collective-permute-done.10), channel_id=1, source_target_pairs={{0,1},{1,0},{2,3},{3,2},{4,5},{5,4},{6,7},{7,6},{8,9},{9,8},{10,11... | collective-permute-start | bytes 1572872 | tf_op jit(solution)/shard_map/attention/ppermute | solution.py:33
  182.5 11.1 %collective-permute-start.14 = (bf16[1024,256]{1,0:T(8,128)(2,1)}, bf16[1024,256]{1,0:T(8,128)(2,1)S(1)}, u32[]{:S(2)}, u32[]{:S(2)}) collective-permute-start(bf16[1024,256]{1,0:T(8,128)(2,1)} %collective-permute-done.11), channel_id=1, source_target_pairs={{0,1},{1,0},{2,3},{3,2},{4,5},{5,4},{6,7},{7,6},{8,9},{9,8},{10,11... | collective-permute-start | bytes 1572872 | tf_op jit(solution)/shard_map/attention/ppermute | solution.py:33
  192.0 2.0 collective-permute-start.17
  207.1 9.4 %collective-permute-start.20 = (bf16[256,128]{1,0:T(8,128)(2,1)S(1)}, bf16[256,128]{1,0:T(8,128)(2,1)S(1)}, u32[]{:S(2)}, u32[]{:S(2)}) collective-permute-start(bf16[256,128]{1,0:T(8,128)(2,1)S(1)} %get-tuple-element.26), channel_id=1, source_target_pairs={{0,130},{2,0},{128,2},{130,128},{1,131},{3,1},{129,3},{131,129},{4... | collective-permute-start | bytes 196616 | tf_op jit(solution)/shard_map/lift/ppermute | solution.py:33
  209.8 5.1 %collective-permute-start.18 = (bf16[256,128]{1,0:T(8,128)(2,1)S(1)}, bf16[256,128]{1,0:T(8,128)(2,1)S(1)}, u32[]{:S(2)}, u32[]{:S(2)}) collective-permute-start(bf16[256,128]{1,0:T(8,128)(2,1)S(1)} %get-tuple-element.27), channel_id=1, source_target_pairs={{0,2},{2,128},{128,130},{130,0},{1,3},{3,129},{129,131},{131,1},{4... | collective-permute-start | bytes 196616 | tf_op jit(solution)/shard_map/lift/ppermute | solution.py:33
  209.8 7.9 %collective-permute-start.19 = (bf16[256,128]{1,0:T(8,128)(2,1)S(1)}, bf16[256,128]{1,0:T(8,128)(2,1)S(1)}, u32[]{:S(2)}, u32[]{:S(2)}) collective-permute-start(bf16[256,128]{1,0:T(8,128)(2,1)S(1)} %get-tuple-element.25), channel_id=1, source_target_pairs={{0,128},{2,130},{128,0},{130,2},{1,129},{3,131},{129,1},{131,3},{4... | collective-permute-start | bytes 196616 | tf_op jit(solution)/shard_map/lift/ppermute | solution.py:33
  217.8 30.5 %copy-start.3 = (bf16[256,1024]{1,0:T(8,128)(2,1)S(1)}, bf16[256,1024]{1,0:T(8,128)(2,1)}, u32[]{:S(2)}) copy-start(bf16[256,1024]{1,0:T(8,128)(2,1)} %get-tuple-element.43) | copy-start | bytes 1572868
  217.8 31.4 %copy-start.1 = (bf16[1024,1024]{1,0:T(8,128)(2,1)S(1)}, bf16[1024,1024]{1,0:T(8,128)(2,1)}, u32[]{:S(2)}) copy-start(bf16[1024,1024]{1,0:T(8,128)(2,1)} %param.15) | copy-start | bytes 6291460
  239.1 9.1 %collective-permute-start.21 = (f32[1,1024]{1,0:T(1,128)S(1)}, f32[1,1024]{1,0:T(1,128)S(1)}, u32[]{:S(2)}, u32[]{:S(2)}) collective-permute-start(f32[1,1024]{1,0:T(1,128)S(1)} %slice.177), channel_id=1, source_target_pairs={{0,1},{1,2},{2,3},{3,4},{4,5},{5,6},{6,7},{7,8},{8,9},{9,10},{10,1... | collective-permute-start | bytes 12296 | tf_op jit(solution)/shard_map/lift/ppermute | solution.py:28
Sparse Core Ops, SparseCore 0:
  157.7 23.6 all-gather.2

commit v4 on v3

--- a/solution.py
+++ b/solution.py
@@ -88,7 +88,7 @@
     return (inputs + dot(local, fine_out)).astype(bf16)
 
 
-def attention_kernel(place_ref, q_ref, *refs):
+def attention_kernel(place_ref, q_ref, inverse_ref, *refs):
     chunks, out_ref = refs[:-1], refs[-1]
     tile = q_ref.shape[0]
     step = pl.program_id(0)
@@ -109,6 +109,7 @@
             s = lax.dot_general(
                 q, chunk[rows, :HEAD], (((1,), (1,)), ((), ())), preferred_element_type=f32
             )
+            s = s * inverse_ref[j : j + 1, rows]
             if masked:
                 s = jnp.where(ahead >= place_ref[j], s, big_negative)
             scores.append(s)
@@ -122,7 +123,8 @@
             if masked:
                 p = jnp.where(ahead >= place_ref[j], p, 0.0)
             sums = p if sums is None else sums + p
-            acc = acc + dot(p.astype(bf16), chunk[rows, HEAD:])
+            p = (p * inverse_ref[j : j + 1, rows]).astype(bf16)
+            acc = acc + dot(p, chunk[rows, HEAD:])
         total = total * fade + jnp.sum(sums, axis=-1, keepdims=True)
         return new_peak, total, acc
 
@@ -136,7 +138,7 @@
     out_ref[...] = (acc / total).astype(bf16)
 
 
-def coarse_attention(q, chunks, places, tile=256):
+def coarse_attention(q, inverses, chunks, places, tile=256):
     rows = q.shape[0]
     whole = pl.BlockSpec(chunks[0].shape, lambda i, place: (0, 0))
     return pl.pallas_call(
@@ -145,15 +147,65 @@
         grid_spec=pltpu.PrefetchScalarGridSpec(
             num_scalar_prefetch=1,
             grid=(rows // tile,),
-            in_specs=[pl.BlockSpec((tile, HEAD), lambda i, place: (i, 0))] + [whole] * len(chunks),
+            in_specs=[
+                pl.BlockSpec((tile, HEAD), lambda i, place: (i, 0)),
+                pl.BlockSpec(inverses.shape, lambda i, place: (0, 0)),
+            ]
+            + [whole] * len(chunks),
             out_specs=pl.BlockSpec((tile, HEAD), lambda i, place: (i, 0)),
         ),
         compiler_params=pltpu.CompilerParams(vmem_limit_bytes=48 << 20),
-    )(places, q, *chunks)
+    )(places, q, inverses, *chunks)
 
 
 def gate(array, earlier):
     return lax.optimization_barrier((array, earlier))[0]
+
+
+def product_kernel(where_ref, down_ref, up_ref, gain_ref, pack_ref, give_ref, keep_ref):
+    core, gram_at = where_ref[0], where_ref[1]
+    gain = gain_ref[...]
+    cols = pack_ref.shape[1]
+    scaled = [
+        (pack_ref[j * cols : (j + 1) * cols, :].astype(f32) * gain).astype(bf16) for j in range(3)
+    ]
+    gram_rows = down_ref[pl.ds(pl.multiple_of(gram_at, 128), 128), :]
+    right, left = [], []
+    for k in range(2):
+        lanes = slice(k * HEAD, (k + 1) * HEAD)
+        right.append(jnp.concatenate([w[:, lanes] for w in scaled], 1))
+        direct = down_ref[pl.ds(pl.multiple_of(where_ref[2 + k], 32), 32), :]
+        start = 3 * cols + k * HEAD
+        left.append(jnp.concatenate([pack_ref[start : start + HEAD, :], direct], 0))
+    half = down_ref.shape[0] // 2
+    for out_ref, side in ((give_ref, 1 - core), (keep_ref, core)):
+        rows = pl.ds(pl.multiple_of(side * half, half), half)
+        one, two = down_ref[rows, :], up_ref[:, rows]
+        gram = lax.dot_general(
+            one, gram_rows, (((1,), (1,)), ((), ())), preferred_element_type=f32
+        ).astype(bf16)
+        for k in range(2):
+            proj = dot(one, right[k]).astype(bf16)
+            lift = dot(left[k], two).astype(bf16)
+            for q in range(4):
+                block = slice(q * 128, (q + 1) * 128)
+                for j in range(3):
+                    out_ref[q, k, j * 128 : (j + 1) * 128, :] = proj[block, j * 128 : (j + 1) * 128]
+                out_ref[q, k, 3 * 128 : 4 * 128, :] = gram[block]
+                out_ref[q, k, 4 * 128 :, :] = lift[:, block]
+
+
+def weight_products(where, down, up, gain, pack):
+    width = down.shape[0]
+    out = jax.ShapeDtypeStruct((4, 2, 4 * 128 + HEAD + 32, width // 8), bf16)
+    whole = pl.BlockSpec(memory_space=pltpu.VMEM)
+    return pl.pallas_call(
+        product_kernel,
+        out_shape=(out, out),
+        in_specs=[pl.BlockSpec(memory_space=pltpu.SMEM)] + [whole] * 4,
+        out_specs=(whole, whole),
+        compiler_params=pltpu.CompilerParams(vmem_limit_bytes=40 << 20),
+    )(where, down, up, gain, pack)
 
 
 def body(
@@ -179,106 +231,90 @@
     swap = [(b * n_tp + a, a * n_tp + b) for a in range(n_seq) for b in range(n_tp)]
 
     with jax.named_scope("weights"):
-        query_here = lax.ppermute(coarse_query, ALL, swap)
-        keyval_here = lax.ppermute(coarse_keyval, ALL, swap)
         out_sent = lax.dynamic_slice(coarse_out, (0, s * cols), (cols, cols))
-        out_here = lax.ppermute(out_sent, ALL, swap)
+        sent = (coarse_query, coarse_keyval[:, 0], coarse_keyval[:, 1], out_sent)
+        pack = lax.ppermute(jnp.concatenate(sent, 0), ALL, swap)
 
     fine_state = fine_layer(tokens, fine_gain, fine_query, fine_keyval, fine_out)
     run_count = tokens.shape[0] // SHORT
     pooled = jnp.mean(fine_state.astype(f32).reshape(run_count, SHORT, width), axis=1).astype(bf16)
 
+    with jax.named_scope("weights"):
+        gain = lax.dynamic_slice(coarse_gain, (t * cols,), (cols,))[:, None]
+        direct_at = 512 * yh + 32 * z
+        where = jnp.stack([c, 128 * z, direct_at, direct_at + 256]).astype(jnp.int32)
+        give, keep = weight_products(where, down_weight, up_weight, gain, gate(pack, pooled))
+        both = keep.astype(f32) + rotated(give, "c", 1).astype(f32)
+        pieces = exchanged(both.astype(bf16), ("x",))
+        pieces = jnp.sum(pieces.astype(f32), axis=0)
+        mine = lax.dynamic_index_in_dim(pieces, yl, 0, keepdims=False)
+        other = lax.dynamic_index_in_dim(pieces, 1 - yl, 0, keepdims=False).astype(bf16)
+        piece = (mine + rotated(other, "yl", 1).astype(f32)).astype(bf16)
+
     with jax.named_scope("gather_rows"):
-        z_rows = gathered(pooled, ("z",)).reshape(-1, width)
-        z_count = z_rows.shape[0]
+        z_rows = gathered(gate(pooled, other), ("z",)).reshape(-1, width)
         y_rows = around_four(z_rows, ("yh", "yl"))
         all_rows = jnp.concatenate(y_rows, 0)
         n = all_rows.shape[0]
 
     with jax.named_scope("weights"):
-        query_here, keyval_here, out_here = gate((query_here, keyval_here, out_here), pooled)
-        gain = lax.dynamic_slice(coarse_gain, (t * cols,), (cols,))[:, None]
-        slot_rows = lax.dynamic_slice(down_weight, (128 * z, 0), (128, cols))
-        gram_rows = jnp.transpose(slot_rows)
+        summed = gathered(gate(piece, (y_rows[1], y_rows[3])), ("c", "x"))
+        proj = summed[:, : 4 * HEAD].reshape(8, 4, HEAD, 128)
+        proj = jnp.swapaxes(proj, 1, 2).reshape(width, 4 * HEAD)
+        second = jnp.swapaxes(summed[:, 4 * HEAD :], 0, 1).reshape(-1, width)
+        second = lax.all_gather(second, ("z",), axis=0)
+
+    with jax.named_scope("project"):
         half = 3 * HEAD
-        from_rows, from_lift = [], []
-        for k in range(2):
-            for w in (query_here, keyval_here[:, 0], keyval_here[:, 1]):
-                w = w[:, k * HEAD : (k + 1) * HEAD]
-                from_rows.append((w.astype(f32) * gain).astype(bf16))
-            from_rows.append(gram_rows)
-            direct = lax.dynamic_slice(slot_rows, (64 * yh + 32 * k, 0), (32, cols))
-            from_lift.append(jnp.transpose(out_here[k * HEAD : (k + 1) * HEAD]))
-            from_lift.append(jnp.transpose(direct))
-        from_rows = jnp.concatenate(from_rows, 1)
-        from_lift = jnp.concatenate(from_lift, 1)
-        down, flipped = gate((down_weight, jnp.transpose(up_weight)), z_rows)
-
-        def products(core):
-            start = core * (width // 2)
-            one = lax.dynamic_slice(down, (start, 0), (width // 2, cols))
-            two = lax.dynamic_slice(flipped, (start, 0), (width // 2, cols))
-            return dot(one, from_rows), dot(two, from_lift)
-
-        sent = [v.astype(bf16) for v in products(1 - c)]
-        both = [v + rotated(w, "c", 1).astype(f32) for v, w in zip(products(c), sent)]
-        pieces = [jnp.swapaxes(v.astype(bf16).reshape(4, 128, 2, -1), 1, 2) for v in both]
-        pieces = jnp.concatenate(pieces, 3).reshape(8, 128, -1)
-        piece = jnp.sum(exchanged(pieces, ("x", "yl")).astype(f32), axis=0).astype(bf16)
-        piece = gate(piece, (y_rows[1], y_rows[3]))
-        summed = gathered(piece, ("c", "x")).reshape(width, -1)
-        proj = summed[:, : 4 * HEAD]
-        second = lax.all_gather(jnp.transpose(summed[:, 4 * HEAD :]), ("yh", "yl"), axis=0)
-
-    with jax.named_scope("project"):
         qkv = dot(all_rows, proj)
+
+        def in_order(parts):
+            twice = jnp.concatenate([parts, parts[:3]], 0)
+            return lax.dynamic_slice_in_dim(twice, (4 - y) % 4, 4, 0)
+
+        def by_row(values):
+            parts = in_order(values.reshape(4, 8, run_count, -1))
+            return jnp.swapaxes(parts.reshape(2, 2, 8, run_count, -1), 1, 2).reshape(n, -1)
+
+        kv = by_row(qkv[:, HEAD:half].astype(bf16))
+        near = [kv] + [rotated(kv, "x", by) for by in (3, 2, 1)]
         slot = lax.dynamic_slice(all_rows, (0, 128 * z), (n, 128))
         squares = jnp.sum(qkv[:, half:] * slot.astype(f32), axis=-1)
         squares = jnp.sum(gathered(squares[None], ("z",)), axis=(0, 1))
-        inverse = lax.rsqrt(jnp.maximum(squares, 0.0) / wide + epsilon)
-
-        def by_row(values):
-            parts = values.reshape(4, 8, run_count, -1)
-            twice = jnp.concatenate([parts, parts[:3]], 0)
-            parts = lax.dynamic_slice_in_dim(twice, (4 - y) % 4, 4, 0)
-            return jnp.swapaxes(parts.reshape(2, 2, 8, run_count, -1), 1, 2).reshape(n, -1)
-
-        kv = by_row(qkv[:, HEAD:half].astype(bf16))
-        inverse = by_row(inverse)
+        inverse = by_row(lax.rsqrt(jnp.maximum(squares, 0.0) / wide + epsilon))
         factor = math.log2(math.e) / math.sqrt(HEAD)
         q = (by_row(qkv[:, :HEAD]) * (inverse * factor)).astype(bf16)
-        near = around_four(kv, ("x",))
-        every_inverse = gate(inverse.reshape(1, n), (near[1], near[3]))
-        every_inverse = gathered(every_inverse, ("x", "c")).reshape(4, 2, n, 1)
+        every_inverse = gathered(inverse.reshape(1, n), ("x", "c")).reshape(4, 2, n)
 
     with jax.named_scope("attention"):
-        chunks, places = [], []
+        chunks, places, scales = [], [], []
         for by in (0, 1, 3, 2):
             mine = near[by]
             other = rotated(mine, "c", 1)
             source = (x + by) % 4
             shift = 128 * (source - x)
             for chunk, core, place in ((mine, c, shift), (other, 1 - c, shift + 32 * (1 - 2 * c))):
-                scale = lax.dynamic_slice(every_inverse, (source, core, 0, 0), (1, 1, n, 1))
-                chunks.append((chunk.astype(f32) * scale.reshape(n, 1)).astype(bf16))
+                scales.append(lax.dynamic_slice(every_inverse, (source, core, 0), (1, 1, n))[0])
+                chunks.append(chunk)
                 places.append(place)
-        heads = coarse_attention(q, chunks, jnp.stack(places).astype(jnp.int32))
+        places = jnp.stack(places).astype(jnp.int32)
+        heads = coarse_attention(q, jnp.concatenate(scales, 0), chunks, places)
 
     with jax.named_scope("lift"):
-        heads = jnp.swapaxes(heads.reshape(2, 8, 2, run_count, HEAD), 1, 2)
-        heads = heads.reshape(4, z_count, HEAD)
-        total = None
-        for by in range(4):
-            part = lax.dynamic_index_in_dim(heads, (y + by) % 4, 0, keepdims=False)
-            if by:
-                part = rotated(part, ("yh", "yl"), by)
-            matrix = lax.dynamic_index_in_dim(second, (y + 4 - by) % 4, 0, keepdims=False)
-            product = dot(part, matrix[:HEAD])
-            total = product if total is None else total + product
-        slot = lax.dynamic_slice(z_rows, (0, 128 * z), (z_count, 128))
-        total = total + dot(slot, second[:, HEAD:].reshape(128, width))
-        lifted = exchanged(total.astype(bf16).reshape(8, run_count, width), ("z",))
-        lifted = jnp.sum(lifted.astype(f32), axis=0)
+        heads = jnp.transpose(heads.reshape(2, 8, 2, run_count, HEAD), (1, 0, 2, 3, 4))
+        heads = exchanged(heads.reshape(8, 4 * run_count, HEAD), ("z",))
+        heads = jnp.swapaxes(heads, 0, 1).reshape(4 * run_count, 8 * HEAD)
+        rows = lax.dynamic_slice(
+            all_rows.reshape(4, 8, run_count, width), (0, z, 0, 256 * y), (4, 1, run_count, 256)
+        )
+        rows = in_order(rows.reshape(4, run_count, 256)).reshape(4 * run_count, 256)
+        after = second[:, :HEAD].reshape(8 * HEAD, width)
+        direct = second[:, HEAD:].reshape(256, width)
+        total = (dot(heads, after) + dot(rows, direct)).reshape(4, run_count, width)
+        lifted = lax.dynamic_index_in_dim(total, y, 0, keepdims=False)
+        for by in (1, 2, 3):
+            part = lax.dynamic_index_in_dim(total, (y + by) % 4, 0, keepdims=False).astype(bf16)
+            lifted = lifted + rotated(part, ("yh", "yl"), by).astype(f32)
         before = from_behind(lifted[run_count - 1 :], ALL, 1)
         lifted = jnp.concatenate([before, lifted[: run_count - 1]], 0)
         result = fine_state.astype(f32) + jnp.repeat(lifted, SHORT, axis=0)

time: 258 us -> 271 us (1.050)
  blocking collectives: 19.8 us -> 58.2 us
  starting transfers between devices: 69.1 us -> 47.6 us
  matrix products: 27.1 us -> 18.7 us
  local copies, waits for them, and re-layouts: 24.4 us -> 29.8 us
  Pallas kernels: 12.9 us -> 16.7 us
  waiting for transfers between devices: 70.1 us -> 67 us
    all_to_all x1 -> x2, blocking collectives: 19.8 us -> 58.2 us  [gathered(): return lax.all_to_all(copies, axes, split_axis=0, concat_axis=0, tiled=True)]
    all_to_all x4 -> x2, starting transfers between devices: 28 us -> 6.97 us  [gathered(): return lax.all_to_all(copies, axes, split_axis=0, concat_axis=0, tiled=True)]
    all_to_all x4 -> x2, waiting for transfers between devices: 23.9 us -> 6.06 us  [gathered(): return lax.all_to_all(copies, axes, split_axis=0, concat_axis=0, tiled=True)]
    all_to_all x1 -> x2, waiting for transfers between devices: 18.1 us -> 29.8 us  [exchanged(): return lax.all_to_all(pieces, axes, split_axis=0, concat_axis=0, tiled=True)]
    ppermute x3 -> x1, starting transfers between devices: 14.4 us -> 4.69 us  [body(): pack = lax.ppermute(jnp.concatenate(sent, 0), ALL, swap)]
    dot_general x14 -> x7, matrix products: 24.2 us -> 15.9 us  [dot(): return jnp.dot(a, b, preferred_element_type=f32)]
    all_to_all x1 -> x2, starting transfers between devices: 3.57 us -> 11 us  [exchanged(): return lax.all_to_all(pieces, axes, split_axis=0, concat_axis=0, tiled=True)]
    slice x4 -> x8, local copies, waits for them, and re-layouts: 1.12 us -> 4.34 us  [the longest x4 1.7 us: in_order(): twice = jnp.concatenate([parts, parts[:3]], 0)]
  transfers between devices with their start and end apart: 28 -> 24, of which waited for: 13 -> 13; matrix products, arithmetic and copies ran while one was open for 20% -> 19% of each run, Pallas kernels for 5% -> 6%
where the time goes in v4:
time: 271 us; the launch traced here: 269 us
  waiting for transfers between devices  67 us (25%)
  blocking collectives  58.2 us (21%)
  starting transfers between devices  47.6 us (18%)
  local copies, waits for them, and re-layouts  29.8 us (11%)
  matrix products  18.7 us (7%)
  other arithmetic  17.1 us (6%)
  Pallas kernels  16.7 us (6%)
  between operations  14 us (5%)
    all_to_all x2, blocking collectives, gathered(): return lax.all_to_all(copies, axes, split_axis=0, concat_axis=0, tiled=True)  58.2 us
    all_to_all x2, waiting for transfers between devices, exchanged(): return lax.all_to_all(pieces, axes, split_axis=0, concat_axis=0, tiled=True)  29.8 us
    ppermute x16, waiting for transfers between devices, rotated(): lax.ppermute(array, axis, [(i, (i + by) % size) for i in range(size)])  23.9 us
    ppermute x16, starting transfers between devices, rotated(): lax.ppermute(array, axis, [(i, (i + by) % size) for i in range(size)])  21.1 us
    dot_general x7, matrix products, dot(): return jnp.dot(a, b, preferred_element_type=f32)  15.9 us
    pallas_call x1, Pallas kernels, coarse_attention(): pl.pallas_call(attention_kernel, out_shape=jax.ShapeDtypeStruct((rows, HE...  15.1 us
    all_to_all x2, starting transfers between devices, exchanged(): return lax.all_to_all(pieces, axes, split_axis=0, concat_axis=0, tiled=True)  11 us
    unnamed x32, local copies, waits for them, and re-layouts  8.83 us
  transfers between devices with their start and end apart: 24, of which 13 were waited for; matrix products, arithmetic and copies ran while one was open for 19% of the time, Pallas kernels for 6%

profile of v4, /device:TPU:16, one launch (start us, length us, event | category | flops | bytes accessed | tf_op | source)
XLA Modules:
  0.0 269.1 jit_solution(9638045058290882045)
XLA Ops:
  6.5 1.4 fusion.25
  7.9 1.2 fusion.27
  9.2 1.9 collective-permute-start
  11.1 1.6 fusion.66
  12.7 0.9 constant_dynamic-slice_fusion.8
  14.5 4.7 %collective-permute-start.1 = (bf16[1024,256]{1,0:T(8,128)(2,1)}, bf16[1024,256]{1,0:T(8,128)(2,1)S(1)}, u32[]{:S(2)}, u32[]{:S(2)}) collective-permute-start(bf16[1024,256]{1,0:T(8,128)(2,1)} %pad_maximum_fusion.1), channel_id=1, source_target_pairs={{0,0},{16,1},{32,2},{48,3},{64,4},{80,5},{96,6},{112,7},{128,8},{1... | collective-permute-start | bytes 1572872 | tf_op jit(solution)/shard_map/weights/ppermute | solution.py:236
  19.2 3.1 %fusion.19 = bf16[32,8,8,128]{3,2,1,0:T(8,128)(2,1)} fusion(bf16[256,1024]{1,0:T(8,128)(2,1)S(1)} %fusion.27, bf16[1024,1024]{1,0:T(8,128)(2,1)} %param.13), kind=kOutput, calls=%fused_computation.27 | convolution fusion | flops 537133056 | bytes 3145728 | tf_op jit(solution)/shard_map/dot_general | solution.py:58
  23.5 3.6 %convolution_convert_fusion = bf16[256,2048]{1,0:T(8,128)(2,1)S(1)} fusion(bf16[256,1024]{1,0:T(8,128)(2,1)S(1)} %fusion.27, bf16[1024,2048]{1,0:T(8,128)(2,1)} %param.14), kind=kOutput, calls=%fused_computation.6 | convolution fusion | flops 1074266112 | bytes 5767168 | tf_op jit(solution)/shard_map/dot_general | solution.py:58
  27.2 2.3 convolution_convert_fusion.1
  29.5 1.5 fusion.35
  31.1 2.3 copy.88
  33.4 1.9 fusion.32
  35.3 2.5 fusion.67
  38.9 1.7 fusion.23
  40.7 1.6 weights.1
  42.3 1.6 collective-permute-start.2
  43.9 2.8 %collective-permute-done.2 = bf16[4,2,672,128]{3,2,1,0:T(8,128)(2,1)S(1)} collective-permute-done((bf16[4,2,672,128]{3,2,1,0:T(8,128)(2,1)S(1)}, bf16[4,2,672,128]{3,2,1,0:T(8,128)(2,1)S(1)}, u32[]{:S(2)}, u32[]{:S(2)}) %collective-permute-start.2) | collective-permute-done | bytes 1376288 | tf_op jit(solution)/shard_map/weights/ppermute | solution.py:33
  46.6 1.5 add_convert_fusion
  48.1 7.6 %all-to-all-start = ((bf16[4,2,672,128]{3,2,1,0:T(8,128)(2,1)}), bf16[4,2,672,128]{3,2,1,0:T(8,128)(2,1)S(1)}, u32[]{:S(2)}, u32[]{:S(2)}) async-start(bf16[4,2,672,128]{3,2,1,0:T(8,128)(2,1)} %add_convert_fusion), calls=%async_computation | async-start | bytes 2752512 | tf_op jit(solution)/shard_map/weights/all_to_all | solution.py:49
  55.7 19.2 %all-to-all-done = bf16[4,2,672,128]{3,2,1,0:T(8,128)(2,1)S(1)} async-done(((bf16[4,2,672,128]{3,2,1,0:T(8,128)(2,1)}), bf16[4,2,672,128]{3,2,1,0:T(8,128)(2,1)S(1)}, u32[]{:S(2)}, u32[]{:S(2)}) %all-to-all-start) | async-done | bytes 1376288 | tf_op jit(solution)/shard_map/weights/all_to_all | solution.py:49
  76.0 36.5 %all_to_all.30 = bf16[8,32,1024]{2,1,0:T(8,128)(2,1)S(1)} all-to-all(bf16[8,32,1024]{2,1,0:T(8,128)(2,1)S(1)} %broadcast_in_dim.49), channel_id=1, replica_groups=mesh['yh'=2,'z'=8,'x'=4,'yl'=2,'c'=2] {'z'}, dimensions={0} | all-to-all | bytes 1048576 | tf_op jit(solution)/shard_map/gather_rows/all_to_all | solution.py:45
  112.6 1.4 collective-permute-start.3
  114.0 2.7 %collective-permute-start.5 = (bf16[256,1024]{1,0:T(8,128)(2,1)S(1)}, bf16[256,1024]{1,0:T(8,128)(2,1)S(1)}, u32[]{:S(2)}, u32[]{:S(2)}) collective-permute-start(bf16[256,1024]{1,0:T(8,128)(2,1)S(1)} %bitcast.152), channel_id=1, source_target_pairs={{0,2},{2,128},{128,130},{130,0},{1,3},{3,129},{129,131},{131,1},{4... | collective-permute-start | bytes 1572872 | tf_op jit(solution)/shard_map/gather_rows/ppermute | solution.py:33
  116.7 3.2 %collective-permute-start.7 = (bf16[672,128]{1,0:T(8,128)(2,1)S(1)}, bf16[672,128]{1,0:T(8,128)(2,1)S(1)}, u32[]{:S(2)}, u32[]{:S(2)}) collective-permute-start(bf16[672,128]{1,0:T(8,128)(2,1)S(1)} %fusion.48), channel_id=1, source_target_pairs={{0,2},{2,0},{1,3},{3,1},{4,6},{6,4},{5,7},{7,5},{8,10},{10,8},{9,1... | collective-permute-start | bytes 516104 | tf_op jit(solution)/shard_map/weights/ppermute | solution.py:33
  119.9 10.2 %collective-permute-done.7 = bf16[672,128]{1,0:T(8,128)(2,1)S(1)} collective-permute-done((bf16[672,128]{1,0:T(8,128)(2,1)S(1)}, bf16[672,128]{1,0:T(8,128)(2,1)S(1)}, u32[]{:S(2)}, u32[]{:S(2)}) %collective-permute-start.7) | collective-permute-done | bytes 172064 | tf_op jit(solution)/shard_map/weights/ppermute | solution.py:33
  130.2 1.0 fusion.46
  132.2 21.6 %all_to_all.31 = bf16[8,672,128]{2,1,0:T(8,128)(2,1)S(1)} all-to-all(bf16[8,672,128]{2,1,0:T(8,128)(2,1)S(1)} %broadcast_in_dim.50), channel_id=1, replica_groups=mesh['yh'=2,'z'=8,'x'=4,'yl'=2,'c'=2] {'c','x'}, dimensions={0} | all-to-all | bytes 2752512 | tf_op jit(solution)/shard_map/weights/all_to_all | solution.py:45
  153.8 0.9 copy.87
  154.7 1.9 reshape.205
  156.6 1.7 slice.99
  158.3 2.4 collective-permute-start.4
  160.7 1.0 slice.100
  161.9 1.9 constant_dynamic-update-slice_fusion.4
  163.7 1.9 constant_dynamic-update-slice_fusion.3
  165.7 1.3 collective-permute-done.4
  166.9 1.7 constant_dynamic-update-slice_fusion.2
  168.6 1.3 collective-permute-done.6
  171.5 1.1 slice.101
  172.6 1.7 copy.81
  174.2 2.9 %fusion.68 = (bf16[1024,512]{1,0:T(8,128)(2,1)S(1)}, f32[1024,512]{1,0:T(8,128)S(1)}) fusion(bf16[1024,1024]{1,0:T(8,128)(2,1)} %constant_dynamic-update-slice_fusion, bf16[64,8,8,128]{3,2,1,0:T(8,128)(2,1)S(1)} %bitcast.163), kind=kOutput, calls=%fused_computation.121 | convolution fusion | flops 1074266112 | bytes 6291456 | tf_op jit(solution)/shard_map/project/dot_general | solution.py:58
  177.6 1.1 collective-permute-start.9
  178.7 1.0 collective-permute-start.11
  179.7 1.2 collective-permute-start.13
  181.6 2.0 fusion.40
  184.2 3.3 %all-to-all-start.3 = ((f32[8,1,1024]{2,1,0:T(1,128)}), f32[8,1,1024]{2,1,0:T(1,128)S(1)}, u32[]{:S(2)}, u32[]{:S(2)}) async-start(f32[8,1,1024]{2,1,0:T(1,128)} %broadcast_in_dim.51), calls=%async_computation.3 | async-start | bytes 65536 | tf_op jit(solution)/shard_map/project/all_to_all | solution.py:45
  187.5 1.1 fusion.37
  188.7 0.9 copy.82
  189.6 6.1 %all-to-all-done.3 = f32[8,1,1024]{2,1,0:T(1,128)S(1)} async-done(((f32[8,1,1024]{2,1,0:T(1,128)}), f32[8,1,1024]{2,1,0:T(1,128)S(1)}, u32[]{:S(2)}, u32[]{:S(2)}) %all-to-all-start.3) | async-done | bytes 32800 | tf_op jit(solution)/shard_map/project/all_to_all | solution.py:45
  196.6 3.6 %all-to-all-start.4 = ((f32[8,1,1024]{2,1,0:T(1,128)}), f32[8,1,1024]{2,1,0:T(1,128)S(1)}, u32[]{:S(2)}, u32[]{:S(2)}) async-start(f32[8,1,1024]{2,1,0:T(1,128)} %broadcast_in_dim.52), calls=%async_computation.4 | async-start | bytes 65536 | tf_op jit(solution)/shard_map/project/all_to_all | solution.py:45
  200.7 4.7 %collective-permute-done.11.refs_4_ = bf16[1024,256]{1,0:T(8,128)(2,1)} collective-permute-done((bf16[1024,256]{1,0:T(8,128)(2,1)S(1)}, bf16[1024,256]{1,0:T(8,128)(2,1)}, u32[]{:S(2)}, u32[]{:S(2)}) %collective-permute-start.11) | collective-permute-done | bytes 524320 | tf_op jit(solution)/shard_map/project/ppermute | solution.py:33
  205.9 1.2 fusion.41.q_ref
  208.4 15.1 %attention.1 = bf16[1024,128]{1,0:T(8,128)(2,1)S(1)} custom-call(s32[8]{0:T(128)S(1)} %stack.50.place_ref, bf16[1024,128]{1,0:T(8,128)(2,1)S(1)} %fusion.41.q_ref, f32[8,1024]{1,0:T(8,128)S(1)} %concatenate.32.inverse_ref, bf16[1024,256]{1,0:T(8,128)(2,1)S(1)} %bitcast.147, bf16[1024,256]{1,0:T(8,128)(2,1)S(1)} %collective-permute-done.8.refs_1_, ...), custom_call_target="tpu_custom_call" | custom-call | tf_op jit(solution)/shard_map/attention/pallas_call | solution.py:144
  224.2 3.4 %all-to-all-start.5 = ((bf16[8,128,128]{2,1,0:T(8,128)(2,1)}), bf16[8,128,128]{2,1,0:T(8,128)(2,1)S(1)}, u32[]{:S(2)}, u32[]{:S(2)}) async-start(bf16[8,128,128]{2,1,0:T(8,128)(2,1)} %bitcast.47), calls=%async_computation.5 | async-start | bytes 524288 | tf_op jit(solution)/shard_map/lift/all_to_all | solution.py:49
  229.4 10.6 %all-to-all-done.5 = bf16[8,128,128]{2,1,0:T(8,128)(2,1)S(1)} async-done(((bf16[8,128,128]{2,1,0:T(8,128)(2,1)}), bf16[8,128,128]{2,1,0:T(8,128)(2,1)S(1)}, u32[]{:S(2)}, u32[]{:S(2)}) %all-to-all-start.5) | async-done | bytes 262176 | tf_op jit(solution)/shard_map/lift/all_to_all | solution.py:49
  240.0 2.0 fusion.20
  243.1 1.2 collective-permute-start.17
  244.3 2.7 collective-permute-start.16
  247.0 1.6 collective-permute-start.15
  248.5 1.8 collective-permute-done.16
  250.3 0.9 collective-permute-done.15
  251.2 0.9 fusion.50
  252.2 1.9 collective-permute-start.18
  254.1 7.2 %collective-permute-done.18 = f32[1,1024]{1,0:T(1,128)S(1)} collective-permute-done((f32[1,1024]{1,0:T(1,128)S(1)}, f32[1,1024]{1,0:T(1,128)S(1)}, u32[]{:S(2)}, u32[]{:S(2)}) %collective-permute-start.18) | collective-permute-done | bytes 4128 | tf_op jit(solution)/shard_map/lift/ppermute | solution.py:28
  261.4 0.9 fusion.24
  (96 shorter events, 15.5 us)
Async XLA Ops:
  6.5 32.2 %copy-start = (bf16[1024,1024]{1,0:T(8,128)(2,1)S(1)}, bf16[1024,1024]{1,0:T(8,128)(2,1)}, u32[]{:S(2)}) copy-start(bf16[1024,1024]{1,0:T(8,128)(2,1)} %param.15) | copy-start | bytes 6291460
  6.5 7.1 %copy-start.12 = (bf16[256,256]{1,0:T(8,128)(2,1)S(1)}, bf16[256,256]{1,0:T(8,128)(2,1)}, u32[]{:S(2)}) copy-start(bf16[256,256]{1,0:T(8,128)(2,1)} %param.18) | copy-start | bytes 393220
  9.2 18.0 %collective-permute-start = (bf16[256,1024]{1,0:T(8,128)(2,1)S(1)}, bf16[256,1024]{1,0:T(8,128)(2,1)}, u32[]{:S(2)}, u32[]{:S(2)}) collective-permute-start(bf16[256,1024]{1,0:T(8,128)(2,1)S(1)} %fusion.27), channel_id=1, source_target_pairs={{0,1},{1,2},{2,3},{3,4},{4,5},{5,6},{6,7},{7,8},{8,9},{9,10},{10,1... | collective-permute-start | bytes 1572872 | tf_op jit(solution)/shard_map/ppermute | solution.py:28
  14.5 26.1 %collective-permute-start.1 = (bf16[1024,256]{1,0:T(8,128)(2,1)}, bf16[1024,256]{1,0:T(8,128)(2,1)S(1)}, u32[]{:S(2)}, u32[]{:S(2)}) collective-permute-start(bf16[1024,256]{1,0:T(8,128)(2,1)} %pad_maximum_fusion.1), channel_id=1, source_target_pairs={{0,0},{16,1},{32,2},{48,3},{64,4},{80,5},{96,6},{112,7},{128,8},{1... | collective-permute-start | bytes 1572872 | tf_op jit(solution)/shard_map/weights/ppermute | solution.py:236
  23.5 3.6 %copy-start.13 = (bf16[1024,2048]{1,0:T(8,128)(2,1)S(1)}, bf16[1024,2048]{1,0:T(8,128)(2,1)}, u32[]{:S(2)}) copy-start(bf16[1024,2048]{1,0:T(8,128)(2,1)} %param.14) | copy-start | bytes 12582916
  31.0 2.3 copy-start.11
  35.3 2.5 copy-start.10
  37.8 1.0 copy-start.3
  38.7 2.0 copy-start.1
  38.7 2.0 copy-start.2
  42.3 4.3 %collective-permute-start.2 = (bf16[4,2,672,128]{3,2,1,0:T(8,128)(2,1)S(1)}, bf16[4,2,672,128]{3,2,1,0:T(8,128)(2,1)S(1)}, u32[]{:S(2)}, u32[]{:S(2)}) collective-permute-start(bf16[4,2,672,128]{3,2,1,0:T(8,128)(2,1)S(1)} %get-tuple-element.12), channel_id=1, source_target_pairs={{0,1},{1,0},{2,3},{3,2},{4,5},{5,4},{6,7},{7,6},{8,9},{9,8},{10,11... | collective-permute-start | bytes 4128776 | tf_op jit(solution)/shard_map/weights/ppermute | solution.py:33
  48.1 26.8 %all-to-all-start = ((bf16[4,2,672,128]{3,2,1,0:T(8,128)(2,1)}), bf16[4,2,672,128]{3,2,1,0:T(8,128)(2,1)S(1)}, u32[]{:S(2)}, u32[]{:S(2)}) async-start(bf16[4,2,672,128]{3,2,1,0:T(8,128)(2,1)} %add_convert_fusion), calls=%async_computation | async-start | bytes 2752512 | tf_op jit(solution)/shard_map/weights/all_to_all | solution.py:49
  55.7 173.7 %all-gather.2.cloned.1.call-start = ((), (), s32[]{:S(2)}) async-start(), calls=%async_computation.6 | async-start | bytes 2949120 | tf_op jit(solution)/shard_map/weights/all_gather | solution.py:265
  75.1 0.8 copy-start.4
  112.6 18.6 %copy-start.5 = (bf16[8,32,1024]{2,1,0:T(8,128)(2,1)}, bf16[8,32,1024]{2,1,0:T(8,128)(2,1)S(1)}, u32[]{:S(2)}) copy-start(bf16[8,32,1024]{2,1,0:T(8,128)(2,1)S(1)} %all_to_all.30) | copy-start | bytes 1572868
  112.6 18.6 %collective-permute-start.3 = (bf16[256,1024]{1,0:T(8,128)(2,1)S(1)}, bf16[256,1024]{1,0:T(8,128)(2,1)}, u32[]{:S(2)}, u32[]{:S(2)}) collective-permute-start(bf16[256,1024]{1,0:T(8,128)(2,1)S(1)} %bitcast.151), channel_id=1, source_target_pairs={{0,130},{2,0},{128,2},{130,128},{1,131},{3,1},{129,3},{131,129},{4... | collective-permute-start | bytes 1572872 | tf_op jit(solution)/shard_map/gather_rows/ppermute | solution.py:33
  114.0 17.2 %collective-permute-start.5 = (bf16[256,1024]{1,0:T(8,128)(2,1)S(1)}, bf16[256,1024]{1,0:T(8,128)(2,1)S(1)}, u32[]{:S(2)}, u32[]{:S(2)}) collective-permute-start(bf16[256,1024]{1,0:T(8,128)(2,1)S(1)} %bitcast.152), channel_id=1, source_target_pairs={{0,2},{2,128},{128,130},{130,0},{1,3},{3,129},{129,131},{131,1},{4... | collective-permute-start | bytes 1572872 | tf_op jit(solution)/shard_map/gather_rows/ppermute | solution.py:33
  116.7 13.4 %collective-permute-start.7 = (bf16[672,128]{1,0:T(8,128)(2,1)S(1)}, bf16[672,128]{1,0:T(8,128)(2,1)S(1)}, u32[]{:S(2)}, u32[]{:S(2)}) collective-permute-start(bf16[672,128]{1,0:T(8,128)(2,1)S(1)} %fusion.48), channel_id=1, source_target_pairs={{0,2},{2,0},{1,3},{3,1},{4,6},{6,4},{5,7},{7,5},{8,10},{10,8},{9,1... | collective-permute-start | bytes 516104 | tf_op jit(solution)/shard_map/weights/ppermute | solution.py:33
  131.2 0.8 copy-start.8
  158.3 8.6 %collective-permute-start.4 = (bf16[128,1024]{1,0:T(8,128)(2,1)}, bf16[128,1024]{1,0:T(8,128)(2,1)}, u32[]{:S(2)}, u32[]{:S(2)}) collective-permute-start(bf16[128,1024]{1,0:T(8,128)(2,1)} %slice.99), channel_id=1, source_target_pairs={{0,130},{2,0},{128,2},{130,128},{1,131},{3,1},{129,3},{131,129},{4... | collective-permute-start | bytes 786440 | tf_op jit(solution)/shard_map/gather_rows/ppermute | solution.py:33
  160.7 9.9 %copy-start.9 = (bf16[256,1024]{1,0:T(8,128)(2,1)S(1)}, bf16[256,1024]{1,0:T(8,128)(2,1)}, u32[]{:S(2)}) copy-start(bf16[256,1024]{1,0:T(8,128)(2,1)} %copy-done.8) | copy-start | bytes 1572868
  161.8 8.1 %collective-permute-start.6 = (bf16[128,1024]{1,0:T(8,128)(2,1)S(1)}, bf16[128,1024]{1,0:T(8,128)(2,1)S(1)}, u32[]{:S(2)}, u32[]{:S(2)}) collective-permute-start(bf16[128,1024]{1,0:T(8,128)(2,1)S(1)} %slice.100), channel_id=1, source_target_pairs={{0,2},{2,128},{128,130},{130,0},{1,3},{3,129},{129,131},{131,1},{4... | collective-permute-start | bytes 786440 | tf_op jit(solution)/shard_map/gather_rows/ppermute | solution.py:33
  177.5 29.9 %collective-permute-start.8 = (bf16[1024,256]{1,0:T(8,128)(2,1)S(1)}, bf16[1024,256]{1,0:T(8,128)(2,1)S(1)}, u32[]{:S(2)}, u32[]{:S(2)}) collective-permute-start(bf16[1024,256]{1,0:T(8,128)(2,1)S(1)} %bitcast.143), channel_id=1, source_target_pairs={{0,1},{1,0},{2,3},{3,2},{4,5},{5,4},{6,7},{7,6},{8,9},{9,8},{10,11... | collective-permute-start | bytes 1572872 | tf_op jit(solution)/shard_map/attention/ppermute | solution.py:33
  177.6 22.7 %collective-permute-start.9 = (bf16[1024,256]{1,0:T(8,128)(2,1)S(1)}, bf16[1024,256]{1,0:T(8,128)(2,1)}, u32[]{:S(2)}, u32[]{:S(2)}) collective-permute-start(bf16[1024,256]{1,0:T(8,128)(2,1)S(1)} %bitcast.144), channel_id=1, source_target_pairs={{0,12},{4,0},{8,4},{12,8},{1,13},{5,1},{9,5},{13,9},{2,14},{6,2},{... | collective-permute-start | bytes 1572872 | tf_op jit(solution)/shard_map/project/ppermute | solution.py:33
  178.7 26.7 %collective-permute-start.11 = (bf16[1024,256]{1,0:T(8,128)(2,1)S(1)}, bf16[1024,256]{1,0:T(8,128)(2,1)}, u32[]{:S(2)}, u32[]{:S(2)}) collective-permute-start(bf16[1024,256]{1,0:T(8,128)(2,1)S(1)} %bitcast.145), channel_id=1, source_target_pairs={{0,4},{4,8},{8,12},{12,0},{1,5},{5,9},{9,13},{13,1},{2,6},{6,10},{... | collective-permute-start | bytes 1572872 | tf_op jit(solution)/shard_map/project/ppermute | solution.py:33
  179.7 25.7 %collective-permute-start.13 = (bf16[1024,256]{1,0:T(8,128)(2,1)S(1)}, bf16[1024,256]{1,0:T(8,128)(2,1)}, u32[]{:S(2)}, u32[]{:S(2)}) collective-permute-start(bf16[1024,256]{1,0:T(8,128)(2,1)S(1)} %bitcast.146), channel_id=1, source_target_pairs={{0,8},{4,12},{8,0},{12,4},{1,9},{5,13},{9,1},{13,5},{2,10},{6,14},... | collective-permute-start | bytes 1572872 | tf_op jit(solution)/shard_map/project/ppermute | solution.py:33
  184.2 11.4 %all-to-all-start.3 = ((f32[8,1,1024]{2,1,0:T(1,128)}), f32[8,1,1024]{2,1,0:T(1,128)S(1)}, u32[]{:S(2)}, u32[]{:S(2)}) async-start(f32[8,1,1024]{2,1,0:T(1,128)} %broadcast_in_dim.51), calls=%async_computation.3 | async-start | bytes 65536 | tf_op jit(solution)/shard_map/project/all_to_all | solution.py:45
  196.6 10.6 %all-to-all-start.4 = ((f32[8,1,1024]{2,1,0:T(1,128)}), f32[8,1,1024]{2,1,0:T(1,128)S(1)}, u32[]{:S(2)}, u32[]{:S(2)}) async-start(f32[8,1,1024]{2,1,0:T(1,128)} %broadcast_in_dim.52), calls=%async_computation.4 | async-start | bytes 65536 | tf_op jit(solution)/shard_map/project/all_to_all | solution.py:45
  200.2 7.2 %collective-permute-start.10 = (bf16[1024,256]{1,0:T(8,128)(2,1)}, bf16[1024,256]{1,0:T(8,128)(2,1)}, u32[]{:S(2)}, u32[]{:S(2)}) collective-permute-start(bf16[1024,256]{1,0:T(8,128)(2,1)} %collective-permute-done.9.refs_2_), channel_id=1, source_target_pairs={{0,1},{1,0},{2,3},{3,2},{4,5},{5,4},{6,7},{7,6},{8,9},{9,8},{10,11... | collective-permute-start | bytes 1572872 | tf_op jit(solution)/shard_map/attention/ppermute | solution.py:33
  205.4 2.3 collective-permute-start.12
  205.4 3.0 %collective-permute-start.14 = (bf16[1024,256]{1,0:T(8,128)(2,1)}, bf16[1024,256]{1,0:T(8,128)(2,1)}, u32[]{:S(2)}, u32[]{:S(2)}) collective-permute-start(bf16[1024,256]{1,0:T(8,128)(2,1)} %collective-permute-done.13.refs_6_), channel_id=1, source_target_pairs={{0,1},{1,0},{2,3},{3,2},{4,5},{5,4},{6,7},{7,6},{8,9},{9,8},{10,11... | collective-permute-start | bytes 1572872 | tf_op jit(solution)/shard_map/attention/ppermute | solution.py:33
  224.2 15.8 %all-to-all-start.5 = ((bf16[8,128,128]{2,1,0:T(8,128)(2,1)}), bf16[8,128,128]{2,1,0:T(8,128)(2,1)S(1)}, u32[]{:S(2)}, u32[]{:S(2)}) async-start(bf16[8,128,128]{2,1,0:T(8,128)(2,1)} %bitcast.47), calls=%async_computation.5 | async-start | bytes 524288 | tf_op jit(solution)/shard_map/lift/all_to_all | solution.py:49
  229.4 12.6 %slice-start = ((bf16[8,160,1024]{2,1,0:T(8,128)(2,1)}), bf16[8,32,1024]{2,1,0:T(8,128)(2,1)S(1)}, s32[]{:S(2)}) async-start(bf16[8,160,1024]{2,1,0:T(8,128)(2,1)} %all-gather.2.cloned.1.call-done), calls=%async_computation.7 | async-start | bytes 1048576 | tf_op jit(solution)/shard_map/lift/slice | solution.py:312
  242.0 19.3 %copy-start.6 = (bf16[256,1024]{1,0:T(8,128)(2,1)S(1)}, bf16[256,1024]{1,0:T(8,128)(2,1)}, u32[]{:S(2)}) copy-start(bf16[256,1024]{1,0:T(8,128)(2,1)} %get-tuple-element.35) | copy-start | bytes 1572868
  242.3 0.8 copy-start.7
  243.1 5.4 %collective-permute-start.17 = (bf16[32,1024]{1,0:T(8,128)(2,1)S(1)}, bf16[32,1024]{1,0:T(8,128)(2,1)S(1)}, u32[]{:S(2)}, u32[]{:S(2)}) collective-permute-start(bf16[32,1024]{1,0:T(8,128)(2,1)S(1)} %get-tuple-element.20), channel_id=1, source_target_pairs={{0,130},{2,0},{128,2},{130,128},{1,131},{3,1},{129,3},{131,129},{4... | collective-permute-start | bytes 196616 | tf_op jit(solution)/shard_map/lift/ppermute | solution.py:33
  244.3 6.0 %collective-permute-start.16 = (bf16[32,1024]{1,0:T(8,128)(2,1)S(1)}, bf16[32,1024]{1,0:T(8,128)(2,1)S(1)}, u32[]{:S(2)}, u32[]{:S(2)}) collective-permute-start(bf16[32,1024]{1,0:T(8,128)(2,1)S(1)} %get-tuple-element.21), channel_id=1, source_target_pairs={{0,128},{2,130},{128,0},{130,2},{1,129},{3,131},{129,1},{131,3},{4... | collective-permute-start | bytes 196616 | tf_op jit(solution)/shard_map/lift/ppermute | solution.py:33
  247.0 4.3 %collective-permute-start.15 = (bf16[32,1024]{1,0:T(8,128)(2,1)S(1)}, bf16[32,1024]{1,0:T(8,128)(2,1)S(1)}, u32[]{:S(2)}, u32[]{:S(2)}) collective-permute-start(bf16[32,1024]{1,0:T(8,128)(2,1)S(1)} %get-tuple-element.19), channel_id=1, source_target_pairs={{0,2},{2,128},{128,130},{130,0},{1,3},{3,129},{129,131},{131,1},{4... | collective-permute-start | bytes 196616 | tf_op jit(solution)/shard_map/lift/ppermute | solution.py:33
  252.2 9.1 %collective-permute-start.18 = (f32[1,1024]{1,0:T(1,128)S(1)}, f32[1,1024]{1,0:T(1,128)S(1)}, u32[]{:S(2)}, u32[]{:S(2)}) collective-permute-start(f32[1,1024]{1,0:T(1,128)S(1)} %slice.110), channel_id=1, source_target_pairs={{0,1},{1,2},{2,3},{3,4},{4,5},{5,6},{6,7},{7,8},{8,9},{9,10},{10,1... | collective-permute-start | bytes 12296 | tf_op jit(solution)/shard_map/lift/ppermute | solution.py:28
Sparse Core Ops, SparseCore 0:
  156.7 38.7 all-gather.1

commit v5 on v4

--- a/solution.py
+++ b/solution.py
@@ -37,7 +37,7 @@
     above, below = rotated(array, axes, 3), rotated(array, axes, 1)
     half = array.shape[0] // 2
     top, bottom = rotated(above[:half], axes, 3), rotated(below[half:], axes, 1)
-    return [array, above, jnp.concatenate([top, bottom], 0), below]
+    return [array, above, top, bottom, below]
 
 
 def gathered(array, axes):
@@ -162,13 +162,10 @@
     return lax.optimization_barrier((array, earlier))[0]
 
 
-def product_kernel(where_ref, down_ref, up_ref, gain_ref, pack_ref, give_ref, keep_ref):
+def product_kernel(where_ref, down_ref, up_ref, pack_ref, give_ref, keep_ref):
     core, gram_at = where_ref[0], where_ref[1]
-    gain = gain_ref[...]
     cols = pack_ref.shape[1]
-    scaled = [
-        (pack_ref[j * cols : (j + 1) * cols, :].astype(f32) * gain).astype(bf16) for j in range(3)
-    ]
+    scaled = [pack_ref[j * cols : (j + 1) * cols, :] for j in range(3)]
     gram_rows = down_ref[pl.ds(pl.multiple_of(gram_at, 128), 128), :]
     right, left = [], []
     for k in range(2):
@@ -195,17 +192,17 @@
                 out_ref[q, k, 4 * 128 :, :] = lift[:, block]
 
 
-def weight_products(where, down, up, gain, pack):
+def weight_products(where, down, up, pack):
     width = down.shape[0]
     out = jax.ShapeDtypeStruct((4, 2, 4 * 128 + HEAD + 32, width // 8), bf16)
     whole = pl.BlockSpec(memory_space=pltpu.VMEM)
     return pl.pallas_call(
         product_kernel,
         out_shape=(out, out),
-        in_specs=[pl.BlockSpec(memory_space=pltpu.SMEM)] + [whole] * 4,
+        in_specs=[pl.BlockSpec(memory_space=pltpu.SMEM)] + [whole] * 3,
         out_specs=(whole, whole),
         compiler_params=pltpu.CompilerParams(vmem_limit_bytes=40 << 20),
-    )(where, down, up, gain, pack)
+    )(where, down, up, pack)
 
 
 def body(
@@ -239,26 +236,33 @@
     run_count = tokens.shape[0] // SHORT
     pooled = jnp.mean(fine_state.astype(f32).reshape(run_count, SHORT, width), axis=1).astype(bf16)
 
+    with jax.named_scope("gather_rows"):
+        around = [pooled] + [rotated(pooled, "z", by) for by in range(7, 0, -1)]
+        around = jnp.stack(around + around[:7])
+        z_rows = lax.dynamic_slice_in_dim(around, (8 - z) % 8, 8, 0).reshape(-1, width)
+        y_rows = around_four(z_rows, ("yh", "yl"))
+        all_rows = jnp.concatenate(y_rows, 0)
+        n = all_rows.shape[0]
+
     with jax.named_scope("weights"):
         gain = lax.dynamic_slice(coarse_gain, (t * cols,), (cols,))[:, None]
         direct_at = 512 * yh + 32 * z
         where = jnp.stack([c, 128 * z, direct_at, direct_at + 256]).astype(jnp.int32)
-        give, keep = weight_products(where, down_weight, up_weight, gain, gate(pack, pooled))
+        ones = jnp.ones((cols, 1), f32)
+        pack = gate(pack, pooled).astype(f32) * jnp.concatenate([gain] * 3 + [ones], 0)
+        pack = gate(pack.astype(bf16), z_rows)
+        give, keep = weight_products(where, down_weight, up_weight, pack)
         both = keep.astype(f32) + rotated(give, "c", 1).astype(f32)
-        pieces = exchanged(both.astype(bf16), ("x",))
+        pieces = exchanged(gate(both.astype(bf16), (y_rows[1], y_rows[4])), ("x",))
         pieces = jnp.sum(pieces.astype(f32), axis=0)
         mine = lax.dynamic_index_in_dim(pieces, yl, 0, keepdims=False)
         other = lax.dynamic_index_in_dim(pieces, 1 - yl, 0, keepdims=False).astype(bf16)
         piece = (mine + rotated(other, "yl", 1).astype(f32)).astype(bf16)
-
-    with jax.named_scope("gather_rows"):
-        z_rows = gathered(gate(pooled, other), ("z",)).reshape(-1, width)
-        y_rows = around_four(z_rows, ("yh", "yl"))
-        all_rows = jnp.concatenate(y_rows, 0)
-        n = all_rows.shape[0]
-
-    with jax.named_scope("weights"):
-        summed = gathered(gate(piece, (y_rows[1], y_rows[3])), ("c", "x"))
+        near_half = gathered(gate(piece, (y_rows[2], y_rows[3])), ("x",))
+        far_half = rotated(near_half, "c", 1)
+        summed = jnp.stack(
+            [jnp.where(c == 0, near_half, far_half), jnp.where(c == 0, far_half, near_half)]
+        ).reshape(8, *piece.shape)
         proj = summed[:, : 4 * HEAD].reshape(8, 4, HEAD, 128)
         proj = jnp.swapaxes(proj, 1, 2).reshape(width, 4 * HEAD)
         second = jnp.swapaxes(summed[:, 4 * HEAD :], 0, 1).reshape(-1, width)

time: 271 us -> 276 us (1.018)
  blocking collectives: 58.2 us -> 12.7 us
  starting transfers between devices: 47.6 us -> 86 us
  waiting for transfers between devices: 67 us -> 90.7 us
  local copies, waits for them, and re-layouts: 29.8 us -> 21.2 us
    all_to_all x2 -> x1, blocking collectives: 58.2 us -> 12.7 us  [gathered(): return lax.all_to_all(copies, axes, split_axis=0, concat_axis=0, tiled=True)]
    ppermute x16 -> x24, starting transfers between devices: 21.1 us -> 60.3 us  [rotated(): lax.ppermute(array, axis, [(i, (i + by) % size) for i in range(size)])]
    ppermute x16 -> x24, waiting for transfers between devices: 23.9 us -> 36.5 us  [rotated(): lax.ppermute(array, axis, [(i, (i + by) % size) for i in range(size)])]
    ppermute x2, waiting for transfers between devices: 7.22 us -> 17.3 us  [from_behind(): return lax.ppermute(array, axis, pairs)]
    all_to_all x2, starting transfers between devices: 11 us -> 7.49 us  [exchanged(): return lax.all_to_all(pieces, axes, split_axis=0, concat_axis=0, tiled=True)]
    unnamed x32 -> x45, local copies, waits for them, and re-layouts: 8.83 us -> 5.77 us
  transfers between devices with their start and end apart: 24 -> 32, of which waited for: 13 -> 19; matrix products, arithmetic and copies ran while one was open for 19% -> 16% of each run, Pallas kernels for 6% -> 5%
where the time goes in v5:
time: 276 us; the launch traced here: 275 us
  waiting for transfers between devices  90.7 us (33%)
  starting transfers between devices  86 us (31%)
  local copies, waits for them, and re-layouts  21.2 us (8%)
  matrix products  18.8 us (7%)
  Pallas kernels  16 us (6%)
  other arithmetic  15.3 us (6%)
  between operations  14.2 us (5%)
  blocking collectives  12.7 us (5%)
    ppermute x24, starting transfers between devices, rotated(): lax.ppermute(array, axis, [(i, (i + by) % size) for i in range(size)])  60.3 us
    ppermute x24, waiting for transfers between devices, rotated(): lax.ppermute(array, axis, [(i, (i + by) % size) for i in range(size)])  36.5 us
    all_to_all x2, waiting for transfers between devices, exchanged(): return lax.all_to_all(pieces, axes, split_axis=0, concat_axis=0, tiled=True)  29.1 us
    ppermute x2, waiting for transfers between devices, from_behind(): return lax.ppermute(array, axis, pairs)  17.3 us
    dot_general x7, matrix products, dot(): return jnp.dot(a, b, preferred_element_type=f32)  16.1 us
    pallas_call x1, Pallas kernels, coarse_attention(): pl.pallas_call(attention_kernel, out_shape=jax.ShapeDtypeStruct((rows, HE...  14.4 us
    all_to_all x1, blocking collectives, gathered(): return lax.all_to_all(copies, axes, split_axis=0, concat_axis=0, tiled=True)  12.7 us
    all_to_all x2, starting transfers between devices, gathered(): return lax.all_to_all(copies, axes, split_axis=0, concat_axis=0, tiled=True)  8.24 us
  transfers between devices with their start and end apart: 32, of which 19 were waited for; matrix products, arithmetic and copies ran while one was open for 16% of the time, Pallas kernels for 5%

profile of v5, /device:TPU:16, one launch (start us, length us, event | category | flops | bytes accessed | tf_op | source)
XLA Modules:
  0.0 275.0 jit_solution(14876214653337407664)
XLA Ops:
  6.5 1.6 fusion.66
  8.2 0.9 constant_dynamic-slice_fusion.8
  10.0 4.7 %collective-permute-start.12 = (bf16[1024,256]{1,0:T(8,128)(2,1)}, bf16[1024,256]{1,0:T(8,128)(2,1)}, u32[]{:S(2)}, u32[]{:S(2)}) collective-permute-start(bf16[1024,256]{1,0:T(8,128)(2,1)} %pad_maximum_fusion.2), channel_id=1, source_target_pairs={{0,0},{16,1},{32,2},{48,3},{64,4},{80,5},{96,6},{112,7},{128,8},{1... | collective-permute-start | bytes 1572872 | tf_op jit(solution)/shard_map/weights/ppermute | solution.py:233
  15.1 3.4 %collective-permute-start = (bf16[256,1024]{1,0:T(8,128)(2,1)S(1)}, bf16[256,1024]{1,0:T(8,128)(2,1)}, u32[]{:S(2)}, u32[]{:S(2)}) collective-permute-start(bf16[256,1024]{1,0:T(8,128)(2,1)S(1)} %fusion.27), channel_id=1, source_target_pairs={{0,1},{1,2},{2,3},{3,4},{4,5},{5,6},{6,7},{7,8},{8,9},{9,10},{10,1... | collective-permute-start | bytes 1572872 | tf_op jit(solution)/shard_map/ppermute | solution.py:28
  18.5 3.1 %fusion.19 = bf16[32,8,8,128]{3,2,1,0:T(8,128)(2,1)} fusion(bf16[256,1024]{1,0:T(8,128)(2,1)S(1)} %fusion.27, bf16[1024,1024]{1,0:T(8,128)(2,1)} %param.13), kind=kOutput, calls=%fused_computation.28 | convolution fusion | flops 537133056 | bytes 3145728 | tf_op jit(solution)/shard_map/dot_general | solution.py:58
  22.7 3.6 %convolution_convert_fusion = bf16[256,2048]{1,0:T(8,128)(2,1)S(1)} fusion(bf16[256,1024]{1,0:T(8,128)(2,1)S(1)} %fusion.27, bf16[1024,2048]{1,0:T(8,128)(2,1)} %param.14), kind=kOutput, calls=%fused_computation.6 | convolution fusion | flops 1074266112 | bytes 5767168 | tf_op jit(solution)/shard_map/dot_general | solution.py:58
  26.4 10.0 %collective-permute-done = bf16[256,1024]{1,0:T(8,128)(2,1)} collective-permute-done((bf16[256,1024]{1,0:T(8,128)(2,1)S(1)}, bf16[256,1024]{1,0:T(8,128)(2,1)}, u32[]{:S(2)}, u32[]{:S(2)}) %collective-permute-start) | collective-permute-done | bytes 524320 | tf_op jit(solution)/shard_map/ppermute | solution.py:28
  36.4 2.3 convolution_convert_fusion.1
  38.7 1.6 fusion.35
  40.3 2.3 copy.84
  42.6 1.9 fusion.32
  44.6 2.5 fusion.67
  47.9 1.7 fusion.23
  49.8 2.5 collective-permute-start.6
  52.2 29.9 %collective-permute-start.5 = (bf16[32,1024]{1,0:T(8,128)(2,1)S(1)}, bf16[32,1024]{1,0:T(8,128)(2,1)S(1)}, u32[]{:S(2)}, u32[]{:S(2)}) collective-permute-start(bf16[32,1024]{1,0:T(8,128)(2,1)S(1)} %get-tuple-element.18), channel_id=1, source_target_pairs={{0,48},{16,64},{32,80},{48,96},{64,112},{80,0},{96,16},{112,32},{1... | collective-permute-start | bytes 196616 | tf_op jit(solution)/shard_map/gather_rows/ppermute | solution.py:33
  82.1 2.7 collective-permute-start.1
  84.8 1.2 multiply_convert_fusion.pack_ref
  86.7 3.3 %collective-permute-start.2 = (bf16[32,1024]{1,0:T(8,128)(2,1)S(1)}, bf16[32,1024]{1,0:T(8,128)(2,1)S(1)}, u32[]{:S(2)}, u32[]{:S(2)}) collective-permute-start(bf16[32,1024]{1,0:T(8,128)(2,1)S(1)} %get-tuple-element.18), channel_id=1, source_target_pairs={{0,96},{16,112},{32,0},{48,16},{64,32},{80,48},{96,64},{112,80},{1... | collective-permute-start | bytes 196616 | tf_op jit(solution)/shard_map/gather_rows/ppermute | solution.py:33
  90.0 1.9 collective-permute-done.2
  91.9 4.6 %collective-permute-start.3 = (bf16[32,1024]{1,0:T(8,128)(2,1)S(1)}, bf16[32,1024]{1,0:T(8,128)(2,1)S(1)}, u32[]{:S(2)}, u32[]{:S(2)}) collective-permute-start(bf16[32,1024]{1,0:T(8,128)(2,1)S(1)} %get-tuple-element.18), channel_id=1, source_target_pairs={{0,80},{16,96},{32,112},{48,0},{64,16},{80,32},{96,48},{112,64},{1... | collective-permute-start | bytes 196616 | tf_op jit(solution)/shard_map/gather_rows/ppermute | solution.py:33
  96.5 5.6 %collective-permute-done.3 = bf16[32,1024]{1,0:T(8,128)(2,1)S(1)} collective-permute-done((bf16[32,1024]{1,0:T(8,128)(2,1)S(1)}, bf16[32,1024]{1,0:T(8,128)(2,1)S(1)}, u32[]{:S(2)}, u32[]{:S(2)}) %collective-permute-start.3) | collective-permute-done | bytes 65568 | tf_op jit(solution)/shard_map/gather_rows/ppermute | solution.py:33
  102.3 1.6 weights.1
  104.1 2.0 collective-permute-start.8
  106.1 1.0 collective-permute-done.13
  107.1 1.5 add_convert_fusion
  108.6 9.7 %collective-permute-done.10 = bf16[256,1024]{1,0:T(8,128)(2,1)S(1)} collective-permute-done((bf16[256,1024]{1,0:T(8,128)(2,1)S(1)}, bf16[256,1024]{1,0:T(8,128)(2,1)S(1)}, u32[]{:S(2)}, u32[]{:S(2)}) %collective-permute-start.10) | collective-permute-done | bytes 524320 | tf_op jit(solution)/shard_map/gather_rows/ppermute | solution.py:33
  118.4 5.2 %collective-permute-done.8 = bf16[256,1024]{1,0:T(8,128)(2,1)} collective-permute-done((bf16[256,1024]{1,0:T(8,128)(2,1)S(1)}, bf16[256,1024]{1,0:T(8,128)(2,1)}, u32[]{:S(2)}, u32[]{:S(2)}) %collective-permute-start.8) | collective-permute-done | bytes 524320 | tf_op jit(solution)/shard_map/gather_rows/ppermute | solution.py:33
  123.5 3.5 %all-to-all-start = ((bf16[4,2,672,128]{3,2,1,0:T(8,128)(2,1)}), bf16[4,2,672,128]{3,2,1,0:T(8,128)(2,1)S(1)}, u32[]{:S(2)}, u32[]{:S(2)}) async-start(bf16[4,2,672,128]{3,2,1,0:T(8,128)(2,1)} %add_convert_fusion), calls=%async_computation | async-start | bytes 2752512 | tf_op jit(solution)/shard_map/weights/all_to_all | solution.py:49
  127.1 18.6 %all-to-all-done = bf16[4,2,672,128]{3,2,1,0:T(8,128)(2,1)S(1)} async-done(((bf16[4,2,672,128]{3,2,1,0:T(8,128)(2,1)}), bf16[4,2,672,128]{3,2,1,0:T(8,128)(2,1)S(1)}, u32[]{:S(2)}, u32[]{:S(2)}) %all-to-all-start) | async-done | bytes 1376288 | tf_op jit(solution)/shard_map/weights/all_to_all | solution.py:49
  146.0 2.7 collective-permute-start.14
  148.8 1.0 slice.99
  149.8 2.1 collective-permute-start.9
  151.9 1.7 collective-permute-done.14
  153.6 2.9 %collective-permute-done.11 = bf16[128,1024]{1,0:T(8,128)(2,1)S(1)} collective-permute-done((bf16[128,1024]{1,0:T(8,128)(2,1)S(1)}, bf16[128,1024]{1,0:T(8,128)(2,1)S(1)}, u32[]{:S(2)}, u32[]{:S(2)}) %collective-permute-start.11) | collective-permute-done | bytes 262176 | tf_op jit(solution)/shard_map/gather_rows/ppermute | solution.py:33
  156.5 1.2 collective-permute-done.9
  158.5 12.7 %all_to_all.25 = bf16[4,672,128]{2,1,0:T(8,128)(2,1)S(1)} all-to-all(bf16[4,672,128]{2,1,0:T(8,128)(2,1)S(1)} %broadcast_in_dim.50), channel_id=1, replica_groups=mesh['yh'=2,'z'=8,'x'=4,'yl'=2,'c'=2] {'x'}, dimensions={0} | all-to-all | bytes 1376256 | tf_op jit(solution)/shard_map/weights/all_to_all | solution.py:45
  171.2 2.1 collective-permute-done.15
  173.7 0.9 reshape.222
  175.6 1.9 constant_dynamic-update-slice_fusion.3
  180.6 2.9 %fusion.68 = (bf16[1024,512]{1,0:T(8,128)(2,1)S(1)}, f32[1024,512]{1,0:T(8,128)S(1)}) fusion(bf16[1024,1024]{1,0:T(8,128)(2,1)} %constant_dynamic-update-slice_fusion, bf16[64,8,8,128]{3,2,1,0:T(8,128)(2,1)S(1)} %bitcast.195), kind=kOutput, calls=%fused_computation.142 | convolution fusion | flops 1074266112 | bytes 6291456 | tf_op jit(solution)/shard_map/project/dot_general | solution.py:58
  183.8 1.4 collective-permute-start.21
  185.2 0.9 collective-permute-start.19
  186.1 2.3 collective-permute-start.17
  189.2 2.0 fusion.40
  191.8 4.9 %all-to-all-start.2 = ((f32[8,1,1024]{2,1,0:T(1,128)}), f32[8,1,1024]{2,1,0:T(1,128)S(1)}, u32[]{:S(2)}, u32[]{:S(2)}) async-start(f32[8,1,1024]{2,1,0:T(1,128)} %broadcast_in_dim.51), calls=%async_computation.2 | async-start | bytes 65536 | tf_op jit(solution)/shard_map/project/all_to_all | solution.py:45
  196.7 1.1 fusion.37
  197.9 0.9 copy.78
  198.8 6.0 %all-to-all-done.2 = f32[8,1,1024]{2,1,0:T(1,128)S(1)} async-done(((f32[8,1,1024]{2,1,0:T(1,128)}), f32[8,1,1024]{2,1,0:T(1,128)S(1)}, u32[]{:S(2)}, u32[]{:S(2)}) %all-to-all-start.2) | async-done | bytes 32800 | tf_op jit(solution)/shard_map/project/all_to_all | solution.py:45
  205.7 3.3 %all-to-all-start.3 = ((f32[8,1,1024]{2,1,0:T(1,128)}), f32[8,1,1024]{2,1,0:T(1,128)S(1)}, u32[]{:S(2)}, u32[]{:S(2)}) async-start(f32[8,1,1024]{2,1,0:T(1,128)} %broadcast_in_dim.52), calls=%async_computation.3 | async-start | bytes 65536 | tf_op jit(solution)/shard_map/project/all_to_all | solution.py:45
  209.5 1.3 collective-permute-done.19.refs_4_
  211.3 1.2 fusion.41.q_ref
  212.5 1.9 all-to-all-done.3
  214.7 14.4 %attention.1 = bf16[1024,128]{1,0:T(8,128)(2,1)S(1)} custom-call(s32[8]{0:T(128)S(1)} %stack.91.place_ref, bf16[1024,128]{1,0:T(8,128)(2,1)S(1)} %fusion.41.q_ref, f32[8,1024]{1,0:T(8,128)S(1)} %concatenate.36.inverse_ref, bf16[1024,256]{1,0:T(8,128)(2,1)S(1)} %bitcast.177, bf16[1024,256]{1,0:T(8,128)(2,1)S(1)} %collective-permute-done.16.refs_1_, ...), custom_call_target="tpu_custom_call" | custom-call | tf_op jit(solution)/shard_map/attention/pallas_call | solution.py:144
  229.8 3.9 %all-to-all-start.4 = ((bf16[8,128,128]{2,1,0:T(8,128)(2,1)}), bf16[8,128,128]{2,1,0:T(8,128)(2,1)S(1)}, u32[]{:S(2)}, u32[]{:S(2)}) async-start(bf16[8,128,128]{2,1,0:T(8,128)(2,1)} %bitcast.59), calls=%async_computation.4 | async-start | bytes 524288 | tf_op jit(solution)/shard_map/lift/all_to_all | solution.py:49
  234.6 0.8 dynamic-slice_bitcast_fusion
  235.5 10.4 %all-to-all-done.4 = bf16[8,128,128]{2,1,0:T(8,128)(2,1)S(1)} async-done(((bf16[8,128,128]{2,1,0:T(8,128)(2,1)}), bf16[8,128,128]{2,1,0:T(8,128)(2,1)S(1)}, u32[]{:S(2)}, u32[]{:S(2)}) %all-to-all-start.4) | async-done | bytes 262176 | tf_op jit(solution)/shard_map/lift/all_to_all | solution.py:49
  246.0 2.2 fusion.20
  249.4 1.9 collective-permute-start.25
  251.3 2.5 collective-permute-start.24
  254.1 3.0 %collective-permute-done.24 = bf16[32,1024]{1,0:T(8,128)(2,1)S(1)} collective-permute-done((bf16[32,1024]{1,0:T(8,128)(2,1)S(1)}, bf16[32,1024]{1,0:T(8,128)(2,1)S(1)}, u32[]{:S(2)}, u32[]{:S(2)}) %collective-permute-start.24) | collective-permute-done | bytes 65568 | tf_op jit(solution)/shard_map/lift/ppermute | solution.py:33
  257.1 0.9 fusion.50
  258.1 1.9 collective-permute-start.26
  260.0 7.2 %collective-permute-done.26 = f32[1,1024]{1,0:T(1,128)S(1)} collective-permute-done((f32[1,1024]{1,0:T(1,128)S(1)}, f32[1,1024]{1,0:T(1,128)S(1)}, u32[]{:S(2)}, u32[]{:S(2)}) %collective-permute-start.26) | collective-permute-done | bytes 4128 | tf_op jit(solution)/shard_map/lift/ppermute | solution.py:28
  267.2 0.9 fusion.24
  (130 shorter events, 16.6 us)
Async XLA Ops:
  6.5 41.4 %copy-start = (bf16[1024,1024]{1,0:T(8,128)(2,1)S(1)}, bf16[1024,1024]{1,0:T(8,128)(2,1)}, u32[]{:S(2)}) copy-start(bf16[1024,1024]{1,0:T(8,128)(2,1)} %param.15) | copy-start | bytes 6291460
  6.5 2.6 copy-start.11
  6.5 8.2 %copy-start.4 = (bf16[256,1024]{1,0:T(8,128)(2,1)S(1)}, bf16[256,1024]{1,0:T(8,128)(2,1)}, u32[]{:S(2)}) copy-start(bf16[256,1024]{1,0:T(8,128)(2,1)} %param.11) | copy-start | bytes 1572868
  6.5 8.4 %copy-start.12 = (f32[1024]{0:T(1024)S(1)}, f32[1024]{0:T(1024)}, u32[]{:S(2)}) copy-start(f32[1024]{0:T(1024)} %param.12) | copy-start | bytes 12292
  10.0 72.1 %collective-permute-start.12 = (bf16[1024,256]{1,0:T(8,128)(2,1)}, bf16[1024,256]{1,0:T(8,128)(2,1)}, u32[]{:S(2)}, u32[]{:S(2)}) collective-permute-start(bf16[1024,256]{1,0:T(8,128)(2,1)} %pad_maximum_fusion.2), channel_id=1, source_target_pairs={{0,0},{16,1},{32,2},{48,3},{64,4},{80,5},{96,6},{112,7},{128,8},{1... | collective-permute-start | bytes 1572872 | tf_op jit(solution)/shard_map/weights/ppermute | solution.py:233
  15.1 21.3 %collective-permute-start = (bf16[256,1024]{1,0:T(8,128)(2,1)S(1)}, bf16[256,1024]{1,0:T(8,128)(2,1)}, u32[]{:S(2)}, u32[]{:S(2)}) collective-permute-start(bf16[256,1024]{1,0:T(8,128)(2,1)S(1)} %fusion.27), channel_id=1, source_target_pairs={{0,1},{1,2},{2,3},{3,4},{4,5},{5,6},{6,7},{7,8},{8,9},{9,10},{10,1... | collective-permute-start | bytes 1572872 | tf_op jit(solution)/shard_map/ppermute | solution.py:28
  22.7 13.7 %copy-start.13 = (bf16[1024,2048]{1,0:T(8,128)(2,1)S(1)}, bf16[1024,2048]{1,0:T(8,128)(2,1)}, u32[]{:S(2)}) copy-start(bf16[1024,2048]{1,0:T(8,128)(2,1)} %param.14) | copy-start | bytes 12582916
  40.3 2.4 copy-start.8
  44.6 2.5 copy-start.7
  49.7 52.6 %copy-start.2 = (bf16[1024,256]{1,0:T(8,128)(2,1)S(1)}, bf16[1024,256]{1,0:T(8,128)(2,1)}, u32[]{:S(2)}) copy-start(bf16[1024,256]{1,0:T(8,128)(2,1)} %down_ref.1) | copy-start | bytes 1572868
  49.7 52.7 %copy-start.3 = (bf16[256,1024]{1,0:T(8,128)(2,1)S(1)}, bf16[256,1024]{1,0:T(8,128)(2,1)}, u32[]{:S(2)}) copy-start(bf16[256,1024]{1,0:T(8,128)(2,1)} %up_ref.1) | copy-start | bytes 1572868
  49.7 52.4 %collective-permute-start.7 = (bf16[32,1024]{1,0:T(8,128)(2,1)S(1)}, bf16[32,1024]{1,0:T(8,128)(2,1)S(1)}, u32[]{:S(2)}, u32[]{:S(2)}) collective-permute-start(bf16[32,1024]{1,0:T(8,128)(2,1)S(1)} %get-tuple-element.18), channel_id=1, source_target_pairs={{0,16},{16,32},{32,48},{48,64},{64,80},{80,96},{96,112},{112,0},{1... | collective-permute-start | bytes 196616 | tf_op jit(solution)/shard_map/gather_rows/ppermute | solution.py:33
  49.8 52.3 %collective-permute-start.6 = (bf16[32,1024]{1,0:T(8,128)(2,1)S(1)}, bf16[32,1024]{1,0:T(8,128)(2,1)S(1)}, u32[]{:S(2)}, u32[]{:S(2)}) collective-permute-start(bf16[32,1024]{1,0:T(8,128)(2,1)S(1)} %get-tuple-element.18), channel_id=1, source_target_pairs={{0,32},{16,48},{32,64},{48,80},{64,96},{80,112},{96,0},{112,16},{1... | collective-permute-start | bytes 196616 | tf_op jit(solution)/shard_map/gather_rows/ppermute | solution.py:33
  52.2 49.8 %collective-permute-start.5 = (bf16[32,1024]{1,0:T(8,128)(2,1)S(1)}, bf16[32,1024]{1,0:T(8,128)(2,1)S(1)}, u32[]{:S(2)}, u32[]{:S(2)}) collective-permute-start(bf16[32,1024]{1,0:T(8,128)(2,1)S(1)} %get-tuple-element.18), channel_id=1, source_target_pairs={{0,48},{16,64},{32,80},{48,96},{64,112},{80,0},{96,16},{112,32},{1... | collective-permute-start | bytes 196616 | tf_op jit(solution)/shard_map/gather_rows/ppermute | solution.py:33
  82.1 20.0 %collective-permute-start.4 = (bf16[32,1024]{1,0:T(8,128)(2,1)S(1)}, bf16[32,1024]{1,0:T(8,128)(2,1)S(1)}, u32[]{:S(2)}, u32[]{:S(2)}) collective-permute-start(bf16[32,1024]{1,0:T(8,128)(2,1)S(1)} %get-tuple-element.18), channel_id=1, source_target_pairs={{0,64},{16,80},{32,96},{48,112},{64,0},{80,16},{96,32},{112,48},{1... | collective-permute-start | bytes 196616 | tf_op jit(solution)/shard_map/gather_rows/ppermute | solution.py:33
  82.1 4.6 %collective-permute-start.1 = (bf16[32,1024]{1,0:T(8,128)(2,1)S(1)}, bf16[32,1024]{1,0:T(8,128)(2,1)S(1)}, u32[]{:S(2)}, u32[]{:S(2)}) collective-permute-start(bf16[32,1024]{1,0:T(8,128)(2,1)S(1)} %get-tuple-element.18), channel_id=1, source_target_pairs={{0,112},{16,0},{32,16},{48,32},{64,48},{80,64},{96,80},{112,96},{1... | collective-permute-start | bytes 196616 | tf_op jit(solution)/shard_map/gather_rows/ppermute | solution.py:33
  86.7 5.2 %collective-permute-start.2 = (bf16[32,1024]{1,0:T(8,128)(2,1)S(1)}, bf16[32,1024]{1,0:T(8,128)(2,1)S(1)}, u32[]{:S(2)}, u32[]{:S(2)}) collective-permute-start(bf16[32,1024]{1,0:T(8,128)(2,1)S(1)} %get-tuple-element.18), channel_id=1, source_target_pairs={{0,96},{16,112},{32,0},{48,16},{64,32},{80,48},{96,64},{112,80},{1... | collective-permute-start | bytes 196616 | tf_op jit(solution)/shard_map/gather_rows/ppermute | solution.py:33
  91.9 10.2 %collective-permute-start.3 = (bf16[32,1024]{1,0:T(8,128)(2,1)S(1)}, bf16[32,1024]{1,0:T(8,128)(2,1)S(1)}, u32[]{:S(2)}, u32[]{:S(2)}) collective-permute-start(bf16[32,1024]{1,0:T(8,128)(2,1)S(1)} %get-tuple-element.18), channel_id=1, source_target_pairs={{0,80},{16,96},{32,112},{48,0},{64,16},{80,32},{96,48},{112,64},{1... | collective-permute-start | bytes 196616 | tf_op jit(solution)/shard_map/gather_rows/ppermute | solution.py:33
  103.9 3.2 %collective-permute-start.13 = (bf16[4,2,672,128]{3,2,1,0:T(8,128)(2,1)S(1)}, bf16[4,2,672,128]{3,2,1,0:T(8,128)(2,1)S(1)}, u32[]{:S(2)}, u32[]{:S(2)}) collective-permute-start(bf16[4,2,672,128]{3,2,1,0:T(8,128)(2,1)S(1)} %get-tuple-element.14), channel_id=1, source_target_pairs={{0,1},{1,0},{2,3},{3,2},{4,5},{5,4},{6,7},{7,6},{8,9},{9,8},{10,11... | collective-permute-start | bytes 4128776 | tf_op jit(solution)/shard_map/weights/ppermute | solution.py:33
  104.0 14.3 %collective-permute-start.10 = (bf16[256,1024]{1,0:T(8,128)(2,1)S(1)}, bf16[256,1024]{1,0:T(8,128)(2,1)S(1)}, u32[]{:S(2)}, u32[]{:S(2)}) collective-permute-start(bf16[256,1024]{1,0:T(8,128)(2,1)S(1)} %bitcast.183), channel_id=1, source_target_pairs={{0,2},{2,128},{128,130},{130,0},{1,3},{3,129},{129,131},{131,1},{4... | collective-permute-start | bytes 1572872 | tf_op jit(solution)/shard_map/gather_rows/ppermute | solution.py:33
  104.1 19.4 %collective-permute-start.8 = (bf16[256,1024]{1,0:T(8,128)(2,1)S(1)}, bf16[256,1024]{1,0:T(8,128)(2,1)}, u32[]{:S(2)}, u32[]{:S(2)}) collective-permute-start(bf16[256,1024]{1,0:T(8,128)(2,1)S(1)} %bitcast.184), channel_id=1, source_target_pairs={{0,130},{2,0},{128,2},{130,128},{1,131},{3,1},{129,3},{131,129},{4... | collective-permute-start | bytes 1572872 | tf_op jit(solution)/shard_map/gather_rows/ppermute | solution.py:33
  123.5 22.2 %all-to-all-start = ((bf16[4,2,672,128]{3,2,1,0:T(8,128)(2,1)}), bf16[4,2,672,128]{3,2,1,0:T(8,128)(2,1)S(1)}, u32[]{:S(2)}, u32[]{:S(2)}) async-start(bf16[4,2,672,128]{3,2,1,0:T(8,128)(2,1)} %add_convert_fusion), calls=%async_computation | async-start | bytes 2752512 | tf_op jit(solution)/shard_map/weights/all_to_all | solution.py:49
  127.1 108.4 %all-gather.2.cloned.1.call-start = ((), (), s32[]{:S(2)}) async-start(), calls=%async_computation.5 | async-start | bytes 2949120 | tf_op jit(solution)/shard_map/weights/all_gather | solution.py:269
  146.0 7.6 %collective-permute-start.14 = (bf16[672,128]{1,0:T(8,128)(2,1)S(1)}, bf16[672,128]{1,0:T(8,128)(2,1)S(1)}, u32[]{:S(2)}, u32[]{:S(2)}) collective-permute-start(bf16[672,128]{1,0:T(8,128)(2,1)S(1)} %fusion.48), channel_id=1, source_target_pairs={{0,2},{2,0},{1,3},{3,1},{4,6},{6,4},{5,7},{7,5},{8,10},{10,8},{9,1... | collective-permute-start | bytes 516104 | tf_op jit(solution)/shard_map/weights/ppermute | solution.py:33
  148.7 7.8 %collective-permute-start.11 = (bf16[128,1024]{1,0:T(8,128)(2,1)S(1)}, bf16[128,1024]{1,0:T(8,128)(2,1)S(1)}, u32[]{:S(2)}, u32[]{:S(2)}) collective-permute-start(bf16[128,1024]{1,0:T(8,128)(2,1)S(1)} %slice.100), channel_id=1, source_target_pairs={{0,2},{2,128},{128,130},{130,0},{1,3},{3,129},{129,131},{131,1},{4... | collective-permute-start | bytes 786440 | tf_op jit(solution)/shard_map/gather_rows/ppermute | solution.py:33
  149.8 7.9 %collective-permute-start.9 = (bf16[128,1024]{1,0:T(8,128)(2,1)S(1)}, bf16[128,1024]{1,0:T(8,128)(2,1)S(1)}, u32[]{:S(2)}, u32[]{:S(2)}) collective-permute-start(bf16[128,1024]{1,0:T(8,128)(2,1)S(1)} %slice.99), channel_id=1, source_target_pairs={{0,130},{2,0},{128,2},{130,128},{1,131},{3,1},{129,3},{131,129},{4... | collective-permute-start | bytes 786440 | tf_op jit(solution)/shard_map/gather_rows/ppermute | solution.py:33
  157.7 0.7 copy-start.9
  171.2 2.1 collective-permute-start.15
  173.7 3.8 %copy-start.10 = (bf16[128,1024]{1,0:T(8,128)(2,1)S(1)}, bf16[128,1024]{1,0:T(8,128)(2,1)}, u32[]{:S(2)}) copy-start(bf16[128,1024]{1,0:T(8,128)(2,1)} %copy-done.9) | copy-start | bytes 786436
  183.8 25.3 %collective-permute-start.21 = (bf16[1024,256]{1,0:T(8,128)(2,1)S(1)}, bf16[1024,256]{1,0:T(8,128)(2,1)S(1)}, u32[]{:S(2)}, u32[]{:S(2)}) collective-permute-start(bf16[1024,256]{1,0:T(8,128)(2,1)S(1)} %bitcast.173), channel_id=1, source_target_pairs={{0,8},{4,12},{8,0},{12,4},{1,9},{5,13},{9,1},{13,5},{2,10},{6,14},... | collective-permute-start | bytes 1572872 | tf_op jit(solution)/shard_map/project/ppermute | solution.py:33
  185.2 25.6 %collective-permute-start.19 = (bf16[1024,256]{1,0:T(8,128)(2,1)S(1)}, bf16[1024,256]{1,0:T(8,128)(2,1)S(1)}, u32[]{:S(2)}, u32[]{:S(2)}) collective-permute-start(bf16[1024,256]{1,0:T(8,128)(2,1)S(1)} %bitcast.174), channel_id=1, source_target_pairs={{0,4},{4,8},{8,12},{12,0},{1,5},{5,9},{9,13},{13,1},{2,6},{6,10},{... | collective-permute-start | bytes 1572872 | tf_op jit(solution)/shard_map/project/ppermute | solution.py:33
  186.1 24.8 %collective-permute-start.17 = (bf16[1024,256]{1,0:T(8,128)(2,1)S(1)}, bf16[1024,256]{1,0:T(8,128)(2,1)S(1)}, u32[]{:S(2)}, u32[]{:S(2)}) collective-permute-start(bf16[1024,256]{1,0:T(8,128)(2,1)S(1)} %bitcast.175), channel_id=1, source_target_pairs={{0,12},{4,0},{8,4},{12,8},{1,13},{5,1},{9,5},{13,9},{2,14},{6,2},{... | collective-permute-start | bytes 1572872 | tf_op jit(solution)/shard_map/project/ppermute | solution.py:33
  188.4 26.3 %collective-permute-start.16 = (bf16[1024,256]{1,0:T(8,128)(2,1)S(1)}, bf16[1024,256]{1,0:T(8,128)(2,1)S(1)}, u32[]{:S(2)}, u32[]{:S(2)}) collective-permute-start(bf16[1024,256]{1,0:T(8,128)(2,1)S(1)} %bitcast.176), channel_id=1, source_target_pairs={{0,1},{1,0},{2,3},{3,2},{4,5},{5,4},{6,7},{7,6},{8,9},{9,8},{10,11... | collective-permute-start | bytes 1572872 | tf_op jit(solution)/shard_map/attention/ppermute | solution.py:33
  191.8 12.9 %all-to-all-start.2 = ((f32[8,1,1024]{2,1,0:T(1,128)}), f32[8,1,1024]{2,1,0:T(1,128)S(1)}, u32[]{:S(2)}, u32[]{:S(2)}) async-start(f32[8,1,1024]{2,1,0:T(1,128)} %broadcast_in_dim.51), calls=%async_computation.2 | async-start | bytes 65536 | tf_op jit(solution)/shard_map/project/all_to_all | solution.py:45
  205.7 8.7 %all-to-all-start.3 = ((f32[8,1,1024]{2,1,0:T(1,128)}), f32[8,1,1024]{2,1,0:T(1,128)S(1)}, u32[]{:S(2)}, u32[]{:S(2)}) async-start(f32[8,1,1024]{2,1,0:T(1,128)} %broadcast_in_dim.52), calls=%async_computation.3 | async-start | bytes 65536 | tf_op jit(solution)/shard_map/project/all_to_all | solution.py:45
  209.1 5.6 %collective-permute-start.22 = (bf16[1024,256]{1,0:T(8,128)(2,1)S(1)}, bf16[1024,256]{1,0:T(8,128)(2,1)S(1)}, u32[]{:S(2)}, u32[]{:S(2)}) collective-permute-start(bf16[1024,256]{1,0:T(8,128)(2,1)S(1)} %collective-permute-done.21.refs_6_), channel_id=1, source_target_pairs={{0,1},{1,0},{2,3},{3,2},{4,5},{5,4},{6,7},{7,6},{8,9},{9,8},{10,11... | collective-permute-start | bytes 1572872 | tf_op jit(solution)/shard_map/attention/ppermute | solution.py:33
  210.8 3.9 %collective-permute-start.20 = (bf16[1024,256]{1,0:T(8,128)(2,1)S(1)}, bf16[1024,256]{1,0:T(8,128)(2,1)}, u32[]{:S(2)}, u32[]{:S(2)}) collective-permute-start(bf16[1024,256]{1,0:T(8,128)(2,1)S(1)} %collective-permute-done.19.refs_4_), channel_id=1, source_target_pairs={{0,1},{1,0},{2,3},{3,2},{4,5},{5,4},{6,7},{7,6},{8,9},{9,8},{10,11... | collective-permute-start | bytes 1572872 | tf_op jit(solution)/shard_map/attention/ppermute | solution.py:33
  210.9 3.8 %collective-permute-start.18 = (bf16[1024,256]{1,0:T(8,128)(2,1)S(1)}, bf16[1024,256]{1,0:T(8,128)(2,1)}, u32[]{:S(2)}, u32[]{:S(2)}) collective-permute-start(bf16[1024,256]{1,0:T(8,128)(2,1)S(1)} %collective-permute-done.17.refs_2_), channel_id=1, source_target_pairs={{0,1},{1,0},{2,3},{3,2},{4,5},{5,4},{6,7},{7,6},{8,9},{9,8},{10,11... | collective-permute-start | bytes 1572872 | tf_op jit(solution)/shard_map/attention/ppermute | solution.py:33
  229.8 16.1 %all-to-all-start.4 = ((bf16[8,128,128]{2,1,0:T(8,128)(2,1)}), bf16[8,128,128]{2,1,0:T(8,128)(2,1)S(1)}, u32[]{:S(2)}, u32[]{:S(2)}) async-start(bf16[8,128,128]{2,1,0:T(8,128)(2,1)} %bitcast.59), calls=%async_computation.4 | async-start | bytes 524288 | tf_op jit(solution)/shard_map/lift/all_to_all | solution.py:49
  235.5 12.7 %slice-start = ((bf16[8,160,1024]{2,1,0:T(8,128)(2,1)}), bf16[8,32,1024]{2,1,0:T(8,128)(2,1)S(1)}, s32[]{:S(2)}) async-start(bf16[8,160,1024]{2,1,0:T(8,128)(2,1)} %all-gather.2.cloned.1.call-done), calls=%async_computation.6 | async-start | bytes 1048576 | tf_op jit(solution)/shard_map/lift/slice | solution.py:316
  246.0 22.2 %copy-start.1 = (bf16[1024,1024]{1,0:T(8,128)(2,1)S(1)}, bf16[1024,1024]{1,0:T(8,128)(2,1)}, u32[]{:S(2)}) copy-start(bf16[1024,1024]{1,0:T(8,128)(2,1)} %param.15) | copy-start | bytes 6291460
  248.2 19.1 %copy-start.5 = (bf16[256,1024]{1,0:T(8,128)(2,1)S(1)}, bf16[256,1024]{1,0:T(8,128)(2,1)}, u32[]{:S(2)}) copy-start(bf16[256,1024]{1,0:T(8,128)(2,1)} %get-tuple-element.41) | copy-start | bytes 1572868
  248.4 0.8 copy-start.6
  249.2 4.7 %collective-permute-start.23 = (bf16[32,1024]{1,0:T(8,128)(2,1)S(1)}, bf16[32,1024]{1,0:T(8,128)(2,1)S(1)}, u32[]{:S(2)}, u32[]{:S(2)}) collective-permute-start(bf16[32,1024]{1,0:T(8,128)(2,1)S(1)} %get-tuple-element.25), channel_id=1, source_target_pairs={{0,2},{2,128},{128,130},{130,0},{1,3},{3,129},{129,131},{131,1},{4... | collective-permute-start | bytes 196616 | tf_op jit(solution)/shard_map/lift/ppermute | solution.py:33
  249.4 4.6 %collective-permute-start.25 = (bf16[32,1024]{1,0:T(8,128)(2,1)S(1)}, bf16[32,1024]{1,0:T(8,128)(2,1)S(1)}, u32[]{:S(2)}, u32[]{:S(2)}) collective-permute-start(bf16[32,1024]{1,0:T(8,128)(2,1)S(1)} %get-tuple-element.26), channel_id=1, source_target_pairs={{0,130},{2,0},{128,2},{130,128},{1,131},{3,1},{129,3},{131,129},{4... | collective-permute-start | bytes 196616 | tf_op jit(solution)/shard_map/lift/ppermute | solution.py:33
  251.3 5.8 %collective-permute-start.24 = (bf16[32,1024]{1,0:T(8,128)(2,1)S(1)}, bf16[32,1024]{1,0:T(8,128)(2,1)S(1)}, u32[]{:S(2)}, u32[]{:S(2)}) collective-permute-start(bf16[32,1024]{1,0:T(8,128)(2,1)S(1)} %get-tuple-element.27), channel_id=1, source_target_pairs={{0,128},{2,130},{128,0},{130,2},{1,129},{3,131},{129,1},{131,3},{4... | collective-permute-start | bytes 196616 | tf_op jit(solution)/shard_map/lift/ppermute | solution.py:33
  258.1 9.1 %collective-permute-start.26 = (f32[1,1024]{1,0:T(1,128)S(1)}, f32[1,1024]{1,0:T(1,128)S(1)}, u32[]{:S(2)}, u32[]{:S(2)}) collective-permute-start(f32[1,1024]{1,0:T(1,128)S(1)} %slice.110), channel_id=1, source_target_pairs={{0,1},{1,2},{2,3},{3,4},{4,5},{5,6},{6,7},{7,8},{8,9},{9,10},{10,1... | collective-permute-start | bytes 12296 | tf_op jit(solution)/shard_map/lift/ppermute | solution.py:28
Sparse Core Ops, SparseCore 0:
  174.7 40.4 all-gather.1
